TPU v7x, 32 devices: a whole 2x2x4 slice. The times are simulated.
32 devices in a mesh: section: 2 (over x), dp: 4 (over z), fsdp: 4 (over y, core).
Axes of the slice: x: 2, y: 2, z: 4, core: 2. Of those that a mesh axis runs over, the one named last changes fastest.
Arguments:
- inputs: float32 [32, 128, 1536], P(('dp', 'fsdp')), may hold values from -6 to 6
- cotangent: float32 [32, 128, 1536], P(('dp', 'fsdp')), may hold values from -6 to 6
- lengths: int32 [32], P(('dp', 'fsdp')), may hold values from 1 to 128, 2560 in all
- norm_gain: float32 [2, 1536], P('section'), may hold values from 0.5 to 1.5
- in_weight: bfloat16 [2, 1536, 6400], P('section', 'fsdp'), may hold values from -0.15625 to 0.15625
- dt_weight: bfloat16 [2, 1536, 48], P('section', 'fsdp'), may hold values from -0.15625 to 0.15625
- conv_weight: float32 [2, 4, 3328], P('section'), may hold values from -3 to 3
- conv_bias: float32 [2, 3328], P('section'), may hold values from -0.5 to 0.5
- dt_bias: float32 [2, 48], P('section'), may hold values from -4 to -1
- decay_log: float32 [2, 48], P('section'), may hold values from -4.6 to 0
- skip_gain: float32 [2, 48], P('section'), may hold values from 0.5 to 1.5
- gate_gain: float32 [2, 3072], P('section'), may hold values from 0.5 to 1.5
- out_weight: bfloat16 [2, 3072, 1536], P('section', 'fsdp'), may hold values from -0.109375 to 0.109375
Outputs:
- layer_outputs: float32 [2, 32, 128, 1536], P('section', ('dp', 'fsdp'))
- input_grads: float32 [2, 32, 128, 1536], P('section', ('dp', 'fsdp'))
- grad_norm_gain: float32 [2, 1536], P('section')
- grad_in_weight: float32 [2, 1536, 6400], P('section', 'fsdp')
- grad_dt_weight: float32 [2, 1536, 48], P('section', 'fsdp')
- grad_conv_weight: float32 [2, 4, 3328], P('section')
- grad_conv_bias: float32 [2, 3328], P('section')
- grad_dt_bias: float32 [2, 48], P('section')
- grad_decay_log: float32 [2, 48], P('section')
- grad_skip_gain: float32 [2, 48], P('section')
- grad_gate_gain: float32 [2, 3072], P('section')
- grad_out_weight: float32 [2, 3072, 1536], P('section', 'fsdp')
Inputs may be any that keep to these rules, and one draw needn't show every extreme that they name: `lengths`: positions from a sequence's length on are padding.
All inputs are finite; a program needn't handle non-finite values. No bound on the sum of `lengths` on one device may be relied on, other than what follows from the above.
Results may differ from a plain program's by a relative error of at most 0.011.
Values may be sent and summed in bfloat16 or wider, within the bound.
No kernel may reach another device: no remote copies, remote signals or barrier semaphores. Data moves between devices by JAX's collectives and lax.ppermute only.
A program may use at most 448 MiB of HBM per device.

v0:
```python
import jax
import jax.numpy as jnp
from jax import lax
from jax.sharding import PartitionSpec as P

INNER = 3072
HEADS = 48
HEAD_DIM = 64
STATE = 128
BLOCK = 64
CONV = 4
BUCKET = 128
MICRO = 2


epsilon = 1e-05
highest = lax.Precision.HIGHEST


def passed_along(block, axis, distance):
    devices = range(lax.axis_size(axis))
    route = [(i - distance, i) for i in devices if i - distance in devices]
    return lax.ppermute(block, axis, route)


def front_norm(residual, norm_gain):
    inverse = lax.rsqrt(jnp.mean(residual * residual, axis=-1, keepdims=True) + epsilon)
    return residual * inverse * norm_gain


def state_space(values, step_sizes, log_decay, inputs_b, outputs_c, skip_gain):
    seq_count, length = (values.shape[0], values.shape[1])
    blocks = length // BLOCK
    values_k = values.reshape(seq_count, blocks, BLOCK, HEADS, HEAD_DIM)
    steps_k = step_sizes.reshape(seq_count, blocks, BLOCK, HEADS)
    totals = jnp.cumsum(log_decay.reshape(seq_count, blocks, BLOCK, HEADS), axis=2)
    in_k = inputs_b.reshape(seq_count, blocks, BLOCK, STATE)
    out_k = outputs_c.reshape(seq_count, blocks, BLOCK, STATE)
    causal = (
        jnp.arange(BLOCK, dtype=jnp.int32)[:, None] >= jnp.arange(BLOCK, dtype=jnp.int32)[None, :]
    )[None, None, :, :, None]
    spread = totals[:, :, :, None, :] - totals[:, :, None, :, :]
    kernel = jnp.where(causal, jnp.exp(jnp.where(causal, spread, 0.0)), 0.0)
    inner_cb = jnp.einsum("skin,skjn->skij", out_k, in_k, precision=highest)
    weighted = inner_cb[..., None] * kernel * steps_k[:, :, None, :, :]
    local_part = jnp.einsum("skijh,skjhp->skihp", weighted, values_k, precision=highest)
    to_end = jnp.exp(totals[:, :, -1:, :] - totals) * steps_k
    scaled_values = values_k * to_end[..., None]
    block_states = jnp.einsum("skjhp,skjn->skhpn", scaled_values, in_k, precision=highest)
    carried = jnp.zeros((seq_count, HEADS, HEAD_DIM, STATE), jnp.float32)
    entering = []
    for block_index in range(blocks):
        entering.append(carried)
        carried = (
            jnp.exp(totals[:, block_index, -1, :])[:, :, None, None] * carried
            + block_states[:, block_index]
        )
    entering_all = jnp.stack(entering, axis=1)
    carried_part = (
        jnp.einsum("skin,skhpn->skihp", out_k, entering_all, precision=highest)
        * jnp.exp(totals)[..., None]
    )
    result = (local_part + carried_part).reshape(seq_count, length, HEADS, HEAD_DIM)
    return result + skip_gain[:, None] * values


def mixer_core(projected, dt_raw, conv_weight, conv_bias, dt_bias, decay_log, skip_gain, gate_gain):
    row_count = projected.shape[0]
    seq_count = row_count // BUCKET
    shaped = projected.reshape(seq_count, BUCKET, projected.shape[1])
    gate_part = shaped[:, :, :INNER]
    conv_input = shaped[:, :, INNER:]
    padded = jnp.pad(conv_input, ((0, 0), (CONV - 1, 0), (0, 0)))
    convolved = conv_bias + conv_weight[0] * padded[:, 0:BUCKET]
    for offset in range(1, CONV):
        convolved = convolved + conv_weight[offset] * padded[:, offset : offset + BUCKET]
    activated = jax.nn.silu(convolved)
    values = activated[:, :, :INNER].reshape(seq_count, BUCKET, HEADS, HEAD_DIM)
    inputs_b = activated[:, :, INNER : INNER + STATE]
    outputs_c = activated[:, :, INNER + STATE :]
    step_sizes = jax.nn.softplus(dt_raw.reshape(seq_count, BUCKET, HEADS) + dt_bias)
    log_decay = -jnp.exp(decay_log) * step_sizes
    scanned = state_space(values, step_sizes, log_decay, inputs_b, outputs_c, skip_gain).reshape(
        seq_count, BUCKET, INNER
    )
    gated_out = scanned * jax.nn.silu(gate_part)
    inverse = lax.rsqrt(jnp.mean(gated_out * gated_out, axis=-1, keepdims=True) + epsilon)
    return (gated_out * inverse * gate_gain).reshape(row_count, INNER)


def layer_forward(residual, params):
    norm_gain, in_weight, dt_weight, small_params, out_weight = params
    normed = front_norm(residual, norm_gain).astype(jnp.bfloat16)
    projected = jnp.dot(normed, in_weight, preferred_element_type=jnp.float32)
    dt_raw = jnp.dot(normed, dt_weight, preferred_element_type=jnp.float32)
    mixed_out = mixer_core(projected, dt_raw, *small_params).astype(jnp.bfloat16)
    output = residual + jnp.dot(mixed_out, out_weight, preferred_element_type=jnp.float32)
    return (output, (normed, projected, dt_raw, mixed_out))


def contract_rows(left, right):
    return lax.dot_general(
        left, right, (((0,), (0,)), ((), ())), preferred_element_type=jnp.float32
    )


def contract_cols(left, right):
    return lax.dot_general(
        left, right, (((1,), (1,)), ((), ())), preferred_element_type=jnp.float32
    )


def column_term(columns, grads):
    return contract_rows(columns, grads)


def reorder(columns, data_groups, owners):
    row_count, total_cols = columns.shape
    shaped = columns.reshape(row_count, owners, data_groups, total_cols // (owners * data_groups))
    return shaped.transpose(0, 2, 1, 3).reshape(row_count, total_cols)


def per_device(
    inputs,
    cotangent,
    lengths,
    norm_gain,
    in_weight,
    dt_weight,
    conv_weight,
    conv_bias,
    dt_bias,
    decay_log,
    skip_gain,
    gate_gain,
    out_weight,
):
    first_section = lax.axis_index("section") == 0
    full_in, full_dt, full_out = (
        lax.all_gather(in_weight[0], "fsdp", axis=0, tiled=True),
        lax.all_gather(dt_weight[0], "fsdp", axis=0, tiled=True),
        lax.all_gather(out_weight[0], "fsdp", axis=0, tiled=True),
    )
    small_params = (
        conv_weight[0],
        conv_bias[0],
        dt_bias[0],
        decay_log[0],
        skip_gain[0],
        gate_gain[0],
    )
    own_gain = norm_gain[0]
    params = (own_gain, full_in, full_dt, small_params, full_out)
    per_micro = inputs.shape[0] // MICRO
    row_count = per_micro * BUCKET
    model_width = inputs.shape[2]
    proj_cols = full_in.shape[1]
    data_groups = lax.axis_size("dp")
    owners = lax.axis_size("fsdp")
    positions = jnp.arange(BUCKET, dtype=jnp.int32)
    empty_rows = jnp.zeros((row_count, model_width), jnp.float32)

    def micro_rows(source, micro_index):
        return source[micro_index * per_micro : (micro_index + 1) * per_micro].reshape(
            row_count, model_width
        )

    def arrange(columns):
        return reorder(columns, data_groups, owners)

    layer_inputs = []
    results = []
    kept_all = []
    for section_tick in range(MICRO + 1):
        if section_tick > 0:
            arrived = passed_along(results[-1], "section", 1)
        else:
            arrived = empty_rows
        own_rows = micro_rows(inputs, section_tick) if section_tick < MICRO else empty_rows
        residual = jnp.where(first_section, own_rows, arrived)
        output, kept_values = layer_forward(residual, params)
        layer_inputs.append(residual)
        results.append(output)
        kept_all.append(kept_values)
    small_acc = (jnp.zeros(own_gain.shape, jnp.float32),) + tuple(
        (jnp.zeros(a.shape, jnp.float32) for a in small_params)
    )
    total_in = None
    total_out = None
    grads_back = []
    for section_tick in range(MICRO + 1):
        if section_tick > 0:
            returned = passed_along(grads_back[-1], "section", -1)
        else:
            returned = empty_rows
        if section_tick < MICRO:
            own_lengths = lengths[section_tick * per_micro : (section_tick + 1) * per_micro]
            live_rows = (positions[None, :] < own_lengths[:, None]).astype(jnp.float32)
            top_grad = micro_rows(cotangent, section_tick) * live_rows.reshape(row_count, 1)
        else:
            top_grad = empty_rows
        later_tick = min(section_tick + 1, MICRO)
        earlier = max(section_tick - 1, 0)
        grad_output = jnp.where(first_section, returned, top_grad)
        residual = jnp.where(first_section, layer_inputs[earlier], layer_inputs[later_tick])
        normed, projected, dt_raw, mixed_out = jax.tree.map(
            lambda a, b: jnp.where(first_section, a, b), kept_all[earlier], kept_all[later_tick]
        )
        grad_rounded = grad_output.astype(jnp.bfloat16)
        grad_mixed = contract_cols(grad_rounded, full_out)
        _, pull_mixer = jax.vjp(mixer_core, projected, dt_raw, *small_params)
        pulled = pull_mixer(grad_mixed)
        grad_proj = pulled[0].astype(jnp.bfloat16)
        grad_dt = pulled[1].astype(jnp.bfloat16)
        grad_cat = jnp.concatenate([grad_proj, grad_dt], axis=1)
        grad_normed = contract_cols(grad_proj, full_in) + contract_cols(grad_dt, full_dt)
        _, pull_front = jax.vjp(front_norm, residual, own_gain)
        grad_residual, grad_gain = pull_front(grad_normed)
        grads_back.append(grad_output + grad_residual)
        small_acc = tuple((a + b for a, b in zip(small_acc, (grad_gain,) + tuple(pulled[2:]))))
        normed_cols = arrange(normed)
        mixed_cols = arrange(mixed_out)
        part_in = lax.psum_scatter(
            column_term(normed_cols, grad_cat), ("dp", "fsdp"), scatter_dimension=0, tiled=True
        )
        part_out = lax.psum_scatter(
            column_term(mixed_cols, grad_rounded), ("dp", "fsdp"), scatter_dimension=0, tiled=True
        )
        total_in = part_in if total_in is None else total_in + part_in
        total_out = part_out if total_out is None else total_out + part_out
    owned_in, owned_out = (
        lax.all_gather(total_in, "dp", axis=0, tiled=True),
        lax.all_gather(total_out, "dp", axis=0, tiled=True),
    )
    small_total = lax.psum(small_acc, ("dp", "fsdp"))
    layer_out = jnp.concatenate(
        [
            jnp.where(first_section, results[m], results[m + 1]).reshape(
                per_micro, BUCKET, model_width
            )
            for m in range(MICRO)
        ],
        axis=0,
    )
    input_grad = jnp.concatenate(
        [
            jnp.where(first_section, grads_back[m + 1], grads_back[m]).reshape(
                per_micro, BUCKET, model_width
            )
            for m in range(MICRO)
        ],
        axis=0,
    )
    grad_in_part = owned_in[:, :proj_cols]
    grad_dt_part = owned_in[:, proj_cols:]
    return (
        layer_out[None],
        input_grad[None],
        small_total[0][None],
        grad_in_part[None],
        grad_dt_part[None],
        small_total[1][None],
        small_total[2][None],
        small_total[3][None],
        small_total[4][None],
        small_total[5][None],
        small_total[6][None],
        owned_out[None],
    )


def solution(mesh):
    in_specs = (
        P(("dp", "fsdp"), None, None),
        P(("dp", "fsdp"), None, None),
        P(("dp", "fsdp")),
        P("section", None),
        P("section", "fsdp", None),
        P("section", "fsdp", None),
        P("section", None, None),
        P("section", None),
        P("section", None),
        P("section", None),
        P("section", None),
        P("section", None),
        P("section", "fsdp", None),
    )
    out_specs = (
        P("section", ("dp", "fsdp"), None, None),
        P("section", ("dp", "fsdp"), None, None),
        P("section", None),
        P("section", "fsdp", None),
        P("section", "fsdp", None),
        P("section", None, None),
        P("section", None),
        P("section", None),
        P("section", None),
        P("section", None),
        P("section", None),
        P("section", "fsdp", None),
    )
    return jax.shard_map(
        per_device, mesh=mesh, in_specs=in_specs, out_specs=out_specs, check_vma=False
    )
```

profile of v0, /device:TPU:0, one launch (start us, length us, event | category | flops | bytes accessed | tf_op | source)
XLA Modules:
  0.0 1780.0 jit_solution(17367377292099813090)
XLA Ops:
  19.5 117.1 %all-gather.12.cloned.1.call-done = bf16[1,1536,6400]{2,1,0:T(8,128)(2,1)} async-done(((bf16[1,384,6400]{2,1,0:T(8,128)(2,1)}), bf16[1,1536,6400]{2,1,0:T(8,128)(2,1)}) %all-gather.12.cloned.1.call-update) | async-done | bytes 19660816 | tf_op jit(solution)/shard_map/all_gather | solution.py:140
  136.7 8.1 fusion.10
  184.4 18.1 %all-gather.14.cloned.1.call-done = bf16[1,3072,1536]{2,1,0:T(8,128)(2,1)} async-done(((bf16[1,768,1536]{2,1,0:T(8,128)(2,1)}), bf16[1,3072,1536]{2,1,0:T(8,128)(2,1)}) %all-gather.14.cloned.1.call-update) | async-done | bytes 9437200 | tf_op jit(solution)/shard_map/all_gather | solution.py:142
  214.1 14.1 collective-permute-done
  231.9 8.2 fusion.8
  310.2 8.7 fusion.396
  321.8 8.4 fusion.6
  370.8 7.8 bitcast_add_fusion.5
  388.8 9.2 fusion.241
  439.4 7.5 multiply_reduce_fusion.20
  464.4 10.0 fusion.225
  530.0 8.0 bitcast_add_fusion.3
  571.6 14.4 fusion.4
  611.8 7.9 fusion.240
  643.2 11.1 fusion.227
  681.2 8.2 fusion.344
  707.1 7.6 bitcast_add_fusion.1
  721.7 7.4 bitcast_add_fusion.2
  754.3 14.3 fusion.2
  784.1 8.0 fusion.404
  792.6 21.3 %add_add_fusion.1 = f32[3072,1536]{1,0:T(8,128)} fusion(f32[3072,1536]{1,0:T(8,128)} %fusion.396, f32[3072,1536]{1,0:T(8,128)} %fusion.404, bf16[128,3072]{0,1:T(8,128)(2,1)} %bitcast.975, f32[128,1536]{1,0:T(8,128)} %collective-permute-done.3, pred[]{:T(512)S(6)} %eq.9), kind=kOutput, calls=%fused_computation.13 | convolution fusion | flops 1217593344 | bytes 58195968 | tf_op jit(solution)/shard_map/dot_general | solution.py:102
  834.1 19.9 %fusion.213 = f32[1536,6448]{1,0:T(8,128)} fusion(bf16[128,1536]{0,1:T(8,128)(2,1)S(1)} %bitcast.1029, bf16[128,48]{1,0:T(8,128)(2,1)} %bitcast.1059, bf16[128,6400]{1,0:T(8,128)(2,1)} %copy-done.45), kind=kOutput, calls=%fused_computation.278 | convolution fusion | flops 2538758144 | bytes 41660416 | tf_op jit(solution)/shard_map/dot_general | solution.py:102
  854.0 17.7 fusion.217
  921.3 10.7 fusion.229
  948.3 7.7 fusion.359
  967.9 40.4 %add_add_fusion = f32[1536,6448]{1,0:T(8,128)} fusion(f32[1536,6448]{1,0:T(8,128)} %fusion.213, f32[1536,6448]{1,0:T(8,128)} %fusion.217, bf16[128,1536]{0,1:T(8,128)(2,1)S(1)} %bitcast.994, bf16[128,48]{1,0:T(8,128)(2,1)S(1)} %bitcast.1058, bf16[128,6400]{1,0:T(8,128)(2,1)S(1)} %fusion.232), kind=kOutput, calls=%fused_computation | convolution fusion | flops 2558566400 | bytes 120893440 | tf_op jit(solution)/shard_map/dot_general | solution.py:102
  1009.5 390.6 %reduce-scatter.3.cloned.1.call-done = f32[96,6448]{1,0:T(8,128)} async-done(((f32[1536,6448]{1,0:T(8,128)}), f32[96,6448]{1,0:T(8,128)}) %reduce-scatter.3.cloned.1.call-update) | async-done | bytes 2476048 | tf_op jit(solution)/shard_map/reduce_scatter | solution.py:223
  1414.6 10.4 fusion
  1433.2 56.9 %all-gather.10.cloned.1.call-done = f32[768,1536]{1,0:T(8,128)} async-done(((f32[192,1536]{1,0:T(8,128)}), f32[768,1536]{1,0:T(8,128)}) %all-gather.10.cloned.1.call-update) | async-done | bytes 4718608 | tf_op jit(solution)/shard_map/all_gather | solution.py:233
  1490.0 176.3 %all-gather.8.cloned.1.call-done = f32[384,6448]{1,0:T(8,128)} async-done(((f32[96,6448]{1,0:T(8,128)}), f32[384,6448]{1,0:T(8,128)}) %all-gather.8.cloned.1.call-update) | async-done | bytes 9904144 | tf_op jit(solution)/shard_map/all_gather | solution.py:232
  1666.3 8.3 slice_bitcast_fusion
  1676.3 83.1 %all-reduce.63.cloned.1.call-done = (f32[1,1536]{1,0:T(1,128)}, f32[1,4,3328]{2,1,0:T(4,128)}, f32[1,3328]{1,0:T(1,128)}, f32[1,48]{1,0:T(1,128)}, f32[1,48]{1,0...) async-done(((f32[1,1536]{1,0:T(1,128)}, f32[1,4,3328]{2,1,0:T(4,128)}, f32[1,3328]{1,0:T(1,128)}, f32[1,48]{1,0:T(1,128)}, f32[1,48]{1,0:T(1,128)}, ...) | async-done | bytes 85584 | tf_op jit(solution)/shard_map/psum | solution.py:235
  (941 shorter events, 614.5 us)
Async XLA Ops:
  7.2 129.5 %all-gather.12.cloned.1.call-start = ((), (), s32[]{:S(2)}) async-start(), calls=%async_computation.4 | async-start | bytes 24576000 | tf_op jit(solution)/shard_map/all_gather | solution.py:140
  8.0 194.5 %all-gather.14.cloned.1.call-start = ((), (), s32[]{:S(2)}) async-start(), calls=%async_computation.5 | async-start | bytes 11796480 | tf_op jit(solution)/shard_map/all_gather | solution.py:142
  8.7 1000.7 %reduce-scatter.5.cloned.1.call-start = ((), (), s32[]{:S(2)}) async-start(), calls=%async_computation.7 | async-start | bytes 20054016 | tf_op jit(solution)/shard_map/reduce_scatter | solution.py:226
  8.8 221.1 %copy-start.142 = (f32[1536]{0:T(1024)}, f32[1536]{0:T(1024)S(1)}, u32[]{:S(2)}) copy-start(f32[1536]{0:T(1024)S(1)} %reduce.80) | copy-start | bytes 18436
  8.9 137.6 %copy-start.211 = (f32[3328]{0:T(1024)}, f32[3328]{0:T(1024)S(1)}, u32[]{:S(2)}) copy-start(f32[3328]{0:T(1024)S(1)} %reduce.78) | copy-start | bytes 39940
  15.5 753.1 %copy-start.78 = (bf16[1,1536,48]{1,2,0:T(8,128)(2,1)}, bf16[1,1536,48]{1,2,0:T(8,128)(2,1)S(1)}, u32[]{:S(2)}) copy-start(bf16[1,1536,48]{1,2,0:T(8,128)(2,1)S(1)} %all-gather.1) | copy-start | bytes 442372
  15.7 129.1 %copy-start.261 = (f32[128]{0:T(128)}, f32[128]{0:T(128)S(1)}, u32[]{:S(2)}) copy-start(f32[128]{0:T(128)S(1)} %add_rsqrt_fusion.5) | copy-start | bytes 1540
  15.7 230.8 %copy-start.253 = (f32[48]{0:T(128)}, f32[48]{0:T(128)S(1)}, u32[]{:S(2)}) copy-start(f32[48]{0:T(128)S(1)} %bitcast_negate_fusion) | copy-start | bytes 580
  16.2 230.4 %copy-start.140 = (f32[128,48]{1,0:T(8,128)}, f32[128,48]{1,0:T(8,128)S(1)}, u32[]{:S(2)}) copy-start(f32[128,48]{1,0:T(8,128)S(1)} %get-tuple-element.253) | copy-start | bytes 73732
  19.3 268.4 %copy-start.135 = (f32[3072]{0:T(1024)}, f32[3072]{0:T(1024)S(1)}, u32[]{:S(2)}) copy-start(f32[3072]{0:T(1024)S(1)} %mul.1954) | copy-start | bytes 36868
  19.3 249.1 %copy-start.194 = (pred[64,64]{1,0:T(8,128)(4,1)}, pred[64,64]{1,0:T(8,128)(4,1)S(1)}, u32[]{:S(2)}) copy-start(pred[64,64]{1,0:T(8,128)(4,1)S(1)} %iota_compare_fusion) | copy-start | bytes 12292
  19.5 220.8 %copy-start.147 = (f32[3328]{0:T(1024)}, f32[3328]{0:T(1024)S(1)}, u32[]{:S(2)}) copy-start(f32[3328]{0:T(1024)S(1)} %get-tuple-element.111) | copy-start | bytes 39940
  19.5 220.8 %copy-start.152 = (f32[3328]{0:T(1024)}, f32[3328]{0:T(1024)S(1)}, u32[]{:S(2)}) copy-start(f32[3328]{0:T(1024)S(1)} %get-tuple-element.112) | copy-start | bytes 39940
  19.5 220.8 %copy-start.157 = (f32[3328]{0:T(1024)}, f32[3328]{0:T(1024)S(1)}, u32[]{:S(2)}) copy-start(f32[3328]{0:T(1024)S(1)} %get-tuple-element.113) | copy-start | bytes 39940
  19.5 220.8 %copy-start.162 = (f32[3328]{0:T(1024)}, f32[3328]{0:T(1024)S(1)}, u32[]{:S(2)}) copy-start(f32[3328]{0:T(1024)S(1)} %get-tuple-element.114) | copy-start | bytes 39940
  184.4 106.4 %copy-start.7 = (f32[1,128,3072]{2,1,0:T(8,128)}, f32[1,128,3072]{2,1,0:T(8,128)S(1)}, u32[]{:S(2)}) copy-start(f32[1,128,3072]{2,1,0:T(8,128)S(1)} %get-tuple-element.181) | copy-start | bytes 4718596
  184.4 23.2 %copy-start.257 = (f32[128]{0:T(128)}, f32[128]{0:T(128)S(1)}, u32[]{:S(2)}) copy-start(f32[128]{0:T(128)S(1)} %add_rsqrt_fusion.4) | copy-start | bytes 1540
  207.6 20.6 %collective-permute-start = (f32[128,1536]{1,0:T(8,128)S(1)}, f32[128,1536]{1,0:T(8,128)S(1)}, u32[]{:S(2)}, u32[]{:S(2)}) collective-permute-start(f32[128,1536]{1,0:T(8,128)S(1)} %fusion.150), channel_id=1, source_target_pairs={{0,16},{1,17},{2,18},{3,19},{4,20},{5,21},{6,22},{7,23},{8,24},{9,... | collective-permute-start | bytes 2359304 | tf_op jit(solution)/shard_map/ppermute | solution.py:23
  297.5 21.3 %collective-permute-start.1 = (f32[128,1536]{1,0:T(8,128)S(1)}, f32[128,1536]{1,0:T(8,128)S(1)}, u32[]{:S(2)}, u32[]{:S(2)}) collective-permute-start(f32[128,1536]{1,0:T(8,128)S(1)} %fusion.153), channel_id=1, source_target_pairs={{0,16},{1,17},{2,18},{3,19},{4,20},{5,21},{6,22},{7,23},{8,24},{9,... | collective-permute-start | bytes 2359304 | tf_op jit(solution)/shard_map/ppermute | solution.py:23
  321.8 28.3 %copy-start.98 = (bf16[128,1536]{1,0:T(8,128)(2,1)}, bf16[128,1536]{1,0:T(8,128)(2,1)S(1)}, u32[]{:S(2)}) copy-start(bf16[128,1536]{1,0:T(8,128)(2,1)S(1)} %get-tuple-element.127) | copy-start | bytes 1179652
  348.8 108.2 %copy-start.118 = (f32[1,128,128]{2,1,0:T(8,128)}, f32[1,128,128]{2,1,0:T(8,128)S(1)}, u32[]{:S(2)}) copy-start(f32[1,128,128]{2,1,0:T(8,128)S(1)} %get-tuple-element.213) | copy-start | bytes 196612
  354.2 109.9 %copy-start.2 = (f32[2,64,48,64]{3,2,1,0:T(8,128)}, f32[2,64,48,64]{3,2,1,0:T(8,128)S(1)}, u32[]{:S(2)}) copy-start(f32[2,64,48,64]{3,2,1,0:T(8,128)S(1)} %reshape.2331) | copy-start | bytes 4718596
  509.5 82.0 %copy-start.112 = (f32[1,128,128]{2,1,0:T(8,128)}, f32[1,128,128]{2,1,0:T(8,128)S(1)}, u32[]{:S(2)}) copy-start(f32[1,128,128]{2,1,0:T(8,128)S(1)} %get-tuple-element.201) | copy-start | bytes 196612
  589.5 20.9 %collective-permute-start.2 = (f32[128,1536]{1,0:T(8,128)}, f32[128,1536]{1,0:T(8,128)}, u32[]{:S(2)}, u32[]{:S(2)}) collective-permute-start(f32[128,1536]{1,0:T(8,128)} %fusion.374), channel_id=1, source_target_pairs={{16,0},{17,1},{18,2},{19,3},{20,4},{21,5},{22,6},{23,7},{24,8},{25... | collective-permute-start | bytes 2359304 | tf_op jit(solution)/shard_map/ppermute | solution.py:23
  772.7 19.9 %collective-permute-start.3 = (f32[128,1536]{1,0:T(8,128)}, f32[128,1536]{1,0:T(8,128)}, u32[]{:S(2)}, u32[]{:S(2)}) collective-permute-start(f32[128,1536]{1,0:T(8,128)} %get-tuple-element.146), channel_id=1, source_target_pairs={{16,0},{17,1},{18,2},{19,3},{20,4},{21,5},{22,6},{23,7},{24,8},{25... | collective-permute-start | bytes 2359304 | tf_op jit(solution)/shard_map/ppermute | solution.py:23
  813.9 586.2 %reduce-scatter.3.cloned.1.call-start = ((), (), s32[]{:S(2)}) async-start(), calls=%async_computation.6 | async-start | bytes 42614784 | tf_op jit(solution)/shard_map/reduce_scatter | solution.py:223
  834.1 37.6 %slice-start = ((s8[9437184]{0:T(1024)(128)(4,1)}), s8[4194304]{0:T(1024)(128)(4,1)S(1)}, s32[]{:S(2)}) async-start(s8[9437184]{0:T(1024)(128)(4,1)} %bitcast.961), calls=%async_computation.9 | async-start | bytes 8388608
  834.1 37.6 %slice-start.1 = ((s8[9437184]{0:T(1024)(128)(4,1)}), s8[4194304]{0:T(1024)(128)(4,1)S(1)}, s32[]{:S(2)}) async-start(s8[9437184]{0:T(1024)(128)(4,1)} %bitcast.961), calls=%async_computation.10 | async-start | bytes 8388608
  1008.4 481.6 %all-gather.10.cloned.1.call-start = ((), (), s32[]{:S(2)}) async-start(), calls=%async_computation.3 | async-start | bytes 5898240 | tf_op jit(solution)/shard_map/all_gather | solution.py:233
  1009.4 390.9 %copy-start.81 = (f32[128,1536]{1,0:T(8,128)S(1)}, f32[128,1536]{1,0:T(8,128)}, u32[]{:S(2)}) copy-start(f32[128,1536]{1,0:T(8,128)} %copy-done.80) | copy-start | bytes 2359300
  1009.5 656.8 %all-gather.8.cloned.1.call-start = ((), (), s32[]{:S(2)}) async-start(), calls=%async_computation.2 | async-start | bytes 12533760 | tf_op jit(solution)/shard_map/all_gather | solution.py:232
  1400.2 359.1 %all-reduce.63.cloned.1.call-start = ((), (), s32[]{:S(2)}) async-start(), calls=%async_computation.8 | async-start | bytes 173056 | tf_op jit(solution)/shard_map/psum | solution.py:235
  (276 other events, 1375.0 us)
Sparse Core Ops, SparseCore 0:
  9.6 127.0 all-gather.11
  138.2 64.2 all-gather.13
  814.1 195.3 reduce-scatter.4
  1013.6 386.4 reduce-scatter.2
  1401.6 88.4 all-gather.9
  1491.4 174.7 all-gather.7
  1671.8 87.5 all-reduce.62
where the time goes:
time: 1790 us; the launch traced here: 1780 us
  waiting for transfers between devices  865 us (48%)
  matrix products  454 us (25%)
  local copies, waits for them, and re-layouts  295 us (16%)
  other arithmetic  132 us (7%)
    reduce_scatter x1, waiting for transfers between devices, per_device(): lax.psum_scatter(column_term(normed_cols, grad_cat), ('dp', 'fsdp'), scat...  391 us
    all_gather x1, waiting for transfers between devices, per_device(): lax.all_gather(total_in, 'dp', axis=0, tiled=True)  176 us
    all_gather x1, waiting for transfers between devices, per_device(): lax.all_gather(in_weight[0], 'fsdp', axis=0, tiled=True)  117 us
    dot_general x6, matrix products, contract_rows(): lax.dot_general(left, right, (((0,), (0,)), ((), ())), preferred_element_...  116 us
    dot_general x12, matrix products, state_space(): jnp.einsum('skijh,skjhp->skihp', weighted, values_k, precision=highest)  93.3 us
    psum x1, waiting for transfers between devices, per_device(): small_total = lax.psum(small_acc, ('dp', 'fsdp'))  83.1 us
    dot_general x9, matrix products, contract_cols(): lax.dot_general(left, right, (((1,), (1,)), ((), ())), preferred_element_...  67 us
    dot_general x12, matrix products, state_space(): jnp.einsum('skjhp,skjn->skhpn', scaled_values, in_k, precision=highest)  65.5 us
  transfers between devices with their start and end apart: 11, of which 10 were waited for; matrix products, arithmetic and copies ran while one was open for 18% of the time, Pallas kernels for 0%

commit v1 on v0

v1 whole, which is shorter than its diff:
```python
import functools

import jax
import jax.numpy as jnp
from jax import lax
from jax.experimental import pallas as pl
from jax.experimental.pallas import tpu as pltpu
from jax.sharding import PartitionSpec as P

HEAD_DIM = 64
STATE = 128
CONV = 4
MICRO = 2
LANES = 128

epsilon = 1e-05
highest = lax.Precision.HIGHEST


def passed_along(block, axis, distance):
    devices = range(lax.axis_size(axis))
    route = [(i - distance, i) for i in devices if i - distance in devices]
    return lax.ppermute(block, axis, route)


def front_norm(residual, norm_gain):
    inverse = lax.rsqrt(jnp.mean(residual * residual, axis=-1, keepdims=True) + epsilon)
    return residual * inverse * norm_gain


def iota(shape, dim):
    return lax.broadcasted_iota(jnp.int32, shape, dim)


def moved_down(block, steps, rows):
    if steps == 0:
        return block
    return jnp.where(rows >= steps, pltpu.roll(block, steps, 0), 0.0)


def moved_up(block, steps, rows):
    if steps == 0:
        return block
    length = block.shape[0]
    return jnp.where(rows < length - steps, pltpu.roll(block, length - steps, 0), 0.0)


def convolved(block, taps, bias, rows):
    total = bias + taps[CONV - 1 : CONV] * block
    for k in range(CONV - 1):
        total = total + taps[k : k + 1] * moved_down(block, CONV - 1 - k, rows)
    return total


def full_dot(left, right, dims=(((1,), (0,)), ((), ()))):
    return lax.dot_general(
        left, right, dims, precision=highest, preferred_element_type=jnp.float32
    )


def bf_dot(left, right, dims=(((1,), (0,)), ((), ()))):
    return lax.dot_general(left, right, dims, preferred_element_type=jnp.float32)


def softplus(x):
    return jnp.maximum(x, 0.0) + jnp.log1p(jnp.exp(-jnp.abs(x)))


def decays(dt_ref, dtb_ref, dlog_ref, cum_t, col_b, step_b, heads):
    length = dt_ref.shape[0]
    square = (length, LANES)
    raw = dt_ref[...] + dtb_ref[...]
    step = softplus(raw)
    rate = -jnp.exp(dlog_ref[...])
    log_decay = rate * step
    lower = jnp.where(iota((length, length), 0) >= iota((length, length), 1), 1.0, 0.0)
    total = full_dot(lower, log_decay)
    cum_t[...] = total.T
    left = iota(square, 1) < HEAD_DIM
    for h in range(heads):
        col_b[h] = jnp.broadcast_to(total[:, h : h + 1], (length, length))
    for i in range(heads // 2):
        step_b[i] = jnp.where(left, step[:, 2 * i : 2 * i + 1], step[:, 2 * i + 1 : 2 * i + 2])
    return raw, step, rate, log_decay


def split_pair(block, left):
    zero = jnp.zeros_like(block)
    return jnp.concatenate(
        [jnp.where(left, block, zero), jnp.where(left, zero, block)], axis=0
    ).astype(jnp.bfloat16)


def mixer_forward_kernel(
    inner, heads, proj_ref, dt_ref, taps_ref, bias_ref, dtb_ref, dlog_ref, skip_ref, gain_ref,
    mixed_ref, local_ref, cum_t, col_b, step_b, gated_s,
):
    length = proj_ref.shape[0]
    square = (length, LANES)
    rows = iota(square, 0)
    left = iota(square, 1) < HEAD_DIM
    decays(dt_ref, dtb_ref, dlog_ref, cum_t, col_b, step_b, heads)

    def activated(offset):
        source = pl.ds(pl.multiple_of(inner + offset, LANES), LANES)
        chan = pl.ds(pl.multiple_of(offset, LANES), LANES)
        pre = convolved(proj_ref[:, source], taps_ref[:, chan], bias_ref[:, chan], rows)
        return pre * jax.nn.sigmoid(pre)

    into = activated(inner)
    out_of = activated(inner + STATE)
    scores = full_dot(out_of, into, (((1,), (1,)), ((), ())))
    scores = jnp.where(iota(scores.shape, 0) >= iota(scores.shape, 1), scores, 0.0)

    def pair(i, squares):
        chan = pl.ds(pl.multiple_of(i * LANES, LANES), LANES)
        values = activated(i * LANES)
        scaled = split_pair(values * step_b[i], left)
        first = scores * jnp.exp(jnp.minimum(col_b[2 * i] - cum_t[pl.ds(2 * i, 1), :], 0.0))
        second = scores * jnp.exp(
            jnp.minimum(col_b[2 * i + 1] - cum_t[pl.ds(2 * i + 1, 1), :], 0.0)
        )
        weights = jnp.concatenate([first, second], axis=1).astype(jnp.bfloat16)
        local = bf_dot(weights, scaled)
        local_ref[:, chan] = local
        gate = proj_ref[:, chan]
        gated = (local + skip_ref[:, chan] * values) * (gate * jax.nn.sigmoid(gate))
        gated_s[:, chan] = gated
        return squares + gated * gated

    squares = lax.fori_loop(0, inner // LANES, pair, jnp.zeros(square, jnp.float32))
    inverse = lax.rsqrt(jnp.sum(squares, axis=1, keepdims=True) / inner + epsilon)

    def scale(i, _):
        chan = pl.ds(pl.multiple_of(i * LANES, LANES), LANES)
        mixed_ref[:, chan] = (gated_s[:, chan] * inverse * gain_ref[:, chan]).astype(jnp.bfloat16)
        return 0

    lax.fori_loop(0, inner // LANES, scale, 0)


def mixer_backward_kernel(
    inner, heads, proj_ref, dt_ref, local_ref, gm_ref,
    taps_ref, bias_ref, dtb_ref, dlog_ref, skip_ref, gain_ref,
    gcat_ref, gtaps_ref, gbias_ref, ggain_ref, gskip_ref, ghead_ref,
    cum_t, col_b, step_b, pre_s,
):
    length = proj_ref.shape[0]
    square = (length, LANES)
    rows = iota(square, 0)
    lanes = iota(square, 1)
    left = lanes < HEAD_DIM
    raw, step, rate, log_decay = decays(dt_ref, dtb_ref, dlog_ref, cum_t, col_b, step_b, heads)
    pairs = inner // LANES

    @pl.when(pl.program_id(0) == 0)
    def _():
        for ref in (gtaps_ref, gbias_ref, ggain_ref, gskip_ref, ghead_ref):
            ref[...] = jnp.zeros_like(ref)

    def column(block):
        return jnp.sum(block, axis=0, keepdims=True)

    def activated(offset):
        source = pl.ds(pl.multiple_of(inner + offset, LANES), LANES)
        chan = pl.ds(pl.multiple_of(offset, LANES), LANES)
        pre = convolved(proj_ref[:, source], taps_ref[:, chan], bias_ref[:, chan], rows)
        pre_s[:, chan] = pre
        return pre * jax.nn.sigmoid(pre)

    def pull_conv(offset, grad_active):
        source = pl.ds(pl.multiple_of(inner + offset, LANES), LANES)
        chan = pl.ds(pl.multiple_of(offset, LANES), LANES)
        pre = pre_s[:, chan]
        sig = jax.nn.sigmoid(pre)
        grad_pre = grad_active * sig * (1.0 + pre * (1.0 - sig))
        block = proj_ref[:, source]
        taps = taps_ref[:, chan]
        grad_block = taps[CONV - 1 : CONV] * grad_pre
        terms = []
        for k in range(CONV - 1):
            grad_block = grad_block + taps[k : k + 1] * moved_up(grad_pre, CONV - 1 - k, rows)
            terms.append(column(grad_pre * moved_down(block, CONV - 1 - k, rows)))
        terms.append(column(grad_pre * block))
        gcat_ref[:, source] = grad_block.astype(jnp.bfloat16)
        gbias_ref[:, chan] += column(grad_pre)
        gtaps_ref[:, chan] += jnp.concatenate(terms, axis=0)

    into = activated(inner)
    out_of = activated(inner + STATE)
    causal_t = iota((length, length), 1) >= iota((length, length), 0)
    scores_t = full_dot(into, out_of, (((1,), (1,)), ((), ())))
    scores_t = jnp.where(causal_t, scores_t, 0.0)

    def measured(i, carry):
        squares, crossed = carry
        chan = pl.ds(pl.multiple_of(i * LANES, LANES), LANES)
        values = activated(i * LANES)
        gate = proj_ref[:, chan]
        gated = (local_ref[:, chan] + skip_ref[:, chan] * values) * (gate * jax.nn.sigmoid(gate))
        return squares + gated * gated, crossed + gated * gm_ref[:, chan] * gain_ref[:, chan]

    zeros = jnp.zeros(square, jnp.float32)
    squares, crossed = lax.fori_loop(0, pairs, measured, (zeros, zeros))
    inverse = lax.rsqrt(jnp.sum(squares, axis=1, keepdims=True) / inner + epsilon)
    pulled = jnp.sum(crossed, axis=1, keepdims=True) * (inverse * inverse * inverse / inner)

    def pair(i, carry):
        grad_scores_t, grad_cum, grad_step = carry
        chan = pl.ds(pl.multiple_of(i * LANES, LANES), LANES)
        pre = pre_s[:, chan]
        values = pre * jax.nn.sigmoid(pre)
        gate = proj_ref[:, chan]
        sig = jax.nn.sigmoid(gate)
        local = local_ref[:, chan]
        skip = skip_ref[:, chan]
        scanned = local + skip * values
        gated = scanned * gate * sig
        grad_mixed = gm_ref[:, chan]
        ggain_ref[:, chan] += column(grad_mixed * gated * inverse)
        grad_gated = inverse * grad_mixed * gain_ref[:, chan] - gated * pulled
        grad_scanned = grad_gated * gate * sig
        gcat_ref[:, chan] = (
            grad_gated * scanned * sig * (1.0 + gate * (1.0 - sig))
        ).astype(jnp.bfloat16)
        gskip_ref[:, chan] += column(grad_scanned * values)
        step_wide = step_b[i]
        grad_low = grad_scanned.astype(jnp.bfloat16)
        grad_even = grad_low.astype(jnp.float32)
        scaled_low = (values * step_wide).astype(jnp.bfloat16)
        scaled = scaled_low.astype(jnp.float32)
        decay_a = jnp.exp(jnp.minimum(cum_t[pl.ds(2 * i, 1), :] - col_b[2 * i], 0.0))
        decay_b = jnp.exp(jnp.minimum(cum_t[pl.ds(2 * i + 1, 1), :] - col_b[2 * i + 1], 0.0))
        weights = jnp.concatenate([scores_t * decay_a, scores_t * decay_b], axis=1)
        grad_scaled = bf_dot(weights.astype(jnp.bfloat16), split_pair(grad_even, left))
        products = bf_dot(split_pair(scaled, left), grad_low, (((1,), (1,)), ((), ())))
        grad_scores_t = grad_scores_t + products[:length] * decay_a + products[length:] * decay_b
        along = grad_even * local - scaled * grad_scaled
        direct = values * grad_scaled
        place = jnp.where(lanes == 2 * i + jnp.where(rows < HEAD_DIM, 0, 1), 1.0, 0.0)
        place = jnp.concatenate([place, place], axis=0).astype(jnp.bfloat16)

        def by_head(block):
            high = block.astype(jnp.bfloat16)
            low = (block - high.astype(jnp.float32)).astype(jnp.bfloat16)
            return bf_dot(jnp.concatenate([high, low], axis=1), place)

        grad_cum = grad_cum + by_head(along)
        grad_step = grad_step + by_head(direct)
        pull_conv(i * LANES, step_wide * grad_scaled + skip * grad_scanned)
        return grad_scores_t, grad_cum, grad_step

    grad_scores_t, grad_cum, grad_step = lax.fori_loop(
        0, pairs, pair, (jnp.zeros((length, length), jnp.float32), zeros, zeros)
    )
    grad_scores_t = jnp.where(causal_t, grad_scores_t, 0.0)
    pull_conv(inner, full_dot(grad_scores_t, out_of))
    pull_conv(inner + STATE, full_dot(grad_scores_t.T, into))
    upper = jnp.where(causal_t, 1.0, 0.0)
    grad_decay = full_dot(upper, grad_cum)
    grad_raw = (grad_step + rate * grad_decay) * jax.nn.sigmoid(raw)
    gcat_ref[:, pl.ds(gcat_ref.shape[1] - LANES, LANES)] = grad_raw.astype(jnp.bfloat16)
    ghead_ref[0:1, :] += column(grad_raw)
    ghead_ref[1:2, :] += column(grad_decay * log_decay)


def whole(block):
    return pl.BlockSpec(block, lambda s: (0,) * len(block))


def by_sequence(length, columns):
    return pl.BlockSpec((length, columns), lambda s: (s, 0))


def kernel_params(small, inner):
    taps, bias, dt_bias, decay_log, skip_gain, gate_gain = small
    heads = inner // HEAD_DIM
    pad = LANES - heads
    return (
        taps,
        bias[None],
        jnp.pad(dt_bias, (0, pad))[None],
        jnp.pad(decay_log, (0, pad))[None],
        jnp.repeat(skip_gain, HEAD_DIM)[None],
        gate_gain[None],
    )


def scratch(length, heads):
    return [
        pltpu.VMEM((LANES, length), jnp.float32),
        pltpu.VMEM((heads, length, length), jnp.float32),
        pltpu.VMEM((heads // 2, length, LANES), jnp.float32),
    ]


def mixer_forward(projected, dt_raw, params, length):
    row_count, cols = projected.shape
    inner = params[5].shape[1]
    heads = inner // HEAD_DIM
    return pl.pallas_call(
        functools.partial(mixer_forward_kernel, inner, heads),
        grid=(row_count // length,),
        in_specs=[by_sequence(length, cols), by_sequence(length, LANES)]
        + [whole(p.shape) for p in params],
        out_specs=[by_sequence(length, inner), by_sequence(length, inner)],
        out_shape=[
            jax.ShapeDtypeStruct((row_count, inner), jnp.bfloat16),
            jax.ShapeDtypeStruct((row_count, inner), jnp.float32),
        ],
        scratch_shapes=scratch(length, heads) + [pltpu.VMEM((length, inner), jnp.float32)],
        compiler_params=pltpu.CompilerParams(vmem_limit_bytes=40 * 1024 * 1024),
        cost_estimate=pl.CostEstimate(
            flops=row_count * inner * 600, bytes_accessed=row_count * (cols * 4 + inner * 6),
            transcendentals=row_count * (heads * length + 2 * cols),
        ),
        name="mixer_forward",
    )(projected, dt_raw, *params)


def mixer_backward(projected, dt_raw, local, grad_mixed, params, length):
    row_count, cols = projected.shape
    inner = params[5].shape[1]
    heads = inner // HEAD_DIM
    chans = params[0].shape[1]
    return pl.pallas_call(
        functools.partial(mixer_backward_kernel, inner, heads),
        grid=(row_count // length,),
        in_specs=[
            by_sequence(length, cols),
            by_sequence(length, LANES),
            by_sequence(length, inner),
            by_sequence(length, inner),
        ]
        + [whole(p.shape) for p in params],
        out_specs=[
            by_sequence(length, cols + LANES),
            whole((CONV, chans)),
            whole((1, chans)),
            whole((1, inner)),
            whole((1, inner)),
            whole((8, LANES)),
        ],
        out_shape=[
            jax.ShapeDtypeStruct((row_count, cols + LANES), jnp.bfloat16),
            jax.ShapeDtypeStruct((CONV, chans), jnp.float32),
            jax.ShapeDtypeStruct((1, chans), jnp.float32),
            jax.ShapeDtypeStruct((1, inner), jnp.float32),
            jax.ShapeDtypeStruct((1, inner), jnp.float32),
            jax.ShapeDtypeStruct((8, LANES), jnp.float32),
        ],
        scratch_shapes=scratch(length, heads) + [pltpu.VMEM((length, chans), jnp.float32)],
        compiler_params=pltpu.CompilerParams(vmem_limit_bytes=48 * 1024 * 1024),
        cost_estimate=pl.CostEstimate(
            flops=row_count * inner * 1500, bytes_accessed=row_count * (cols * 6 + inner * 8),
            transcendentals=row_count * (heads * length + 3 * cols),
        ),
        name="mixer_backward",
    )(projected, dt_raw, local, grad_mixed, *params)


def product_kernel(sources, first, count, *refs):
    lefts = refs[:sources]
    rights = refs[sources:-1]
    out_ref = refs[-1]
    per_source = len(rights) // sources
    total = None
    for j in range(sources):
        block = [rights[j * per_source + m][...] for m in range(per_source)]
        term = bf_dot(lefts[j][first : first + count, :], jnp.concatenate(block, axis=0))
        total = term if total is None else total + term
    out_ref[...] = total.astype(out_ref.dtype)


def tile_of(columns, most):
    return max(t for t in range(LANES, most + 1, LANES) if columns % t == 0)


def summed_product(lefts, rights, first, count, most, name):
    length, columns = rights[0].shape
    tile = tile_of(columns, most)
    return pl.pallas_call(
        functools.partial(product_kernel, len(lefts), first, count),
        grid=(columns // tile,),
        in_specs=[pl.BlockSpec(a.shape, lambda t: (0, 0)) for a in lefts]
        + [pl.BlockSpec((length, tile), lambda t: (0, t)) for _ in rights],
        out_specs=pl.BlockSpec((count, tile), lambda t: (0, t)),
        out_shape=jax.ShapeDtypeStruct((count, columns), jnp.bfloat16),
        compiler_params=pltpu.CompilerParams(vmem_limit_bytes=48 * 1024 * 1024),
        cost_estimate=pl.CostEstimate(
            flops=2 * count * columns * length * len(rights),
            bytes_accessed=2 * columns * (length * len(rights) + count),
            transcendentals=0,
        ),
        name=name,
    )(*lefts, *rights)


def contract_cols(left, right):
    return lax.dot_general(
        left, right, (((1,), (1,)), ((), ())), preferred_element_type=jnp.float32
    )


def target(index, hop, flip, size):
    chips = size // 2
    return ((index // 2 + hop) % chips) * 2 + (index % 2 + flip) % 2


def routed(block, axis, hop, flip):
    size = lax.axis_size(axis)
    return lax.ppermute(block, axis, [(i, target(i, hop, flip, size)) for i in range(size)])


def spread_blocks(block_for, axis):
    size = lax.axis_size(axis)
    me = lax.axis_index(axis)
    received = []
    for flip in range(2):
        for hop in range(size // 2):
            block = block_for(target(me, hop, flip, size))
            received.append(routed(block, axis, hop, flip) if hop or flip else block)
    return received


def gathered_blocks(block, axis):
    chips = lax.axis_size(axis) // 2
    same = [block] + [routed(block, axis, hop, 0) for hop in range(1, chips)]
    return same + [routed(b, axis, 0, 1) for b in same]


def per_device(
    inputs,
    cotangent,
    lengths,
    norm_gain,
    in_weight,
    dt_weight,
    conv_weight,
    conv_bias,
    dt_bias,
    decay_log,
    skip_gain,
    gate_gain,
    out_weight,
):
    first_section = lax.axis_index("section") == 0
    full_in, full_dt, full_out = (
        lax.all_gather(in_weight[0], "fsdp", axis=0, tiled=True),
        lax.all_gather(dt_weight[0], "fsdp", axis=0, tiled=True),
        lax.all_gather(out_weight[0], "fsdp", axis=0, tiled=True),
    )
    own_gain = norm_gain[0]
    inner = gate_gain.shape[1]
    heads = decay_log.shape[1]
    full_dt = jnp.pad(full_dt, ((0, 0), (0, LANES - heads)))
    small = kernel_params(
        (conv_weight[0], conv_bias[0], dt_bias[0], decay_log[0], skip_gain[0], gate_gain[0]), inner
    )
    per_micro = inputs.shape[0] // MICRO
    length = inputs.shape[1]
    row_count = per_micro * length
    model_width = inputs.shape[2]
    proj_cols = full_in.shape[1]
    in_rows = in_weight.shape[1]
    out_rows = out_weight.shape[1]
    positions = jnp.arange(length, dtype=jnp.int32)
    empty_rows = jnp.zeros((row_count, model_width), jnp.float32)

    def micro_rows(source, micro_index):
        return source[micro_index * per_micro : (micro_index + 1) * per_micro].reshape(
            row_count, model_width
        )

    def relayed(rows, distance):
        return passed_along(rows.astype(jnp.bfloat16), "section", distance).astype(jnp.float32)

    def either(a, b):
        return jax.tree.map(lambda x, y: jnp.where(first_section, x, y), a, b)

    layer_inputs = []
    results = []
    kept_all = []
    for tick in range(MICRO + 1):
        arrived = relayed(results[-1], 1) if tick > 0 else empty_rows
        own_rows = micro_rows(inputs, tick) if tick < MICRO else empty_rows
        residual = jnp.where(first_section, own_rows, arrived)
        normed = front_norm(residual, own_gain).astype(jnp.bfloat16)
        projected = jnp.dot(normed, full_in, preferred_element_type=jnp.float32)
        dt_raw = jnp.dot(normed, full_dt, preferred_element_type=jnp.float32)
        mixed, local = mixer_forward(projected, dt_raw, small, length)
        output = residual + jnp.dot(mixed, full_out, preferred_element_type=jnp.float32)
        layer_inputs.append(residual)
        results.append(output)
        kept_all.append((normed, mixed, projected, dt_raw, local))

    columns = [
        jnp.concatenate([either(kept_all[m][j], kept_all[m + 1][j]) for m in range(MICRO)], axis=0).T
        for j in range(2)
    ]

    def columns_of(owner):
        return jnp.concatenate(
            [
                lax.dynamic_slice_in_dim(columns[0], owner * in_rows, in_rows, 0),
                lax.dynamic_slice_in_dim(columns[1], owner * out_rows, out_rows, 0),
            ],
            axis=0,
        )

    lefts = spread_blocks(columns_of, "fsdp")

    grads_back = []
    rounded_all = []
    terms_all = []
    small_all = []
    for tick in range(MICRO + 1):
        returned = relayed(grads_back[-1], -1) if tick > 0 else empty_rows
        if tick < MICRO:
            own_lengths = lengths[tick * per_micro : (tick + 1) * per_micro]
            live_rows = (positions[None, :] < own_lengths[:, None]).astype(jnp.float32)
            top_grad = micro_rows(cotangent, tick) * live_rows.reshape(row_count, 1)
        else:
            top_grad = empty_rows
        later_tick = min(tick + 1, MICRO)
        earlier = max(tick - 1, 0)
        grad_output = jnp.where(first_section, returned, top_grad)
        if tick == 0 or tick == MICRO:
            source = later_tick if tick == 0 else earlier
            residual, kept = layer_inputs[source], kept_all[source][2:]
        else:
            residual, kept = either(
                (layer_inputs[earlier], kept_all[earlier][2:]),
                (layer_inputs[later_tick], kept_all[later_tick][2:]),
            )
        projected, dt_raw, local = kept
        grad_rounded = grad_output.astype(jnp.bfloat16)
        grad_mixed = contract_cols(grad_rounded, full_out)
        grad_cat, *small_terms = mixer_backward(
            projected, dt_raw, local, grad_mixed, small, length
        )
        grad_normed = contract_cols(grad_cat[:, :proj_cols], full_in) + contract_cols(
            grad_cat[:, proj_cols:], full_dt
        )
        _, pull_front = jax.vjp(front_norm, residual, own_gain)
        grad_residual, grad_gain = pull_front(grad_normed)
        grads_back.append(grad_output + grad_residual)
        rounded_all.append(grad_rounded)
        terms_all.append(grad_cat)
        small_all.append([grad_gain] + small_terms)

    gathered_rounded = []
    gathered_terms = []
    for m in range(MICRO):
        gathered_rounded.append(
            gathered_blocks(either(rounded_all[m + 1], rounded_all[m]), "fsdp")
        )
        gathered_terms.append(gathered_blocks(either(terms_all[m + 1], terms_all[m]), "fsdp"))

    def by_source(gathered):
        return [gathered[m][j] for j in range(len(lefts)) for m in range(MICRO)]

    part_out = summed_product(
        lefts, by_source(gathered_rounded), in_rows, out_rows, 768, "out_grad"
    )
    total_out = lax.psum_scatter(part_out, "dp", scatter_dimension=0, tiled=True)
    part_in = summed_product(lefts, by_source(gathered_terms), 0, in_rows, 2304, "in_grad")
    total_in = lax.psum_scatter(part_in, "dp", scatter_dimension=0, tiled=True)
    owned_out = lax.all_gather(total_out, "dp", axis=0, tiled=True).astype(jnp.float32)
    owned_in = lax.all_gather(total_in, "dp", axis=0, tiled=True).astype(jnp.float32)

    gain, taps, bias, gate, skip, head = [sum(terms) for terms in zip(*small_all)]
    skip = skip.reshape(heads, HEAD_DIM).sum(axis=1)
    pieces = [
        gain, taps.reshape(-1), bias[0], head[0, :heads], head[1, :heads], skip, gate[0]
    ]
    flat = lax.psum(jnp.concatenate(pieces), ("dp", "fsdp"))
    totals = []
    start = 0
    for piece in pieces:
        totals.append(flat[start : start + piece.shape[0]])
        start += piece.shape[0]

    layer_out = jnp.concatenate(
        [
            jnp.where(first_section, results[m], results[m + 1]).reshape(
                per_micro, length, model_width
            )
            for m in range(MICRO)
        ],
        axis=0,
    )
    input_grad = jnp.concatenate(
        [
            jnp.where(first_section, grads_back[m + 1], grads_back[m]).reshape(
                per_micro, length, model_width
            )
            for m in range(MICRO)
        ],
        axis=0,
    )
    return (
        layer_out[None],
        input_grad[None],
        totals[0][None],
        owned_in[:, :proj_cols][None],
        owned_in[:, proj_cols : proj_cols + heads][None],
        totals[1].reshape(conv_weight.shape),
        totals[2][None],
        totals[3][None],
        totals[4][None],
        totals[5][None],
        totals[6][None],
        owned_out[None],
    )


def solution(mesh):
    in_specs = (
        P(("dp", "fsdp"), None, None),
        P(("dp", "fsdp"), None, None),
        P(("dp", "fsdp")),
        P("section", None),
        P("section", "fsdp", None),
        P("section", "fsdp", None),
        P("section", None, None),
        P("section", None),
        P("section", None),
        P("section", None),
        P("section", None),
        P("section", None),
        P("section", "fsdp", None),
    )
    out_specs = (
        P("section", ("dp", "fsdp"), None, None),
        P("section", ("dp", "fsdp"), None, None),
        P("section", None),
        P("section", "fsdp", None),
        P("section", "fsdp", None),
        P("section", None, None),
        P("section", None),
        P("section", None),
        P("section", None),
        P("section", None),
        P("section", None),
        P("section", "fsdp", None),
    )
    return jax.shard_map(
        per_device, mesh=mesh, in_specs=in_specs, out_specs=out_specs, check_vma=False
    )
```

time: 1790 us -> 873 us (0.49)
  matrix products: 454 us -> 98.2 us
  waiting for transfers between devices: 865 us -> 551 us
  local copies, waits for them, and re-layouts: 295 us -> 48 us
  other arithmetic: 132 us -> 38.1 us
  Pallas kernels: 0 us -> 89.5 us
    dot_general x63 -> x9, matrix products: 387 us -> 45.1 us  [the longest x3 27.8 us: per_device(): projected = jnp.dot(normed, full_in, preferred_element_type=jnp.float32)]
    reduce_scatter x2, waiting for transfers between devices: 392 us -> 72 us  [the longest x1 72 us: per_device(): total_in = lax.psum_scatter(part_in, 'dp', scatter_dimension=0, tiled=True)]
    all_gather x2, waiting for transfers between devices: 233 us -> 135 us  [the longest x1 90.1 us: per_device(): lax.all_gather(total_in, 'dp', axis=0, tiled=True).astype(jnp.float32)]
    reshape x27 -> x3, local copies, waits for them, and re-layouts: 91.5 us -> 1.36 us  [the longest x1 0.64 us: per_device(): taps.reshape(-1)]
    pallas_call x0 -> x8, Pallas kernels: none -> 89.5 us  [the longest x3 51.3 us: mixer_backward(): pl.pallas_call(functools.partial(mixer_backward_kernel, inner, heads), gr...]
    ppermute x0 -> x15, waiting for transfers between devices: none -> 89.1 us  [routed(): lax.ppermute(block, axis, [(i, target(i, hop, flip, size)) for i in range...]
    reduce_sum x26 -> x1, other arithmetic: 61.7 us -> 0.63 us  [per_device(): skip = skip.reshape(heads, HEAD_DIM).sum(axis=1)]
    unnamed x603 -> x235, local copies, waits for them, and re-layouts: 48.6 us -> 17.5 us
  transfers between devices with their start and end apart: 11 -> 26, of which waited for: 10 -> 13; matrix products, arithmetic and copies ran while one was open for 18% -> 15% of each run, Pallas kernels for 0% -> 7%
where the time goes in v1:
time: 873 us; the launch traced here: 867 us
  waiting for transfers between devices  551 us (63%)
  matrix products  98.2 us (11%)
  Pallas kernels  89.5 us (10%)
  local copies, waits for them, and re-layouts  48 us (5%)
  other arithmetic  38.1 us (4%)
  starting transfers between devices  19.6 us (2%)
  between operations  16.1 us (2%)
    all_gather x1, waiting for transfers between devices, per_device(): lax.all_gather(in_weight[0], 'fsdp', axis=0, tiled=True)  118 us
    all_gather x1, waiting for transfers between devices, per_device(): lax.all_gather(total_in, 'dp', axis=0, tiled=True).astype(jnp.float32)  90.1 us
    ppermute x15, waiting for transfers between devices, routed(): lax.ppermute(block, axis, [(i, target(i, hop, flip, size)) for i in range...  89.1 us
    psum x1, waiting for transfers between devices, per_device(): flat = lax.psum(jnp.concatenate(pieces), ('dp', 'fsdp'))  81.1 us
    reduce_scatter x1, waiting for transfers between devices, per_device(): total_in = lax.psum_scatter(part_in, 'dp', scatter_dimension=0, tiled=True)  72 us
    dot_general x9, matrix products, contract_cols(): lax.dot_general(left, right, (((1,), (1,)), ((), ())), preferred_element_...  53 us
    pallas_call x3, Pallas kernels, mixer_backward(): pl.pallas_call(functools.partial(mixer_backward_kernel, inner, heads), gr...  51.3 us
    all_gather x1, waiting for transfers between devices, per_device(): lax.all_gather(out_weight[0], 'fsdp', axis=0, tiled=True)  47.3 us
  transfers between devices with their start and end apart: 26, of which 13 were waited for; matrix products, arithmetic and copies ran while one was open for 15% of the time, Pallas kernels for 7%

profile of v1, /device:TPU:0, one launch (start us, length us, event | category | flops | bytes accessed | tf_op | source)
XLA Modules:
  0.0 866.8 jit_solution(6002514285264677518)
XLA Ops:
  9.2 6.6 all-gather.1
  18.4 118.3 %all-gather.12.cloned.1.call-done = bf16[1,1536,6400]{2,1,0:T(8,128)(2,1)} async-done(((bf16[1,384,6400]{2,1,0:T(8,128)(2,1)}), bf16[1,1536,6400]{2,1,0:T(8,128)(2,1)}) %all-gather.12.cloned.1.call-update) | async-done | bytes 19660816 | tf_op jit(solution)/shard_map/all_gather | solution.py:449
  136.7 8.1 fusion.10.proj_ref
  144.9 7.5 mixer_forward.3
  155.2 47.3 %all-gather.14.cloned.1.call-done = bf16[1,3072,1536]{2,1,0:T(8,128)(2,1)} async-done(((bf16[1,768,1536]{2,1,0:T(8,128)(2,1)}), bf16[1,3072,1536]{2,1,0:T(8,128)(2,1)}) %all-gather.14.cloned.1.call-update) | async-done | bytes 9437200 | tf_op jit(solution)/shard_map/all_gather | solution.py:451
  202.5 6.2 fusion.99
  224.3 8.2 fusion.8.proj_ref
  232.5 7.5 mixer_forward.4
  241.0 17.5 %mixer_backward.3 = (bf16[128,6528]{1,0:T(8,128)(2,1)S(1)}, f32[4,3328]{1,0:T(4,128)S(1)}, f32[1,3328]{1,0:T(1,128)S(1)}, f32[1,3072]{1,0:T(1,128)S(1)}, f32[1,3072]{1,0:T(1,128)S(1)}, /*index=5*/f32[8,128]{1,0:T(8,128)S(1)}) custom-call(f32[128,6400]{1,0:T(8,128)} %copy-done, f32[128,128]{1,0:T(8,128)S(1)} %fusion.58.dt_ref, ...), custom_call_target="tpu_custom_call" | custom-call | flops 589824000 | bytes 8060928 | tf_op jit(solution)/shard_map/mixer_backward/pallas_call | solution.py:326
  258.5 10.3 %fusion.4 = f32[128,1536]{1,0:T(8,128)S(1)} fusion(bf16[1,1536,6400]{2,1,0:T(8,128)(2,1)} %all-gather.12.cloned.1.call-done, bf16[128,6528]{1,0:T(8,128)(2,1)S(1)} %get-tuple-element.40), kind=kOutput, calls=%fused_computation.4 | convolution fusion | flops 2516582400 | bytes 22085632 | tf_op jit(solution)/shard_map/dot_general | solution.py:400
  274.6 5.2 fusion.27
  280.9 5.6 collective-permute-start.1
  289.2 5.0 collective-permute-done.1
  294.5 11.5 %broadcast_select_fusion.2 = (f32[128,6400]{1,0:T(8,128)}, f32[128,6400]{1,0:T(8,128)S(1)}) fusion(f32[128,6400]{1,0:T(8,128)S(1)} %copy-done.2, pred[]{:T(512)S(6)} %eq.16, bf16[1,1536,6400]{2,1,0:T(8,128)(2,1)} %all-gather.12.cloned.1.call-done, bf16[128,1536]{1,0:T(8,128)(2,1)S(1)} %collective-permute-done.1, f32[128]{0:T(128)S(1)} %add_rsqrt_fusion, ...), kind=kOutput, calls=%fused_computation.47 | convolution fusion | flops 2518384640 | bytes 29891072 | tf_op jit(solution)/shard_map/dot_general | solution.py:489
  306.3 8.0 mixer_forward.5
  321.5 6.9 fusion.14.gm_ref
  328.4 16.9 %mixer_backward.4 = (bf16[128,6528]{1,0:T(8,128)(2,1)S(1)}, f32[4,3328]{1,0:T(4,128)S(1)}, f32[1,3328]{1,0:T(1,128)S(1)}, f32[1,3072]{1,0:T(1,128)S(1)}, f32[1,3072]{1,0:T(1,128)S(1)}, /*index=5*/f32[8,128]{1,0:T(8,128)S(1)}) custom-call(f32[128,6400]{1,0:T(8,128)} %get-tuple-element.116.proj_ref, f32[128,128]{1,0:T(8,128)S(1)} %get-tuple-element.118.dt_ref, ...), custom_call_target="tpu_custom_call" | custom-call | flops 589824000 | bytes 8060928 | tf_op jit(solution)/shard_map/mixer_backward/pallas_call | solution.py:326
  347.1 11.0 %fusion.2 = f32[128,1536]{1,0:T(8,128)S(1)} fusion(bf16[1,1536,6400]{2,1,0:T(8,128)(2,1)} %all-gather.12.cloned.1.call-done, bf16[128,6528]{1,0:T(8,128)(2,1)S(1)} %get-tuple-element.43), kind=kOutput, calls=%fused_computation.2 | convolution fusion | flops 2516582400 | bytes 22085632 | tf_op jit(solution)/shard_map/dot_general | solution.py:400
  384.2 6.9 collective-permute-done.4.refs_1_
  391.9 7.6 collective-permute-done.14.refs_7_
  399.5 6.8 fusion.12.gm_ref
  406.3 17.0 %mixer_backward.5 = (bf16[128,6528]{1,0:T(8,128)(2,1)S(1)}, f32[4,3328]{1,0:T(4,128)S(1)}, f32[1,3328]{1,0:T(1,128)S(1)}, f32[1,3072]{1,0:T(1,128)S(1)}, f32[1,3072]{1,0:T(1,128)S(1)}, /*index=5*/f32[8,128]{1,0:T(8,128)S(1)}) custom-call(f32[128,6400]{1,0:T(8,128)} %copy-done, f32[128,128]{1,0:T(8,128)S(1)} %fusion.58.dt_ref, f32[128,3072]{1,0:T(8,128)S(1)} %copy-done.5, ...), custom_call_target="tpu_custom_call" | custom-call | flops 589824000 | bytes 8060928 | tf_op jit(solution)/shard_map/mixer_backward/pallas_call | solution.py:326
  426.4 5.3 out_grad.1
  437.0 36.8 %collective-permute-done.7.refs_6_ = bf16[128,6528]{1,0:T(8,128)(2,1)S(1)} collective-permute-done((bf16[128,6528]{1,0:T(8,128)(2,1)S(1)}, bf16[128,6528]{1,0:T(8,128)(2,1)S(1)}, u32[]{:S(2)}, u32[]{:S(2)}) %collective-permute-start.7) | collective-permute-done | bytes 1671200 | tf_op jit(solution)/shard_map/ppermute | solution.py:412
  473.9 35.4 %collective-permute-done.8.refs_7_ = bf16[128,6528]{1,0:T(8,128)(2,1)S(1)} collective-permute-done((bf16[128,6528]{1,0:T(8,128)(2,1)S(1)}, bf16[128,6528]{1,0:T(8,128)(2,1)S(1)}, u32[]{:S(2)}, u32[]{:S(2)}) %collective-permute-start.8) | collective-permute-done | bytes 1671200 | tf_op jit(solution)/shard_map/ppermute | solution.py:412
  513.0 9.9 %in_grad.1 = bf16[384,6528]{1,0:T(8,128)(2,1)} custom-call(bf16[1152,256]{1,0:T(8,128)(2,1)S(1)} %copy-done.12, bf16[1152,256]{1,0:T(8,128)(2,1)S(1)} %copy-done.16, bf16[1152,256]{1,0:T(8,128)(2,1)} %collective-permute-done.5.refs_2_, bf16[1152,256]{1,0:T(8,128)(2,1)S(1)} %copy-done.18, bf16[128,6528]{1,0:T(8,128)(2,1)S(1)} %get-tuple-element.93.refs_4_, ...), custom_call_target="tpu_custom_call" | custom-call | flops 5133828096 | bytes 18382848 | tf_op jit(solution)/shard_map/in_grad/pallas_call | solution.py:382
  526.3 11.1 %fusion = f32[128,1536]{1,0:T(8,128)S(1)} fusion(bf16[1,1536,6400]{2,1,0:T(8,128)(2,1)} %all-gather.12.cloned.1.call-done, bf16[128,6528]{1,0:T(8,128)(2,1)S(1)} %get-tuple-element.44), kind=kOutput, calls=%fused_computation | convolution fusion | flops 2516582400 | bytes 22085632 | tf_op jit(solution)/shard_map/dot_general | solution.py:400
  541.7 72.0 %reduce-scatter.3.cloned.1.call-done = bf16[96,6528]{1,0:T(8,128)(2,1)} async-done(((bf16[384,6528]{1,0:T(8,128)(2,1)}), bf16[96,6528]{1,0:T(8,128)(2,1)}) %reduce-scatter.3.cloned.1.call-update) | async-done | bytes 1253392 | tf_op jit(solution)/shard_map/reduce_scatter | solution.py:568
  613.7 5.2 fusion.36
  623.4 81.1 %all-reduce.5.cloned.1.call-done = f32[21392]{0:T(1024)} async-done(((f32[21392]{0:T(1024)}), f32[21392]{0:T(1024)}) %all-reduce.5.cloned.1.call-update) | async-done | bytes 85584 | tf_op jit(solution)/shard_map/psum | solution.py:577
  711.4 45.3 %all-gather.10.cloned.1.call-done = bf16[768,1536]{1,0:T(8,128)(2,1)} async-done(((bf16[192,1536]{1,0:T(8,128)(2,1)}), bf16[768,1536]{1,0:T(8,128)(2,1)}) %all-gather.10.cloned.1.call-update) | async-done | bytes 2359312 | tf_op jit(solution)/shard_map/all_gather | solution.py:569
  761.2 90.1 %all-gather.8.cloned.1.call-done = bf16[384,6528]{1,0:T(8,128)(2,1)} async-done(((bf16[96,6528]{1,0:T(8,128)(2,1)}), bf16[384,6528]{1,0:T(8,128)(2,1)}) %all-gather.8.cloned.1.call-update) | async-done | bytes 5013520 | tf_op jit(solution)/shard_map/all_gather | solution.py:570
  (361 shorter events, 112.9 us)
Async XLA Ops:
  7.2 129.5 %all-gather.12.cloned.1.call-start = ((), (), s32[]{:S(2)}) async-start(), calls=%async_computation.7 | async-start | bytes 24576000 | tf_op jit(solution)/shard_map/all_gather | solution.py:449
  8.0 194.5 %all-gather.14.cloned.1.call-start = ((), (), s32[]{:S(2)}) async-start(), calls=%async_computation.8 | async-start | bytes 11796480 | tf_op jit(solution)/shard_map/all_gather | solution.py:451
  8.7 532.4 %reduce-scatter.5.cloned.1.call-start = ((), (), s32[]{:S(2)}) async-start(), calls=%async_computation.5 | async-start | bytes 2949120 | tf_op jit(solution)/shard_map/reduce_scatter | solution.py:566
  9.1 357.3 %copy-start.96 = (f32[1536]{0:T(1024)}, f32[1536]{0:T(1024)S(1)}, u32[]{:S(2)}) copy-start(f32[1536]{0:T(1024)S(1)} %reduce) | copy-start | bytes 18436
  15.8 129.0 %copy-start.91 = (bf16[1,1536,48]{1,2,0:T(8,128)(2,1)}, bf16[1,1536,48]{1,2,0:T(8,128)(2,1)S(1)}, u32[]{:S(2)}) copy-start(bf16[1,1536,48]{1,2,0:T(8,128)(2,1)S(1)} %all-gather.1) | copy-start | bytes 442372
  17.7 288.6 %copy-start.46 = (f32[1,128]{1,0:T(1,128)}, f32[1,128]{1,0:T(1,128)S(1)}, u32[]{:S(2)}) copy-start(f32[1,128]{1,0:T(1,128)S(1)} %get-tuple-element.123.dtb_ref) | copy-start | bytes 1540
  17.8 310.6 %copy-start.44 = (f32[1,128]{1,0:T(1,128)}, f32[1,128]{1,0:T(1,128)S(1)}, u32[]{:S(2)}) copy-start(f32[1,128]{1,0:T(1,128)S(1)} %get-tuple-element.122.dlog_ref) | copy-start | bytes 1540
  18.3 126.5 %copy-start.55 = (f32[128,128]{1,0:T(8,128)}, f32[128,128]{1,0:T(8,128)S(1)}, u32[]{:S(2)}) copy-start(f32[128,128]{1,0:T(8,128)S(1)} %fusion.60.dt_ref) | copy-start | bytes 196612
  18.3 126.5 %copy-start.19 = (f32[1,4,3328]{2,1,0:T(4,128)S(1)}, f32[1,4,3328]{2,1,0:T(4,128)}, u32[]{:S(2)}) copy-start(f32[1,4,3328]{2,1,0:T(4,128)} %param.19) | copy-start | bytes 159748
  208.7 12.6 %collective-permute-start = (bf16[128,1536]{1,0:T(8,128)(2,1)}, bf16[128,1536]{1,0:T(8,128)(2,1)}, u32[]{:S(2)}, u32[]{:S(2)}) collective-permute-start(bf16[128,1536]{1,0:T(8,128)(2,1)} %get-tuple-element.113), channel_id=1, source_target_pairs={{0,16},{1,17},{2,18},{3,19},{4,20},{5,21},{6,22},{7,23},{8,24},{9,... | collective-permute-start | bytes 1179656 | tf_op jit(solution)/shard_map/ppermute | solution.py:23
  271.7 14.8 %collective-permute-start.2 = (bf16[128,1536]{1,0:T(8,128)(2,1)}, bf16[128,1536]{1,0:T(8,128)(2,1)}, u32[]{:S(2)}, u32[]{:S(2)}) collective-permute-start(bf16[128,1536]{1,0:T(8,128)(2,1)} %get-tuple-element.86), channel_id=1, source_target_pairs={{16,0},{17,1},{18,2},{19,3},{20,4},{21,5},{22,6},{23,7},{24,8},{25... | collective-permute-start | bytes 1179656 | tf_op jit(solution)/shard_map/ppermute | solution.py:23
  280.9 13.3 %collective-permute-start.1 = (bf16[128,1536]{1,0:T(8,128)(2,1)S(1)}, bf16[128,1536]{1,0:T(8,128)(2,1)S(1)}, u32[]{:S(2)}, u32[]{:S(2)}) collective-permute-start(bf16[128,1536]{1,0:T(8,128)(2,1)S(1)} %get-tuple-element.105), channel_id=1, source_target_pairs={{0,16},{1,17},{2,18},{3,19},{4,20},{5,21},{6,22},{7,23},{8,24},{9,... | collective-permute-start | bytes 1179656 | tf_op jit(solution)/shard_map/ppermute | solution.py:23
  288.6 94.8 %collective-permute-start.13 = (bf16[128,1536]{1,0:T(8,128)(2,1)}, bf16[128,1536]{1,0:T(8,128)(2,1)}, u32[]{:S(2)}, u32[]{:S(2)}) collective-permute-start(bf16[128,1536]{1,0:T(8,128)(2,1)} %get-tuple-element.80.refs_4_), channel_id=1, source_target_pairs={{0,2},{1,3},{2,0},{3,1},{4,6},{5,7},{6,4},{7,5},{8,10},{9,11},{10,... | collective-permute-start | bytes 1179656 | tf_op jit(solution)/shard_map/ppermute | solution.py:412
  289.2 94.7 %collective-permute-start.15 = (bf16[128,1536]{1,0:T(8,128)(2,1)}, bf16[128,1536]{1,0:T(8,128)(2,1)}, u32[]{:S(2)}, u32[]{:S(2)}) collective-permute-start(bf16[128,1536]{1,0:T(8,128)(2,1)} %get-tuple-element.80.refs_4_), channel_id=1, source_target_pairs={{0,1},{1,0},{2,3},{3,2},{4,5},{5,4},{6,7},{7,6},{8,9},{9,8},{10,11... | collective-permute-start | bytes 1179656 | tf_op jit(solution)/shard_map/ppermute | solution.py:412
  363.8 16.8 %collective-permute-start.3 = (bf16[128,1536]{1,0:T(8,128)(2,1)}, bf16[128,1536]{1,0:T(8,128)(2,1)S(1)}, u32[]{:S(2)}, u32[]{:S(2)}) collective-permute-start(bf16[128,1536]{1,0:T(8,128)(2,1)} %convert_element_type.82), channel_id=1, source_target_pairs={{16,0},{17,1},{18,2},{19,3},{20,4},{21,5},{22,6},{23,7},{24,8},{25... | collective-permute-start | bytes 1179656 | tf_op jit(solution)/shard_map/ppermute | solution.py:23
  374.6 16.4 %collective-permute-start.4 = (bf16[1152,256]{1,0:T(8,128)(2,1)}, bf16[1152,256]{1,0:T(8,128)(2,1)S(1)}, u32[]{:S(2)}, u32[]{:S(2)}) collective-permute-start(bf16[1152,256]{1,0:T(8,128)(2,1)} %pad_maximum_fusion.1), channel_id=1, source_target_pairs={{0,2},{1,3},{2,0},{3,1},{4,6},{5,7},{6,4},{7,5},{8,10},{9,11},{10,... | collective-permute-start | bytes 1769480 | tf_op jit(solution)/shard_map/ppermute | solution.py:412
  378.9 47.4 %collective-permute-start.5 = (bf16[1152,256]{1,0:T(8,128)(2,1)}, bf16[1152,256]{1,0:T(8,128)(2,1)}, u32[]{:S(2)}, u32[]{:S(2)}) collective-permute-start(bf16[1152,256]{1,0:T(8,128)(2,1)} %pad_maximum_fusion.2), channel_id=1, source_target_pairs={{0,1},{1,0},{2,3},{3,2},{4,5},{5,4},{6,7},{7,6},{8,9},{9,8},{10,11... | collective-permute-start | bytes 1769480 | tf_op jit(solution)/shard_map/ppermute | solution.py:412
  380.8 18.7 %collective-permute-start.14 = (bf16[128,1536]{1,0:T(8,128)(2,1)S(1)}, bf16[128,1536]{1,0:T(8,128)(2,1)S(1)}, u32[]{:S(2)}, u32[]{:S(2)}) collective-permute-start(bf16[128,1536]{1,0:T(8,128)(2,1)S(1)} %broadcast_select_fusion.6.refs_5_), channel_id=1, source_target_pairs={{0,2},{1,3},{2,0},{3,1},{4,6},{5,7},{6,4},{7,5},{8,10},{9,11},{10,... | collective-permute-start | bytes 1179656 | tf_op jit(solution)/shard_map/ppermute | solution.py:412
  383.5 42.8 %collective-permute-start.6 = (bf16[1152,256]{1,0:T(8,128)(2,1)S(1)}, bf16[1152,256]{1,0:T(8,128)(2,1)S(1)}, u32[]{:S(2)}, u32[]{:S(2)}) collective-permute-start(bf16[1152,256]{1,0:T(8,128)(2,1)S(1)} %pad_maximum_fusion.3), channel_id=1, source_target_pairs={{0,3},{1,2},{2,1},{3,0},{4,7},{5,6},{6,5},{7,4},{8,11},{9,10},{10,... | collective-permute-start | bytes 1769480 | tf_op jit(solution)/shard_map/ppermute | solution.py:412
  383.9 42.4 %collective-permute-start.16 = (bf16[128,1536]{1,0:T(8,128)(2,1)S(1)}, bf16[128,1536]{1,0:T(8,128)(2,1)S(1)}, u32[]{:S(2)}, u32[]{:S(2)}) collective-permute-start(bf16[128,1536]{1,0:T(8,128)(2,1)S(1)} %broadcast_select_fusion.6.refs_5_), channel_id=1, source_target_pairs={{0,1},{1,0},{2,3},{3,2},{4,5},{5,4},{6,7},{7,6},{8,9},{9,8},{10,11... | collective-permute-start | bytes 1179656 | tf_op jit(solution)/shard_map/ppermute | solution.py:412
  391.9 34.4 %collective-permute-start.17 = (bf16[128,1536]{1,0:T(8,128)(2,1)}, bf16[128,1536]{1,0:T(8,128)(2,1)S(1)}, u32[]{:S(2)}, u32[]{:S(2)}) collective-permute-start(bf16[128,1536]{1,0:T(8,128)(2,1)} %collective-permute-done.13.refs_6_), channel_id=1, source_target_pairs={{0,1},{1,0},{2,3},{3,2},{4,5},{5,4},{6,7},{7,6},{8,9},{9,8},{10,11... | collective-permute-start | bytes 1179656 | tf_op jit(solution)/shard_map/ppermute | solution.py:412
  399.5 26.8 %collective-permute-start.18 = (bf16[128,1536]{1,0:T(8,128)(2,1)S(1)}, bf16[128,1536]{1,0:T(8,128)(2,1)S(1)}, u32[]{:S(2)}, u32[]{:S(2)}) collective-permute-start(bf16[128,1536]{1,0:T(8,128)(2,1)S(1)} %collective-permute-done.14.refs_7_), channel_id=1, source_target_pairs={{0,1},{1,0},{2,3},{3,2},{4,5},{5,4},{6,7},{7,6},{8,9},{9,8},{10,11... | collective-permute-start | bytes 1179656 | tf_op jit(solution)/shard_map/ppermute | solution.py:412
  432.5 181.2 %reduce-scatter.3.cloned.1.call-start = ((), (), s32[]{:S(2)}) async-start(), calls=%async_computation.3 | async-start | bytes 6266880 | tf_op jit(solution)/shard_map/reduce_scatter | solution.py:568
  434.4 39.4 %collective-permute-start.7 = (bf16[128,6528]{1,0:T(8,128)(2,1)S(1)}, bf16[128,6528]{1,0:T(8,128)(2,1)S(1)}, u32[]{:S(2)}, u32[]{:S(2)}) collective-permute-start(bf16[128,6528]{1,0:T(8,128)(2,1)S(1)} %get-tuple-element.93.refs_4_), channel_id=1, source_target_pairs={{0,2},{1,3},{2,0},{3,1},{4,6},{5,7},{6,4},{7,5},{8,10},{9,11},{10,... | collective-permute-start | bytes 5013512 | tf_op jit(solution)/shard_map/ppermute | solution.py:412
  435.1 74.2 %collective-permute-start.8 = (bf16[128,6528]{1,0:T(8,128)(2,1)S(1)}, bf16[128,6528]{1,0:T(8,128)(2,1)S(1)}, u32[]{:S(2)}, u32[]{:S(2)}) collective-permute-start(bf16[128,6528]{1,0:T(8,128)(2,1)S(1)} %get-tuple-element.92.refs_5_), channel_id=1, source_target_pairs={{0,2},{1,3},{2,0},{3,1},{4,6},{5,7},{6,4},{7,5},{8,10},{9,11},{10,... | collective-permute-start | bytes 5013512 | tf_op jit(solution)/shard_map/ppermute | solution.py:412
  436.5 72.7 %collective-permute-start.9 = (bf16[128,6528]{1,0:T(8,128)(2,1)S(1)}, bf16[128,6528]{1,0:T(8,128)(2,1)S(1)}, u32[]{:S(2)}, u32[]{:S(2)}) collective-permute-start(bf16[128,6528]{1,0:T(8,128)(2,1)S(1)} %get-tuple-element.93.refs_4_), channel_id=1, source_target_pairs={{0,1},{1,0},{2,3},{3,2},{4,5},{5,4},{6,7},{7,6},{8,9},{9,8},{10,11... | collective-permute-start | bytes 5013512 | tf_op jit(solution)/shard_map/ppermute | solution.py:412
  436.5 72.7 %collective-permute-start.10 = (bf16[128,6528]{1,0:T(8,128)(2,1)S(1)}, bf16[128,6528]{1,0:T(8,128)(2,1)S(1)}, u32[]{:S(2)}, u32[]{:S(2)}) collective-permute-start(bf16[128,6528]{1,0:T(8,128)(2,1)S(1)} %get-tuple-element.92.refs_5_), channel_id=1, source_target_pairs={{0,1},{1,0},{2,3},{3,2},{4,5},{5,4},{6,7},{7,6},{8,9},{9,8},{10,11... | collective-permute-start | bytes 5013512 | tf_op jit(solution)/shard_map/ppermute | solution.py:412
  473.9 35.4 %collective-permute-start.11 = (bf16[128,6528]{1,0:T(8,128)(2,1)S(1)}, bf16[128,6528]{1,0:T(8,128)(2,1)S(1)}, u32[]{:S(2)}, u32[]{:S(2)}) collective-permute-start(bf16[128,6528]{1,0:T(8,128)(2,1)S(1)} %collective-permute-done.7.refs_6_), channel_id=1, source_target_pairs={{0,1},{1,0},{2,3},{3,2},{4,5},{5,4},{6,7},{7,6},{8,9},{9,8},{10,11... | collective-permute-start | bytes 5013512 | tf_op jit(solution)/shard_map/ppermute | solution.py:412
  509.2 3.7 collective-permute-start.12
  523.0 181.5 %all-reduce.5.cloned.1.call-start = ((), (), s32[]{:S(2)}) async-start(), calls=%async_computation.2 | async-start | bytes 172032 | tf_op jit(solution)/shard_map/psum | solution.py:577
  541.0 215.7 %all-gather.10.cloned.1.call-start = ((), (), s32[]{:S(2)}) async-start(), calls=%async_computation.6 | async-start | bytes 2949120 | tf_op jit(solution)/shard_map/all_gather | solution.py:569
  541.6 309.7 %all-gather.8.cloned.1.call-start = ((), (), s32[]{:S(2)}) async-start(), calls=%async_computation.4 | async-start | bytes 6266880 | tf_op jit(solution)/shard_map/all_gather | solution.py:570
  (111 other events, 1456.5 us)
Sparse Core Ops, SparseCore 0:
  9.6 127.0 all-gather.11
  138.2 64.2 all-gather.13
  432.6 48.2 reduce-scatter.4
  523.1 90.5 reduce-scatter.2
  617.0 87.4 all-reduce.4
  705.9 50.7 all-gather.9
  758.3 93.0 all-gather.7

commit v2 on v1

--- a/solution.py
+++ b/solution.py
@@ -6,6 +6,7 @@
 from jax.experimental import pallas as pl
 from jax.experimental.pallas import tpu as pltpu
 from jax.sharding import PartitionSpec as P
+
 
 HEAD_DIM = 64
 STATE = 128
@@ -93,7 +94,7 @@
 
 def mixer_forward_kernel(
     inner, heads, proj_ref, dt_ref, taps_ref, bias_ref, dtb_ref, dlog_ref, skip_ref, gain_ref,
-    mixed_ref, local_ref, cum_t, col_b, step_b, gated_s,
+    mixed_ref, mixed_t_ref, local_ref, cum_t, col_b, step_b, gated_s,
 ):
     length = proj_ref.shape[0]
     square = (length, LANES)
@@ -133,7 +134,9 @@
 
     def scale(i, _):
         chan = pl.ds(pl.multiple_of(i * LANES, LANES), LANES)
-        mixed_ref[:, chan] = (gated_s[:, chan] * inverse * gain_ref[:, chan]).astype(jnp.bfloat16)
+        mixed = gated_s[:, chan] * inverse * gain_ref[:, chan]
+        mixed_ref[:, chan] = mixed.astype(jnp.bfloat16)
+        mixed_t_ref[chan, :] = mixed.T.astype(jnp.bfloat16)
         return 0
 
     lax.fori_loop(0, inner // LANES, scale, 0)
@@ -150,7 +153,7 @@
     rows = iota(square, 0)
     lanes = iota(square, 1)
     left = lanes < HEAD_DIM
-    raw, step, rate, log_decay = decays(dt_ref, dtb_ref, dlog_ref, cum_t, col_b, step_b, heads)
+    raw, _, rate, log_decay = decays(dt_ref, dtb_ref, dlog_ref, cum_t, col_b, step_b, heads)
     pairs = inner // LANES
 
     @pl.when(pl.program_id(0) == 0)
@@ -303,9 +306,14 @@
         grid=(row_count // length,),
         in_specs=[by_sequence(length, cols), by_sequence(length, LANES)]
         + [whole(p.shape) for p in params],
-        out_specs=[by_sequence(length, inner), by_sequence(length, inner)],
+        out_specs=[
+            by_sequence(length, inner),
+            pl.BlockSpec((inner, length), lambda s: (0, s)),
+            by_sequence(length, inner),
+        ],
         out_shape=[
             jax.ShapeDtypeStruct((row_count, inner), jnp.bfloat16),
+            jax.ShapeDtypeStruct((inner, row_count), jnp.bfloat16),
             jax.ShapeDtypeStruct((row_count, inner), jnp.float32),
         ],
         scratch_shapes=scratch(length, heads) + [pltpu.VMEM((length, inner), jnp.float32)],
@@ -376,7 +384,7 @@
     return max(t for t in range(LANES, most + 1, LANES) if columns % t == 0)
 
 
-def summed_product(lefts, rights, first, count, most, name):
+def summed_product(lefts, rights, first, count, most):
     length, columns = rights[0].shape
     tile = tile_of(columns, most)
     return pl.pallas_call(
@@ -392,8 +400,175 @@
             bytes_accessed=2 * columns * (length * len(rights) + count),
             transcendentals=0,
         ),
-        name=name,
     )(*lefts, *rights)
+
+
+def relative_rows(pieces):
+    return jnp.concatenate([piece[...] for piece in pieces], axis=0)
+
+
+def aligned(rows):
+    return rows % LANES == 0
+
+
+def forward_product_kernel(rows, count, order_ref, left_ref, *refs):
+    pieces, left_s, outs = refs[:count], refs[-1], refs[count:-1]
+
+    @pl.when(pl.program_id(0) == 0)
+    def _():
+        if aligned(rows):
+            for j in range(left_ref.shape[1] // rows):
+                source = pl.ds(pl.multiple_of(order_ref[j] * rows, LANES), rows)
+                left_s[:, j * rows : (j + 1) * rows] = left_ref[:, source]
+        else:
+            left_s[...] = left_ref[...]
+
+    total = bf_dot(left_s[...], relative_rows(pieces))
+    if len(outs) == 1:
+        outs[0][...] = total
+    else:
+        total = total + outs[0][...]
+        outs[1][...] = total
+        outs[2][...] = total.astype(jnp.bfloat16)
+
+
+def reordered(block, rows, places):
+    return jnp.concatenate(
+        [
+            lax.dynamic_slice_in_dim(block, places[j] * rows, rows, 1)
+            for j in range(block.shape[1] // rows)
+        ],
+        axis=1,
+    )
+
+
+def piece_specs(pieces, tile):
+    return [pl.BlockSpec((p.shape[0], tile), lambda t, order: (0, t)) for p in pieces]
+
+
+def forward_product(left, pieces, rows, order, most, residual=None):
+    row_count, depth = left.shape
+    columns = pieces[0].shape[1]
+    tile = tile_of(columns, most)
+    if not aligned(rows):
+        left = reordered(left, rows, order)
+    block = pl.BlockSpec((row_count, tile), lambda t, order: (0, t))
+    shape = jax.ShapeDtypeStruct((row_count, columns), jnp.float32)
+    extra = [] if residual is None else [residual]
+    out = pl.pallas_call(
+        functools.partial(forward_product_kernel, rows, len(pieces)),
+        grid_spec=pltpu.PrefetchScalarGridSpec(
+            num_scalar_prefetch=1,
+            grid=(columns // tile,),
+            in_specs=[pl.BlockSpec((row_count, depth), lambda t, order: (0, 0))]
+            + piece_specs(pieces, tile)
+            + [block for _ in extra],
+            out_specs=[block] + [block for _ in extra],
+            scratch_shapes=[pltpu.VMEM((row_count, depth), jnp.bfloat16)],
+        ),
+        out_shape=[shape]
+        + [jax.ShapeDtypeStruct((row_count, columns), jnp.bfloat16) for _ in extra],
+        compiler_params=pltpu.CompilerParams(vmem_limit_bytes=32 * 1024 * 1024),
+        cost_estimate=pl.CostEstimate(
+            flops=2 * row_count * depth * columns,
+            bytes_accessed=2 * depth * columns + 4 * row_count * columns,
+            transcendentals=0,
+        ),
+    )(order, left, *pieces, *extra)
+    return out if extra else out[0]
+
+
+def backward_product_kernel(rows, count, order_ref, left_ref, *refs):
+    pieces, out_ref, total_s = refs[:count], refs[count], refs[-1]
+    step = pl.program_id(0)
+    term = lax.dot_general(
+        left_ref[...],
+        relative_rows(pieces),
+        (((1,), (1,)), ((), ())),
+        preferred_element_type=jnp.float32,
+    )
+
+    @pl.when(step == 0)
+    def _():
+        total_s[...] = term
+
+    @pl.when(step > 0)
+    def _():
+        total_s[...] += term
+
+    @pl.when(step == pl.num_programs(0) - 1)
+    def _():
+        if aligned(rows):
+            for j in range(out_ref.shape[1] // rows):
+                where = pl.ds(pl.multiple_of(order_ref[j] * rows, LANES), rows)
+                out_ref[:, where] = total_s[:, j * rows : (j + 1) * rows]
+        else:
+            out_ref[...] = total_s[...]
+
+
+def backward_product(left, pieces, rows, order, places, most):
+    row_count = left.shape[0]
+    depth = sum(p.shape[0] for p in pieces)
+    columns = pieces[0].shape[1]
+    tile = tile_of(columns, most)
+    out = pl.pallas_call(
+        functools.partial(backward_product_kernel, rows, len(pieces)),
+        grid_spec=pltpu.PrefetchScalarGridSpec(
+            num_scalar_prefetch=1,
+            grid=(columns // tile,),
+            in_specs=[pl.BlockSpec((row_count, tile), lambda t, order: (0, t))]
+            + piece_specs(pieces, tile),
+            out_specs=pl.BlockSpec((row_count, depth), lambda t, order: (0, 0)),
+            scratch_shapes=[pltpu.VMEM((row_count, depth), jnp.float32)],
+        ),
+        out_shape=jax.ShapeDtypeStruct((row_count, depth), jnp.float32),
+        compiler_params=pltpu.CompilerParams(vmem_limit_bytes=32 * 1024 * 1024),
+        cost_estimate=pl.CostEstimate(
+            flops=2 * row_count * depth * columns,
+            bytes_accessed=2 * depth * columns + 4 * row_count * depth,
+            transcendentals=0,
+        ),
+    )(order, left, *pieces)
+    return out if aligned(rows) else reordered(out, rows, places)
+
+
+def expand_kernel(pairs, extra, order_ref, first_ref, *refs):
+    moved, outs = refs[: 2 * pairs], refs[2 * pairs + extra :]
+    rows = first_ref.shape[0]
+    wide = outs[0].shape[1]
+    for k in range(pairs + 1):
+        if k == 0:
+            block = first_ref[...].astype(jnp.float32)
+        else:
+            block = jnp.where(order_ref[0] >= k, moved[2 * k - 2][...], moved[2 * k - 1][...])
+            block = block.astype(jnp.float32)
+        where = pl.ds(pl.multiple_of(order_ref[k] * rows, 8), rows)
+        outs[0][where, :] = block[:, :wide]
+        if len(outs) > 1:
+            outs[1][where, :] = block[:, wide:]
+
+
+def expanded(parts, order, chunk, chunks, wide, before):
+    first, pairs = parts
+    moved = [block for pair in pairs for block in pair]
+    rows, columns = first.shape
+    total = rows * (len(pairs) + 1)
+    widths = [wide] if wide == columns else [wide, columns - wide]
+    prior = [] if before is None else list(before)
+    inputs = [first] + moved
+    return pl.pallas_call(
+        functools.partial(expand_kernel, len(pairs), len(prior)),
+        grid_spec=pltpu.PrefetchScalarGridSpec(
+            num_scalar_prefetch=1,
+            grid=(1,),
+            in_specs=[pl.BlockSpec((rows, columns), lambda t, order: (0, 0)) for _ in inputs]
+            + [pl.BlockSpec(memory_space=pl.ANY) for _ in prior],
+            out_specs=[pl.BlockSpec((total, w), lambda t, order: (chunk, 0)) for w in widths],
+        ),
+        out_shape=[jax.ShapeDtypeStruct((total * chunks, w), jnp.float32) for w in widths],
+        input_output_aliases={1 + len(inputs) + i: i for i in range(len(prior))},
+        compiler_params=pltpu.CompilerParams(vmem_limit_bytes=40 * 1024 * 1024),
+    )(order, *inputs, *prior)
 
 
 def contract_cols(left, right):
@@ -427,6 +602,111 @@
     chips = lax.axis_size(axis) // 2
     same = [block] + [routed(block, axis, hop, 0) for hop in range(1, chips)]
     return same + [routed(b, axis, 0, 1) for b in same]
+
+
+def line_pipeline(ready, parts, axis):
+    size = lax.axis_size(axis)
+    here = lax.axis_index(axis)
+    rights = [{0: ready}] + [{} for _ in parts]
+    lefts = [{0: ready}] + [{} for _ in parts]
+    sums = [None for _ in parts]
+
+    def block_of(part, index):
+        owned = part.reshape(size, part.shape[0] // size, part.shape[1])
+        at = jnp.clip(index, 0, size - 1)
+        return lax.dynamic_index_in_dim(owned, at, 0, keepdims=False).astype(jnp.float32)
+
+    def added(block, *others):
+        for other in others:
+            block = block + other.astype(jnp.float32)
+        return block.astype(jnp.bfloat16)
+
+    for slot in range(1, size * (len(parts) + 1)):
+        moved, keys = [], []
+        adding, passing = None, None
+        for i, part in enumerate(parts):
+            step = slot - size * i - 1
+            if 1 <= step < size:
+                before = sums[i] or ()
+                up = added(block_of(part, size - step + here), *before[:1])
+                down = added(block_of(part, step - size + here), *before[1:])
+                adding = (i, step, up, down)
+        for i in range(len(parts) + 1):
+            step = slot - size * i
+            if 1 <= step < size:
+                passing = (i, step, rights[i][step - 1], lefts[i][step - 1])
+        every = range(size)
+        if adding and passing and adding[2].shape == passing[2].shape:
+            step = adding[1]
+            up = jnp.where(here < step, adding[2], passing[2])
+            down = jnp.where(here > size - 1 - step, adding[3], passing[3])
+            up = lax.ppermute(up, axis, [(j, j + 1) for j in every if j + 1 < size])
+            down = lax.ppermute(down, axis, [(j, j - 1) for j in every if j > 0])
+            moved += [(up, down)] * 2
+            keys += [("sum", adding[0]), ("pass", *passing[:2])]
+        else:
+            for what, job in (("sum", adding), ("pass", passing)):
+                if job is None:
+                    continue
+                first = 0 if what == "sum" else job[1] - 1
+                last = job[1] if what == "sum" else size
+                ups = [(j, j + 1) for j in every if first <= j < last and j + 1 < size]
+                downs = [(size - 1 - a, size - 1 - b) for a, b in ups]
+                up = lax.ppermute(job[2], axis, ups)
+                down = lax.ppermute(job[3], axis, downs)
+                moved.append((up, down))
+                keys.append((what, *job[:2]))
+        got = dict(zip(keys, lax.optimization_barrier(tuple(moved))))
+        for (what, i, *step), (up, down) in got.items():
+            if what == "pass":
+                rights[i][step[0]], lefts[i][step[0]] = up, down
+            else:
+                sums[i] = (up, down)
+                if slot - size * i == size:
+                    own = added(block_of(parts[i], here), up, down)
+                    rights[i + 1][0] = lefts[i + 1][0] = own
+    return [
+        (rights[i][0], [(rights[i][k], lefts[i][size - k]) for k in range(1, size)])
+        for i in range(len(parts) + 1)
+    ]
+
+
+def gathered_weights(owns, narrow, share):
+    size = lax.axis_size("dp")
+    chips = lax.axis_size("fsdp") // 2
+    stripes = [int(own.shape[0] * share) // (16 * size) * 16 for own in owns]
+    directs = [own.shape[0] - stripe * size for own, stripe in zip(owns, stripes)]
+    arrived = []
+    for i, own in enumerate(owns):
+        start = directs[i] + lax.axis_index("dp") * stripes[i]
+        part = lax.dynamic_slice_in_dim(own, start, stripes[i], 0)
+        hops = range(1, chips) if stripes[i] else ()
+        arrived.append([routed(part, "fsdp", hop, 0) for hop in hops])
+    narrows = [narrow] + [routed(narrow, "fsdp", hop, 0) for hop in range(1, chips)]
+    narrows += [routed(block, "fsdp", 0, 1) for block in narrows]
+    arrived, owns, narrows = lax.optimization_barrier((arrived, owns, narrows))
+    full = []
+    for i, own in enumerate(owns):
+        same = [own]
+        for hop in range(1, chips):
+            same.append(routed(own[: directs[i]], "fsdp", hop, 0))
+            if stripes[i]:
+                same.append(
+                    lax.all_gather(arrived[i][hop - 1], "dp", axis=0, tiled=True)
+                )
+        other = [routed(own, "fsdp", 0, 1)]
+        other += [routed(piece, "fsdp", 0, 1) for piece in same[1:]]
+        full.append(same + other)
+    return full, narrows
+
+
+def butterfly_sum(block, axis):
+    size = lax.axis_size(axis)
+    distance = 1
+    while distance < size:
+        block = block + lax.ppermute(block, axis, [(i, i ^ distance) for i in range(size)])
+        distance *= 2
+    return block
 
 
 def per_device(
@@ -445,14 +725,32 @@
     out_weight,
 ):
     first_section = lax.axis_index("section") == 0
-    full_in, full_dt, full_out = (
-        lax.all_gather(in_weight[0], "fsdp", axis=0, tiled=True),
-        lax.all_gather(dt_weight[0], "fsdp", axis=0, tiled=True),
-        lax.all_gather(out_weight[0], "fsdp", axis=0, tiled=True),
-    )
+    (in_pieces, out_pieces), dt_blocks = gathered_weights(
+        (in_weight[0], out_weight[0]), dt_weight[0], 1 / 2
+    )
+    ranks = lax.axis_size("fsdp")
+    chips = ranks // 2
+    place = lax.axis_index("fsdp")
+    order = jnp.stack(
+        [
+            (place // 2 - hop) % chips * 2 + (place + flip) % 2
+            for flip in range(2)
+            for hop in range(chips)
+        ]
+    ).astype(jnp.int32)
+    places = jnp.stack(
+        [
+            (place + owner) % 2 * chips + (place // 2 - owner // 2) % chips
+            for owner in range(ranks)
+        ]
+    ).astype(jnp.int32)
+    depth = lax.axis_size("dp")
+    line = ((lax.axis_index("dp") - jnp.arange(depth)) % depth).astype(jnp.int32)
     own_gain = norm_gain[0]
     inner = gate_gain.shape[1]
     heads = decay_log.shape[1]
+    dt_blocks = jnp.stack(dt_blocks)
+    full_dt = jnp.concatenate([dt_blocks[places[owner]] for owner in range(ranks)], axis=0)
     full_dt = jnp.pad(full_dt, ((0, 0), (0, LANES - heads)))
     small = kernel_params(
         (conv_weight[0], conv_bias[0], dt_bias[0], decay_log[0], skip_gain[0], gate_gain[0]), inner
@@ -461,7 +759,7 @@
     length = inputs.shape[1]
     row_count = per_micro * length
     model_width = inputs.shape[2]
-    proj_cols = full_in.shape[1]
+    proj_cols = in_weight.shape[2]
     in_rows = in_weight.shape[1]
     out_rows = out_weight.shape[1]
     positions = jnp.arange(length, dtype=jnp.int32)
@@ -473,30 +771,25 @@
         )
 
     def relayed(rows, distance):
-        return passed_along(rows.astype(jnp.bfloat16), "section", distance).astype(jnp.float32)
-
-    def either(a, b):
-        return jax.tree.map(lambda x, y: jnp.where(first_section, x, y), a, b)
+        return passed_along(rows, "section", distance).astype(jnp.float32)
 
     layer_inputs = []
     results = []
     kept_all = []
     for tick in range(MICRO + 1):
-        arrived = relayed(results[-1], 1) if tick > 0 else empty_rows
-        own_rows = micro_rows(inputs, tick) if tick < MICRO else empty_rows
-        residual = jnp.where(first_section, own_rows, arrived)
+        arrived = relayed(output_low, 1) if tick > 0 else empty_rows
+        residual = jnp.where(first_section, micro_rows(inputs, tick % MICRO), arrived)
         normed = front_norm(residual, own_gain).astype(jnp.bfloat16)
-        projected = jnp.dot(normed, full_in, preferred_element_type=jnp.float32)
+        projected = forward_product(normed, in_pieces, in_rows, order, 1280)
         dt_raw = jnp.dot(normed, full_dt, preferred_element_type=jnp.float32)
-        mixed, local = mixer_forward(projected, dt_raw, small, length)
-        output = residual + jnp.dot(mixed, full_out, preferred_element_type=jnp.float32)
+        mixed, mixed_t, local = mixer_forward(projected, dt_raw, small, length)
+        output, output_low = forward_product(mixed, out_pieces, out_rows, order, 512, residual)
         layer_inputs.append(residual)
         results.append(output)
-        kept_all.append((normed, mixed, projected, dt_raw, local))
+        kept_all.append((normed.T, mixed_t, projected, dt_raw, local))
 
     columns = [
-        jnp.concatenate([either(kept_all[m][j], kept_all[m + 1][j]) for m in range(MICRO)], axis=0).T
-        for j in range(2)
+        jnp.concatenate([kept_all[tick][j] for tick in (MICRO, 1)], axis=1) for j in range(2)
     ]
 
     def columns_of(owner):
@@ -511,70 +804,60 @@
     lefts = spread_blocks(columns_of, "fsdp")
 
     grads_back = []
+    small_all = []
     rounded_all = []
     terms_all = []
-    small_all = []
     for tick in range(MICRO + 1):
-        returned = relayed(grads_back[-1], -1) if tick > 0 else empty_rows
-        if tick < MICRO:
-            own_lengths = lengths[tick * per_micro : (tick + 1) * per_micro]
-            live_rows = (positions[None, :] < own_lengths[:, None]).astype(jnp.float32)
-            top_grad = micro_rows(cotangent, tick) * live_rows.reshape(row_count, 1)
+        if tick > 0:
+            returned = relayed(grads_back[-1].astype(jnp.bfloat16), -1)
         else:
-            top_grad = empty_rows
-        later_tick = min(tick + 1, MICRO)
-        earlier = max(tick - 1, 0)
+            returned = empty_rows
+        micro = tick % MICRO
+        own_lengths = lengths[micro * per_micro : (micro + 1) * per_micro]
+        live_rows = (positions[None, :] < own_lengths[:, None]).astype(jnp.float32)
+        top_grad = micro_rows(cotangent, micro) * live_rows.reshape(row_count, 1)
         grad_output = jnp.where(first_section, returned, top_grad)
-        if tick == 0 or tick == MICRO:
-            source = later_tick if tick == 0 else earlier
-            residual, kept = layer_inputs[source], kept_all[source][2:]
-        else:
-            residual, kept = either(
-                (layer_inputs[earlier], kept_all[earlier][2:]),
-                (layer_inputs[later_tick], kept_all[later_tick][2:]),
-            )
-        projected, dt_raw, local = kept
+        source = MICRO if tick == 1 else 1
+        residual = layer_inputs[source]
+        projected, dt_raw, local = kept_all[source][2:]
         grad_rounded = grad_output.astype(jnp.bfloat16)
-        grad_mixed = contract_cols(grad_rounded, full_out)
-        grad_cat, *small_terms = mixer_backward(
-            projected, dt_raw, local, grad_mixed, small, length
-        )
-        grad_normed = contract_cols(grad_cat[:, :proj_cols], full_in) + contract_cols(
-            grad_cat[:, proj_cols:], full_dt
-        )
+        grad_mixed = backward_product(grad_rounded, out_pieces, out_rows, order, places, 512)
+        grad_cat, *small_terms = mixer_backward(projected, dt_raw, local, grad_mixed, small, length)
+        grad_normed = backward_product(grad_cat, in_pieces, in_rows, order, places, 1280)
+        grad_normed = grad_normed + contract_cols(grad_cat[:, proj_cols:], full_dt)
         _, pull_front = jax.vjp(front_norm, residual, own_gain)
         grad_residual, grad_gain = pull_front(grad_normed)
         grads_back.append(grad_output + grad_residual)
-        rounded_all.append(grad_rounded)
-        terms_all.append(grad_cat)
-        small_all.append([grad_gain] + small_terms)
-
-    gathered_rounded = []
-    gathered_terms = []
-    for m in range(MICRO):
-        gathered_rounded.append(
-            gathered_blocks(either(rounded_all[m + 1], rounded_all[m]), "fsdp")
-        )
-        gathered_terms.append(gathered_blocks(either(terms_all[m + 1], terms_all[m]), "fsdp"))
+        if tick > 0:
+            small_all.append([grad_gain] + small_terms)
+            rounded_all.append(gathered_blocks(grad_rounded, "fsdp"))
+            terms_all.append(gathered_blocks(grad_cat, "fsdp"))
 
     def by_source(gathered):
-        return [gathered[m][j] for j in range(len(lefts)) for m in range(MICRO)]
-
-    part_out = summed_product(
-        lefts, by_source(gathered_rounded), in_rows, out_rows, 768, "out_grad"
-    )
-    total_out = lax.psum_scatter(part_out, "dp", scatter_dimension=0, tiled=True)
-    part_in = summed_product(lefts, by_source(gathered_terms), 0, in_rows, 2304, "in_grad")
-    total_in = lax.psum_scatter(part_in, "dp", scatter_dimension=0, tiled=True)
-    owned_out = lax.all_gather(total_out, "dp", axis=0, tiled=True).astype(jnp.float32)
-    owned_in = lax.all_gather(total_in, "dp", axis=0, tiled=True).astype(jnp.float32)
+        return [blocks[j] for j in range(len(lefts)) for blocks in gathered]
+
+    def scattered(part):
+        return lax.psum_scatter(part, "dp", scatter_dimension=0, tiled=True)
+
+    part_out = summed_product(lefts, by_source(rounded_all), in_rows, out_rows, 768)
+    chunks = 2 if in_rows % (16 * depth) == 0 else 1
+    count = in_rows // chunks
+    rights = by_source(terms_all)
+    parts = [summed_product(lefts, rights, chunk * count, count, 2304) for chunk in range(chunks)]
+    moved = line_pipeline(scattered(part_out), parts, "dp")
+    owned_out = expanded(moved[0], line, 0, 1, model_width, None)[0]
+    owned = None
+    for chunk in range(chunks):
+        owned = expanded(moved[chunk + 1], line, chunk, chunks, proj_cols, owned)
+    owned_in, owned_dt = owned
+    owned_dt = owned_dt[:, :heads]
 
     gain, taps, bias, gate, skip, head = [sum(terms) for terms in zip(*small_all)]
     skip = skip.reshape(heads, HEAD_DIM).sum(axis=1)
     pieces = [
         gain, taps.reshape(-1), bias[0], head[0, :heads], head[1, :heads], skip, gate[0]
     ]
-    flat = lax.psum(jnp.concatenate(pieces), ("dp", "fsdp"))
+    flat = butterfly_sum(butterfly_sum(jnp.concatenate(pieces), "fsdp"), "dp")
     totals = []
     start = 0
     for piece in pieces:
@@ -583,19 +866,19 @@
 
     layer_out = jnp.concatenate(
         [
-            jnp.where(first_section, results[m], results[m + 1]).reshape(
+            jnp.where(first_section, results[a], results[b]).reshape(
                 per_micro, length, model_width
             )
-            for m in range(MICRO)
+            for a, b in ((MICRO, 1), (1, MICRO))
         ],
         axis=0,
     )
     input_grad = jnp.concatenate(
         [
-            jnp.where(first_section, grads_back[m + 1], grads_back[m]).reshape(
+            jnp.where(first_section, grads_back[a], grads_back[b]).reshape(
                 per_micro, length, model_width
             )
-            for m in range(MICRO)
+            for a, b in ((1, MICRO), (MICRO, 1))
         ],
         axis=0,
     )
@@ -603,8 +886,8 @@
         layer_out[None],
         input_grad[None],
         totals[0][None],
-        owned_in[:, :proj_cols][None],
-        owned_in[:, proj_cols : proj_cols + heads][None],
+        owned_in[None],
+        owned_dt[None],
         totals[1].reshape(conv_weight.shape),
         totals[2][None],
         totals[3][None],

time: 873 us -> 699 us (0.80)
  waiting for transfers between devices: 551 us -> 260 us
  Pallas kernels: 89.5 us -> 212 us
  matrix products: 98.2 us -> 4.83 us
  starting transfers between devices: 19.6 us -> 84.5 us
  local copies, waits for them, and re-layouts: 48 us -> 66.5 us
    all_gather x4 -> x2, waiting for transfers between devices: 301 us -> 0.01 us  [gathered_weights(): same.append(lax.all_gather(arrived[i][hop - 1], 'dp', axis=0, tiled=True))]
    pallas_call x0 -> x15, Pallas kernels: none -> 103 us  [the longest x6 49.1 us: backward_product(): pl.pallas_call(functools.partial(backward_product_kernel, rows, len(piece...]
    ppermute x0 -> x30, waiting for transfers between devices: none -> 86 us  [the longest x11 45 us: line_pipeline(): down = lax.ppermute(job[3], axis, downs)]
    psum x1 -> x0, waiting for transfers between devices: 81.1 us -> none  [per_device(): flat = lax.psum(jnp.concatenate(pieces), ('dp', 'fsdp'))]
    ppermute x15 -> x28, waiting for transfers between devices: 89.1 us -> 162 us  [routed(): lax.ppermute(block, axis, [(i, target(i, hop, flip, size)) for i in range...]
    reduce_scatter x2 -> x1, waiting for transfers between devices: 72 us -> 0.01 us  [scattered(): return lax.psum_scatter(part, 'dp', scatter_dimension=0, tiled=True)]
    ppermute x0 -> x30, starting transfers between devices: none -> 58.6 us  [the longest x11 30.9 us: line_pipeline(): up = lax.ppermute(job[2], axis, ups)]
    dot_general x9 -> x3, matrix products: 53 us -> 4.1 us  [contract_cols(): lax.dot_general(left, right, (((1,), (1,)), ((), ())), preferred_element_...]
  transfers between devices with their start and end apart: 26 -> 65, of which waited for: 13 -> 30; matrix products, arithmetic and copies ran while one was open for 15% -> 7% of each run, Pallas kernels for 7% -> 16%
where the time goes in v2:
time: 699 us; the launch traced here: 689 us
  waiting for transfers between devices  260 us (37%)
  Pallas kernels  212 us (30%)
  starting transfers between devices  84.5 us (12%)
  local copies, waits for them, and re-layouts  66.5 us (10%)
  other arithmetic  44.2 us (6%)
  between operations  16.2 us (2%)
    ppermute x28, waiting for transfers between devices, routed(): lax.ppermute(block, axis, [(i, target(i, hop, flip, size)) for i in range...  162 us
    pallas_call x3, Pallas kernels, mixer_backward(): pl.pallas_call(functools.partial(mixer_backward_kernel, inner, heads), gr...  54.3 us
    pallas_call x6, Pallas kernels, backward_product(): pl.pallas_call(functools.partial(backward_product_kernel, rows, len(piece...  49.1 us
    ppermute x11, waiting for transfers between devices, line_pipeline(): down = lax.ppermute(job[3], axis, downs)  45 us
    unnamed x320, local copies, waits for them, and re-layouts  39.9 us
    pallas_call x6, Pallas kernels, forward_product(): pl.pallas_call(functools.partial(forward_product_kernel, rows, len(pieces...  39.1 us
    ppermute x11, starting transfers between devices, line_pipeline(): up = lax.ppermute(job[2], axis, ups)  30.9 us
    pallas_call x3, Pallas kernels, mixer_forward(): pl.pallas_call(functools.partial(mixer_forward_kernel, inner, heads), gri...  30.3 us
  transfers between devices with their start and end apart: 65, of which 30 were waited for; matrix products, arithmetic and copies ran while one was open for 7% of the time, Pallas kernels for 16%

profile of v2, /device:TPU:0, one launch (start us, length us, event | category | flops | bytes accessed | tf_op | source)
XLA Modules:
  0.0 688.8 jit_solution(17998679088684436981)
XLA Ops:
  14.5 17.9 %collective-permute-done.2 = bf16[384,48]{0,1:T(8,128)(2,1)S(1)} collective-permute-done((bf16[384,48]{0,1:T(8,128)(2,1)S(1)}, bf16[384,48]{0,1:T(8,128)(2,1)S(1)}, u32[]{:S(2)}, u32[]{:S(2)}) %collective-permute-start.2) | collective-permute-done | bytes 36896 | tf_op jit(solution)/shard_map/ppermute | solution.py:587
  40.0 54.2 %collective-permute-done.5.refs_1_ = bf16[192,6400]{1,0:T(8,128)(2,1)} collective-permute-done((bf16[192,6400]{1,0:T(8,128)(2,1)}, bf16[192,6400]{1,0:T(8,128)(2,1)}, u32[]{:S(2)}, u32[]{:S(2)}) %collective-permute-start.5) | collective-permute-done | bytes 2457632 | tf_op jit(solution)/shard_map/ppermute | solution.py:587
  106.1 17.8 %collective-permute-done.9.refs_1_ = bf16[384,1536]{1,0:T(8,128)(2,1)S(1)} collective-permute-done((bf16[384,1536]{1,0:T(8,128)(2,1)}, bf16[384,1536]{1,0:T(8,128)(2,1)S(1)}, u32[]{:S(2)}, u32[]{:S(2)}) %collective-permute-start.9) | collective-permute-done | bytes 1179680 | tf_op jit(solution)/shard_map/ppermute | solution.py:587
  130.8 7.9 %shard_map.220.proj_ref = f32[128,6400]{1,0:T(8,128)S(1)} custom-call(s32[4]{0:T(128)S(1)} %pad_add_fusion.order_ref, bf16[128,1536]{1,0:T(8,128)(2,1)S(1)} %multiply_convert_fusion.2.left_ref, bf16[384,6400]{1,0:T(8,128)(2,1)S(1)} %bitcast.139, bf16[192,6400]{1,0:T(8,128)(2,1)} %collective-permute-done.5.refs_1_, bf16[192,6400]{1,0:T(8,128)(2,1)S(1)} %copy-done.2, ...), custom_call_target="tpu_custom_call" | custom-call | flops 2516582400 | bytes 22937600 | tf_op jit(solution)/shard_map/pallas_call | solution.py:458
  138.8 11.0 %mixer_forward.3 = (bf16[128,3072]{1,0:T(8,128)(2,1)S(1)}, bf16[3072,128]{1,0:T(8,128)(2,1)}, f32[128,3072]{1,0:T(8,128)}) custom-call(f32[128,6400]{1,0:T(8,128)S(1)} %shard_map.220.proj_ref, f32[128,128]{1,0:T(8,128)S(1)} %fusion.51.dt_ref, f32[4,3328]{1,0:T(4,128)S(1)} %bitcast.160, f32[1,3328]{1,0:T(1,128)S(1)} %copy-done.64, f32[1,128]{1,0:T(1,128)S(1)} %copy-done.94, ...), custom_call_target="tpu_custom_call" | custom-call | flops 235929600 | bytes 5636096 | tf_op jit(solution)/shard_map/mixer_forward/pallas_call | solution.py:304
  165.1 6.2 shard_map.226.gm_ref
  175.1 7.9 %shard_map.222.proj_ref = f32[128,6400]{1,0:T(8,128)S(1)} custom-call(s32[4]{0:T(128)S(1)} %pad_add_fusion.order_ref, bf16[128,1536]{1,0:T(8,128)(2,1)S(1)} %multiply_convert_fusion.1.left_ref, bf16[384,6400]{1,0:T(8,128)(2,1)S(1)} %bitcast.142, bf16[192,6400]{1,0:T(8,128)(2,1)} %collective-permute-done.5.refs_1_, bf16[192,6400]{1,0:T(8,128)(2,1)S(1)} %copy-done.3, ...), custom_call_target="tpu_custom_call" | custom-call | flops 2516582400 | bytes 22937600 | tf_op jit(solution)/shard_map/pallas_call | solution.py:458
  183.1 9.7 %mixer_forward.4 = (bf16[128,3072]{1,0:T(8,128)(2,1)S(1)}, bf16[3072,128]{1,0:T(8,128)(2,1)S(1)}, f32[128,3072]{1,0:T(8,128)S(1)}) custom-call(f32[128,6400]{1,0:T(8,128)S(1)} %shard_map.222.proj_ref, f32[128,128]{1,0:T(8,128)S(1)} %fusion.49.dt_ref, f32[4,3328]{1,0:T(4,128)S(1)} %bitcast.161, f32[1,3328]{1,0:T(1,128)S(1)} %copy-done.65, ...), custom_call_target="tpu_custom_call" | custom-call | flops 235929600 | bytes 5636096 | tf_op jit(solution)/shard_map/mixer_forward/pallas_call | solution.py:304
  198.5 17.5 %mixer_backward.3 = (bf16[128,6528]{1,0:T(8,128)(2,1)S(1)}, f32[4,3328]{1,0:T(4,128)}, f32[1,3328]{1,0:T(1,128)}, f32[1,3072]{1,0:T(1,128)}, f32[1,3072]{1,0:T(1,128)}, /*index=5*/f32[8,128]{1,0:T(8,128)}) custom-call(f32[128,6400]{1,0:T(8,128)} %copy-done.22, f32[128,128]{1,0:T(8,128)S(1)} %fusion.49.dt_ref, f32[128,3072]{1,0:T(8,128)S(1)} %copy-done.31, ...), custom_call_target="tpu_custom_call" | custom-call | flops 589824000 | bytes 8060928 | tf_op jit(solution)/shard_map/mixer_backward/pallas_call | solution.py:334
  218.6 10.3 %shard_map.227 = f32[128,1536]{1,0:T(8,128)S(1)} custom-call(s32[4]{0:T(128)S(1)} %pad_add_fusion.order_ref, bf16[128,6528]{1,0:T(8,128)(2,1)S(1)} %copy-done.47, bf16[384,6400]{1,0:T(8,128)(2,1)S(1)} %bitcast.143, bf16[192,6400]{1,0:T(8,128)(2,1)} %collective-permute-done.5.refs_1_, bf16[192,6400]{1,0:T(8,128)(2,1)S(1)} %copy-done.3, ...), custom_call_target="tpu_custom_call" | custom-call | flops 2516582400 | bytes 20447232 | tf_op jit(solution)/shard_map/pallas_call | solution.py:514
  237.1 8.4 %collective-permute-done.14 = bf16[128,1536]{1,0:T(8,128)(2,1)S(1)} collective-permute-done((bf16[128,1536]{1,0:T(8,128)(2,1)S(1)}, bf16[128,1536]{1,0:T(8,128)(2,1)S(1)}, u32[]{:S(2)}, u32[]{:S(2)}) %collective-permute-start.14) | collective-permute-done | bytes 393248 | tf_op jit(solution)/shard_map/ppermute | solution.py:24
  248.7 7.9 %shard_map.224.proj_ref = f32[128,6400]{1,0:T(8,128)S(1)} custom-call(s32[4]{0:T(128)S(1)} %pad_add_fusion.order_ref, bf16[128,1536]{1,0:T(8,128)(2,1)S(1)} %get-tuple-element.202.left_ref, bf16[384,6400]{1,0:T(8,128)(2,1)S(1)} %bitcast.144, bf16[192,6400]{1,0:T(8,128)(2,1)} %collective-permute-done.5.refs_1_, bf16[192,6400]{1,0:T(8,128)(2,1)S(1)} %copy-done.3, ...), custom_call_target="tpu_custom_call" | custom-call | flops 2516582400 | bytes 22937600 | tf_op jit(solution)/shard_map/pallas_call | solution.py:458
  256.7 9.7 %mixer_forward.5 = (bf16[128,3072]{1,0:T(8,128)(2,1)S(1)}, bf16[3072,128]{1,0:T(8,128)(2,1)S(1)}, f32[128,3072]{1,0:T(8,128)S(1)}) custom-call(f32[128,6400]{1,0:T(8,128)S(1)} %shard_map.224.proj_ref, f32[128,128]{1,0:T(8,128)S(1)} %fusion.47.dt_ref, f32[4,3328]{1,0:T(4,128)S(1)} %bitcast.163, f32[1,3328]{1,0:T(1,128)S(1)} %copy-done.65, ...), custom_call_target="tpu_custom_call" | custom-call | flops 235929600 | bytes 5636096 | tf_op jit(solution)/shard_map/mixer_forward/pallas_call | solution.py:304
  276.4 6.1 shard_map.228.gm_ref
  286.5 18.3 %mixer_backward.4 = (bf16[128,6528]{1,0:T(8,128)(2,1)}, f32[4,3328]{1,0:T(4,128)S(1)}, f32[1,3328]{1,0:T(1,128)S(1)}, f32[1,3072]{1,0:T(1,128)S(1)}, f32[1,3072]{1,0:T(1,128)S(1)}, /*index=5*/f32[8,128]{1,0:T(8,128)S(1)}) custom-call(f32[128,6400]{1,0:T(8,128)} %copy-done.25, f32[128,128]{1,0:T(8,128)S(1)} %copy-done.73, f32[128,3072]{1,0:T(8,128)S(1)} %copy-done.49, ...), custom_call_target="tpu_custom_call" | custom-call | flops 589824000 | bytes 8060928 | tf_op jit(solution)/shard_map/mixer_backward/pallas_call | solution.py:334
  307.9 10.3 %shard_map.229 = f32[128,1536]{1,0:T(8,128)S(1)} custom-call(s32[4]{0:T(128)S(1)} %pad_add_fusion.order_ref, bf16[128,6528]{1,0:T(8,128)(2,1)} %get-tuple-element.96.left_ref.refs_4_, bf16[384,6400]{1,0:T(8,128)(2,1)S(1)} %bitcast.147, bf16[192,6400]{1,0:T(8,128)(2,1)} %collective-permute-done.5.refs_1_, bf16[192,6400]{1,0:T(8,128)(2,1)S(1)} %copy-done.4, ...), custom_call_target="tpu_custom_call" | custom-call | flops 2516582400 | bytes 20447232 | tf_op jit(solution)/shard_map/pallas_call | solution.py:514
  342.2 7.9 %collective-permute-done.32.refs_6_ = bf16[128,1536]{1,0:T(8,128)(2,1)} collective-permute-done((bf16[128,1536]{1,0:T(8,128)(2,1)}, bf16[128,1536]{1,0:T(8,128)(2,1)}, u32[]{:S(2)}, u32[]{:S(2)}) %collective-permute-start.32) | collective-permute-done | bytes 393248 | tf_op jit(solution)/shard_map/ppermute | solution.py:587
  350.1 8.4 %collective-permute-done.33.refs_7_ = bf16[128,1536]{1,0:T(8,128)(2,1)} collective-permute-done((bf16[128,1536]{1,0:T(8,128)(2,1)}, bf16[128,1536]{1,0:T(8,128)(2,1)}, u32[]{:S(2)}, u32[]{:S(2)}) %collective-permute-start.33) | collective-permute-done | bytes 393248 | tf_op jit(solution)/shard_map/ppermute | solution.py:587
  361.4 7.1 %collective-permute-done.23.refs_3_ = bf16[1152,256]{1,0:T(8,128)(2,1)} collective-permute-done((bf16[1152,256]{1,0:T(8,128)(2,1)}, bf16[1152,256]{1,0:T(8,128)(2,1)}, u32[]{:S(2)}, u32[]{:S(2)}) %collective-permute-start.23) | collective-permute-done | bytes 589856 | tf_op jit(solution)/shard_map/ppermute | solution.py:587
  368.5 6.1 shard_map.234
  378.9 6.1 shard_map.230.gm_ref
  385.0 18.5 %mixer_backward.5 = (bf16[128,6528]{1,0:T(8,128)(2,1)}, f32[4,3328]{1,0:T(4,128)S(1)}, f32[1,3328]{1,0:T(1,128)S(1)}, f32[1,3072]{1,0:T(1,128)S(1)}, f32[1,3072]{1,0:T(1,128)S(1)}, /*index=5*/f32[8,128]{1,0:T(8,128)S(1)}) custom-call(f32[128,6400]{1,0:T(8,128)} %copy-done.22, f32[128,128]{1,0:T(8,128)S(1)} %copy-done.63, f32[128,3072]{1,0:T(8,128)S(1)} %copy-done.32, ...), custom_call_target="tpu_custom_call" | custom-call | flops 589824000 | bytes 8060928 | tf_op jit(solution)/shard_map/mixer_backward/pallas_call | solution.py:334
  408.4 6.9 %collective-permute-done.24.refs_6_ = bf16[128,6528]{1,0:T(8,128)(2,1)} collective-permute-done((bf16[128,6528]{1,0:T(8,128)(2,1)}, bf16[128,6528]{1,0:T(8,128)(2,1)}, u32[]{:S(2)}, u32[]{:S(2)}) %collective-permute-start.24) | collective-permute-done | bytes 1671200 | tf_op jit(solution)/shard_map/ppermute | solution.py:587
  415.3 35.6 %collective-permute-done.25.refs_7_ = bf16[128,6528]{1,0:T(8,128)(2,1)} collective-permute-done((bf16[128,6528]{1,0:T(8,128)(2,1)}, bf16[128,6528]{1,0:T(8,128)(2,1)}, u32[]{:S(2)}, u32[]{:S(2)}) %collective-permute-start.25) | collective-permute-done | bytes 1671200 | tf_op jit(solution)/shard_map/ppermute | solution.py:587
  455.8 9.4 %shard_map.233 = bf16[192,6528]{1,0:T(8,128)(2,1)} custom-call(bf16[1152,256]{1,0:T(8,128)(2,1)S(1)} %copy-done.38, bf16[1152,256]{1,0:T(8,128)(2,1)} %collective-permute-done.21.refs_1_, bf16[1152,256]{1,0:T(8,128)(2,1)} %collective-permute-done.22.refs_2_, bf16[1152,256]{1,0:T(8,128)(2,1)} %collective-permute-done.23.refs_3_, ...), custom_call_target="tpu_custom_call" | custom-call | flops 2566914048 | bytes 15876096 | tf_op jit(solution)/shard_map/pallas_call | solution.py:390
  495.3 11.0 %collective-permute-done.41.refs_3_ = bf16[192,1536]{1,0:T(8,128)(2,1)} collective-permute-done((bf16[192,1536]{1,0:T(8,128)(2,1)}, bf16[192,1536]{1,0:T(8,128)(2,1)}, u32[]{:S(2)}, u32[]{:S(2)}) %collective-permute-start.41) | collective-permute-done | bytes 589856 | tf_op jit(solution)/shard_map/ppermute | solution.py:656
  518.0 12.6 %collective-permute-done.45.refs_1_ = bf16[192,1536]{1,0:T(8,128)(2,1)} collective-permute-done((bf16[192,1536]{1,0:T(8,128)(2,1)}, bf16[192,1536]{1,0:T(8,128)(2,1)}, u32[]{:S(2)}, u32[]{:S(2)}) %collective-permute-start.45) | collective-permute-done | bytes 589856 | tf_op jit(solution)/shard_map/ppermute | solution.py:656
  537.2 7.4 %collective-permute-done.46 = bf16[48,6528]{1,0:T(8,128)(2,1)} collective-permute-done((bf16[48,6528]{1,0:T(8,128)(2,1)}, bf16[48,6528]{1,0:T(8,128)(2,1)}, u32[]{:S(2)}, u32[]{:S(2)}) %collective-permute-start.46) | collective-permute-done | bytes 626720 | tf_op jit(solution)/shard_map/ppermute | solution.py:655
  556.8 9.4 %shard_map.232 = bf16[192,6528]{1,0:T(8,128)(2,1)} custom-call(bf16[1152,256]{1,0:T(8,128)(2,1)S(1)} %copy-done.39, bf16[1152,256]{1,0:T(8,128)(2,1)} %collective-permute-done.21.refs_1_, bf16[1152,256]{1,0:T(8,128)(2,1)} %collective-permute-done.22.refs_2_, bf16[1152,256]{1,0:T(8,128)(2,1)} %collective-permute-done.23.refs_3_, ...), custom_call_target="tpu_custom_call" | custom-call | flops 2566914048 | bytes 15876096 | tf_op jit(solution)/shard_map/pallas_call | solution.py:390
  575.9 5.8 collective-permute-done.50.refs_2_
  610.2 10.2 %shard_map.231 = f32[128,1536]{1,0:T(8,128)S(1)} custom-call(s32[4]{0:T(128)S(1)} %pad_add_fusion.order_ref, bf16[128,6528]{1,0:T(8,128)(2,1)} %get-tuple-element.97.left_ref.refs_5_, bf16[384,6400]{1,0:T(8,128)(2,1)S(1)} %bitcast.150, bf16[192,6400]{1,0:T(8,128)(2,1)} %collective-permute-done.5.refs_1_, bf16[192,6400]{1,0:T(8,128)(2,1)S(1)} %copy-done.5, ...), custom_call_target="tpu_custom_call" | custom-call | flops 2516582400 | bytes 20447232 | tf_op jit(solution)/shard_map/pallas_call | solution.py:514
  647.9 6.8 collective-permute-done.59.refs_3_
  (534 shorter events, 282.4 us)
Async XLA Ops:
  7.2 87.1 %all-gather.3.cloned.1.call-start = ((), (), s32[]{:S(2)}) async-start(), calls=%async_computation.1 | async-start | bytes 3072000 | tf_op jit(solution)/shard_map/all_gather | solution.py:695
  8.4 25.3 %collective-permute-start = (bf16[48,6400]{1,0:T(8,128)(2,1)S(1)}, bf16[48,6400]{1,0:T(8,128)(2,1)S(1)}, u32[]{:S(2)}, u32[]{:S(2)}) collective-permute-start(bf16[48,6400]{1,0:T(8,128)(2,1)S(1)} %dynamic-slice_bitcast_fusion.2), channel_id=1, source_target_pairs={{0,2},{1,3},{2,0},{3,1},{4,6},{5,7},{6,4},{7,5},{8,10},{9,11},{10,... | collective-permute-start | bytes 1843208 | tf_op jit(solution)/shard_map/ppermute | solution.py:587
  12.4 21.2 %collective-permute-start.1 = (bf16[96,1536]{1,0:T(8,128)(2,1)S(1)}, bf16[96,1536]{1,0:T(8,128)(2,1)S(1)}, u32[]{:S(2)}, u32[]{:S(2)}) collective-permute-start(bf16[96,1536]{1,0:T(8,128)(2,1)S(1)} %dynamic-slice_bitcast_fusion.3), channel_id=1, source_target_pairs={{0,2},{1,3},{2,0},{3,1},{4,6},{5,7},{6,4},{7,5},{8,10},{9,11},{10,... | collective-permute-start | bytes 884744 | tf_op jit(solution)/shard_map/ppermute | solution.py:587
  12.5 19.9 %collective-permute-start.2 = (bf16[384,48]{0,1:T(8,128)(2,1)S(1)}, bf16[384,48]{0,1:T(8,128)(2,1)S(1)}, u32[]{:S(2)}, u32[]{:S(2)}) collective-permute-start(bf16[384,48]{0,1:T(8,128)(2,1)S(1)} %bitcast.177), channel_id=1, source_target_pairs={{0,2},{1,3},{2,0},{3,1},{4,6},{5,7},{6,4},{7,5},{8,10},{9,11},{10,... | collective-permute-start | bytes 110600 | tf_op jit(solution)/shard_map/ppermute | solution.py:587
  14.5 17.9 %collective-permute-start.3 = (bf16[384,48]{0,1:T(8,128)(2,1)S(1)}, bf16[384,48]{0,1:T(8,128)(2,1)S(1)}, u32[]{:S(2)}, u32[]{:S(2)}) collective-permute-start(bf16[384,48]{0,1:T(8,128)(2,1)S(1)} %bitcast.178), channel_id=1, source_target_pairs={{0,1},{1,0},{2,3},{3,2},{4,5},{5,4},{6,7},{7,6},{8,9},{9,8},{10,11... | collective-permute-start | bytes 110600 | tf_op jit(solution)/shard_map/ppermute | solution.py:587
  34.5 89.4 %all-gather.5.cloned.1.call-start = ((), (), s32[]{:S(2)}) async-start(), calls=%async_computation.2 | async-start | bytes 1474560 | tf_op jit(solution)/shard_map/all_gather | solution.py:695
  34.6 89.4 %collective-permute-start.6 = (bf16[384,6400]{1,0:T(8,128)(2,1)}, bf16[384,6400]{1,0:T(8,128)(2,1)}, u32[]{:S(2)}, u32[]{:S(2)}) collective-permute-start(bf16[384,6400]{1,0:T(8,128)(2,1)} %bitcast.137), channel_id=1, source_target_pairs={{0,1},{1,0},{2,3},{3,2},{4,5},{5,4},{6,7},{7,6},{8,9},{9,8},{10,11... | collective-permute-start | bytes 14745608 | tf_op jit(solution)/shard_map/ppermute | solution.py:587
  38.2 56.0 %collective-permute-start.5 = (bf16[192,6400]{1,0:T(8,128)(2,1)}, bf16[192,6400]{1,0:T(8,128)(2,1)}, u32[]{:S(2)}, u32[]{:S(2)}) collective-permute-start(bf16[192,6400]{1,0:T(8,128)(2,1)} %slice.68), channel_id=1, source_target_pairs={{0,2},{1,3},{2,0},{3,1},{4,6},{5,7},{6,4},{7,5},{8,10},{9,11},{10,... | collective-permute-start | bytes 7372808 | tf_op jit(solution)/shard_map/ppermute | solution.py:587
  40.0 425.2 %reduce-scatter.2.cloned.1.call-start = ((), (), s32[]{:S(2)}) async-start(), calls=%async_computation.3 | async-start | bytes 2949120 | tf_op jit(solution)/shard_map/reduce_scatter | solution.py:840
  94.2 33.1 %collective-permute-start.7 = (bf16[192,6400]{1,0:T(8,128)(2,1)}, bf16[192,6400]{1,0:T(8,128)(2,1)}, u32[]{:S(2)}, u32[]{:S(2)}) collective-permute-start(bf16[192,6400]{1,0:T(8,128)(2,1)} %collective-permute-done.5.refs_1_), channel_id=1, source_target_pairs={{0,1},{1,0},{2,3},{3,2},{4,5},{5,4},{6,7},{7,6},{8,9},{9,8},{10,11... | collective-permute-start | bytes 7372808 | tf_op jit(solution)/shard_map/ppermute | solution.py:587
  94.2 33.0 %collective-permute-start.8 = (bf16[192,6400]{1,0:T(8,128)(2,1)}, bf16[192,6400]{1,0:T(8,128)(2,1)}, u32[]{:S(2)}, u32[]{:S(2)}) collective-permute-start(bf16[192,6400]{1,0:T(8,128)(2,1)} %all-gather.3.cloned.1.call-done.refs_2_), channel_id=1, source_target_pairs={{0,1},{1,0},{2,3},{3,2},{4,5},{5,4},{6,7},{7,6},{8,9},{9,8},{10,11... | collective-permute-start | bytes 7372808 | tf_op jit(solution)/shard_map/ppermute | solution.py:587
  95.8 28.1 %collective-permute-start.9 = (bf16[384,1536]{1,0:T(8,128)(2,1)}, bf16[384,1536]{1,0:T(8,128)(2,1)S(1)}, u32[]{:S(2)}, u32[]{:S(2)}) collective-permute-start(bf16[384,1536]{1,0:T(8,128)(2,1)} %slice.69), channel_id=1, source_target_pairs={{0,2},{1,3},{2,0},{3,1},{4,6},{5,7},{6,4},{7,5},{8,10},{9,11},{10,... | collective-permute-start | bytes 3538952 | tf_op jit(solution)/shard_map/ppermute | solution.py:587
  97.6 52.2 %collective-permute-start.10 = (bf16[768,1536]{1,0:T(8,128)(2,1)S(1)}, bf16[768,1536]{1,0:T(8,128)(2,1)}, u32[]{:S(2)}, u32[]{:S(2)}) collective-permute-start(bf16[768,1536]{1,0:T(8,128)(2,1)S(1)} %bitcast.152), channel_id=1, source_target_pairs={{0,1},{1,0},{2,3},{3,2},{4,5},{5,4},{6,7},{7,6},{8,9},{9,8},{10,11... | collective-permute-start | bytes 7077896 | tf_op jit(solution)/shard_map/ppermute | solution.py:587
  123.9 25.8 %collective-permute-start.11 = (bf16[384,1536]{1,0:T(8,128)(2,1)S(1)}, bf16[384,1536]{1,0:T(8,128)(2,1)}, u32[]{:S(2)}, u32[]{:S(2)}) collective-permute-start(bf16[384,1536]{1,0:T(8,128)(2,1)S(1)} %collective-permute-done.9.refs_1_), channel_id=1, source_target_pairs={{0,1},{1,0},{2,3},{3,2},{4,5},{5,4},{6,7},{7,6},{8,9},{9,8},{10,11... | collective-permute-start | bytes 3538952 | tf_op jit(solution)/shard_map/ppermute | solution.py:587
  123.9 25.8 %collective-permute-start.12 = (bf16[384,1536]{1,0:T(8,128)(2,1)}, bf16[384,1536]{1,0:T(8,128)(2,1)S(1)}, u32[]{:S(2)}, u32[]{:S(2)}) collective-permute-start(bf16[384,1536]{1,0:T(8,128)(2,1)} %all-gather.5.cloned.1.call-done.refs_2_), channel_id=1, source_target_pairs={{0,1},{1,0},{2,3},{3,2},{4,5},{5,4},{6,7},{7,6},{8,9},{9,8},{10,11... | collective-permute-start | bytes 3538952 | tf_op jit(solution)/shard_map/ppermute | solution.py:587
  247.2 26.9 %collective-permute-start.15 = (bf16[128,1536]{1,0:T(8,128)(2,1)}, bf16[128,1536]{1,0:T(8,128)(2,1)}, u32[]{:S(2)}, u32[]{:S(2)}) collective-permute-start(bf16[128,1536]{1,0:T(8,128)(2,1)} %get-tuple-element.201), channel_id=1, source_target_pairs={{16,0},{17,1},{18,2},{19,3},{20,4},{21,5},{22,6},{23,7},{24,8},{25... | collective-permute-start | bytes 1179656 | tf_op jit(solution)/shard_map/ppermute | solution.py:24
  332.1 18.0 %collective-permute-start.32 = (bf16[128,1536]{1,0:T(8,128)(2,1)}, bf16[128,1536]{1,0:T(8,128)(2,1)}, u32[]{:S(2)}, u32[]{:S(2)}) collective-permute-start(bf16[128,1536]{1,0:T(8,128)(2,1)} %fusion.24.left_ref.refs_4_), channel_id=1, source_target_pairs={{0,2},{1,3},{2,0},{3,1},{4,6},{5,7},{6,4},{7,5},{8,10},{9,11},{10,... | collective-permute-start | bytes 1179656 | tf_op jit(solution)/shard_map/ppermute | solution.py:587
  338.1 20.5 %collective-permute-start.33 = (bf16[128,1536]{1,0:T(8,128)(2,1)}, bf16[128,1536]{1,0:T(8,128)(2,1)}, u32[]{:S(2)}, u32[]{:S(2)}) collective-permute-start(bf16[128,1536]{1,0:T(8,128)(2,1)} %fusion.23.left_ref.refs_5_), channel_id=1, source_target_pairs={{0,2},{1,3},{2,0},{3,1},{4,6},{5,7},{6,4},{7,5},{8,10},{9,11},{10,... | collective-permute-start | bytes 1179656 | tf_op jit(solution)/shard_map/ppermute | solution.py:587
  340.5 28.0 %collective-permute-start.23 = (bf16[1152,256]{1,0:T(8,128)(2,1)}, bf16[1152,256]{1,0:T(8,128)(2,1)}, u32[]{:S(2)}, u32[]{:S(2)}) collective-permute-start(bf16[1152,256]{1,0:T(8,128)(2,1)} %pad_maximum_fusion.3), channel_id=1, source_target_pairs={{0,3},{1,2},{2,1},{3,0},{4,7},{5,6},{6,5},{7,4},{8,11},{9,10},{10,... | collective-permute-start | bytes 1769480 | tf_op jit(solution)/shard_map/ppermute | solution.py:587
  341.7 26.8 %collective-permute-start.34 = (bf16[128,1536]{1,0:T(8,128)(2,1)}, bf16[128,1536]{1,0:T(8,128)(2,1)}, u32[]{:S(2)}, u32[]{:S(2)}) collective-permute-start(bf16[128,1536]{1,0:T(8,128)(2,1)} %fusion.24.left_ref.refs_4_), channel_id=1, source_target_pairs={{0,1},{1,0},{2,3},{3,2},{4,5},{5,4},{6,7},{7,6},{8,9},{9,8},{10,11... | collective-permute-start | bytes 1179656 | tf_op jit(solution)/shard_map/ppermute | solution.py:587
  341.7 26.8 %collective-permute-start.35 = (bf16[128,1536]{1,0:T(8,128)(2,1)}, bf16[128,1536]{1,0:T(8,128)(2,1)}, u32[]{:S(2)}, u32[]{:S(2)}) collective-permute-start(bf16[128,1536]{1,0:T(8,128)(2,1)} %fusion.23.left_ref.refs_5_), channel_id=1, source_target_pairs={{0,1},{1,0},{2,3},{3,2},{4,5},{5,4},{6,7},{7,6},{8,9},{9,8},{10,11... | collective-permute-start | bytes 1179656 | tf_op jit(solution)/shard_map/ppermute | solution.py:587
  350.1 18.4 %collective-permute-start.36 = (bf16[128,1536]{1,0:T(8,128)(2,1)}, bf16[128,1536]{1,0:T(8,128)(2,1)}, u32[]{:S(2)}, u32[]{:S(2)}) collective-permute-start(bf16[128,1536]{1,0:T(8,128)(2,1)} %collective-permute-done.32.refs_6_), channel_id=1, source_target_pairs={{0,1},{1,0},{2,3},{3,2},{4,5},{5,4},{6,7},{7,6},{8,9},{9,8},{10,11... | collective-permute-start | bytes 1179656 | tf_op jit(solution)/shard_map/ppermute | solution.py:587
  375.5 39.8 %collective-permute-start.24 = (bf16[128,6528]{1,0:T(8,128)(2,1)}, bf16[128,6528]{1,0:T(8,128)(2,1)}, u32[]{:S(2)}, u32[]{:S(2)}) collective-permute-start(bf16[128,6528]{1,0:T(8,128)(2,1)} %get-tuple-element.96.left_ref.refs_4_), channel_id=1, source_target_pairs={{0,2},{1,3},{2,0},{3,1},{4,6},{5,7},{6,4},{7,5},{8,10},{9,11},{10,... | collective-permute-start | bytes 5013512 | tf_op jit(solution)/shard_map/ppermute | solution.py:587
  406.5 44.4 %collective-permute-start.25 = (bf16[128,6528]{1,0:T(8,128)(2,1)}, bf16[128,6528]{1,0:T(8,128)(2,1)}, u32[]{:S(2)}, u32[]{:S(2)}) collective-permute-start(bf16[128,6528]{1,0:T(8,128)(2,1)} %get-tuple-element.97.left_ref.refs_5_), channel_id=1, source_target_pairs={{0,2},{1,3},{2,0},{3,1},{4,6},{5,7},{6,4},{7,5},{8,10},{9,11},{10,... | collective-permute-start | bytes 5013512 | tf_op jit(solution)/shard_map/ppermute | solution.py:587
  407.8 43.0 %collective-permute-start.26 = (bf16[128,6528]{1,0:T(8,128)(2,1)}, bf16[128,6528]{1,0:T(8,128)(2,1)}, u32[]{:S(2)}, u32[]{:S(2)}) collective-permute-start(bf16[128,6528]{1,0:T(8,128)(2,1)} %get-tuple-element.96.left_ref.refs_4_), channel_id=1, source_target_pairs={{0,1},{1,0},{2,3},{3,2},{4,5},{5,4},{6,7},{7,6},{8,9},{9,8},{10,11... | collective-permute-start | bytes 5013512 | tf_op jit(solution)/shard_map/ppermute | solution.py:587
  408.1 42.8 %collective-permute-start.27 = (bf16[128,6528]{1,0:T(8,128)(2,1)}, bf16[128,6528]{1,0:T(8,128)(2,1)}, u32[]{:S(2)}, u32[]{:S(2)}) collective-permute-start(bf16[128,6528]{1,0:T(8,128)(2,1)} %get-tuple-element.97.left_ref.refs_5_), channel_id=1, source_target_pairs={{0,1},{1,0},{2,3},{3,2},{4,5},{5,4},{6,7},{7,6},{8,9},{9,8},{10,11... | collective-permute-start | bytes 5013512 | tf_op jit(solution)/shard_map/ppermute | solution.py:587
  415.3 35.6 %collective-permute-start.28 = (bf16[128,6528]{1,0:T(8,128)(2,1)}, bf16[128,6528]{1,0:T(8,128)(2,1)}, u32[]{:S(2)}, u32[]{:S(2)}) collective-permute-start(bf16[128,6528]{1,0:T(8,128)(2,1)} %collective-permute-done.24.refs_6_), channel_id=1, source_target_pairs={{0,1},{1,0},{2,3},{3,2},{4,5},{5,4},{6,7},{7,6},{8,9},{9,8},{10,11... | collective-permute-start | bytes 5013512 | tf_op jit(solution)/shard_map/ppermute | solution.py:587
  473.2 22.1 %collective-permute-start.30 = (bf16[48,6528]{1,0:T(8,128)(2,1)}, bf16[48,6528]{1,0:T(8,128)(2,1)}, u32[]{:S(2)}, u32[]{:S(2)}) collective-permute-start(bf16[48,6528]{1,0:T(8,128)(2,1)} %get-tuple-element.183), channel_id=1, source_target_pairs={{0,4},{1,5},{2,6},{3,7},{16,20},{17,21},{18,22},{19,23}} | collective-permute-start | bytes 1880072 | tf_op jit(solution)/shard_map/ppermute | solution.py:655
  488.3 18.0 %collective-permute-start.41 = (bf16[192,1536]{1,0:T(8,128)(2,1)}, bf16[192,1536]{1,0:T(8,128)(2,1)}, u32[]{:S(2)}, u32[]{:S(2)}) collective-permute-start(bf16[192,1536]{1,0:T(8,128)(2,1)} %collective-permute-done.39.refs_5_), channel_id=1, source_target_pairs={{8,4},{4,0},{9,5},{5,1},{10,6},{6,2},{11,7},{7,3},{24,20},{20,16},... | collective-permute-start | bytes 1769480 | tf_op jit(solution)/shard_map/ppermute | solution.py:656
  509.3 21.4 %collective-permute-start.42 = (bf16[48,6528]{1,0:T(8,128)(2,1)}, bf16[48,6528]{1,0:T(8,128)(2,1)}, u32[]{:S(2)}, u32[]{:S(2)}) collective-permute-start(bf16[48,6528]{1,0:T(8,128)(2,1)} %get-tuple-element.181), channel_id=1, source_target_pairs={{0,4},{4,8},{1,5},{5,9},{2,6},{6,10},{3,7},{7,11},{16,20},{20,24},... | collective-permute-start | bytes 1880072 | tf_op jit(solution)/shard_map/ppermute | solution.py:655
  654.7 21.6 %collective-permute-start.60 = (bf16[48,6528]{1,0:T(8,128)(2,1)}, bf16[48,6528]{1,0:T(8,128)(2,1)}, u32[]{:S(2)}, u32[]{:S(2)}) collective-permute-start(bf16[48,6528]{1,0:T(8,128)(2,1)} %collective-permute-done.58.refs_2_), channel_id=1, source_target_pairs={{8,12},{9,13},{10,14},{11,15},{24,28},{25,29},{26,30},{27,31}} | collective-permute-start | bytes 1880072 | tf_op jit(solution)/shard_map/ppermute | solution.py:655
  656.2 20.1 %collective-permute-start.61 = (bf16[48,6528]{1,0:T(8,128)(2,1)}, bf16[48,6528]{1,0:T(8,128)(2,1)}, u32[]{:S(2)}, u32[]{:S(2)}) collective-permute-start(bf16[48,6528]{1,0:T(8,128)(2,1)} %collective-permute-done.59.refs_3_), channel_id=1, source_target_pairs={{4,0},{5,1},{6,2},{7,3},{20,16},{21,17},{22,18},{23,19}} | collective-permute-start | bytes 1880072 | tf_op jit(solution)/shard_map/ppermute | solution.py:656
  (192 other events, 1680.3 us)
Sparse Core Ops, SparseCore 0:
  34.6 53.3 all-gather.2
  90.2 28.8 all-gather.4
  375.6 51.8 reduce-scatter.1

commit v3 on v2

--- a/solution.py
+++ b/solution.py
@@ -7,6 +7,8 @@
 from jax.experimental.pallas import tpu as pltpu
 from jax.sharding import PartitionSpec as P
 
+
+SECTION, FSDP, DP = ("section", "fsdp", "dp")
 
 HEAD_DIM = 64
 STATE = 128
@@ -93,8 +95,8 @@
 
 
 def mixer_forward_kernel(
-    inner, heads, proj_ref, dt_ref, taps_ref, bias_ref, dtb_ref, dlog_ref, skip_ref, gain_ref,
-    mixed_ref, mixed_t_ref, local_ref, cum_t, col_b, step_b, gated_s,
+    inner, heads, transposed, proj_ref, dt_ref,
+    taps_ref, bias_ref, dtb_ref, dlog_ref, skip_ref, gain_ref, mixed_ref, mixed_t_ref, local_ref, cum_t, col_b, step_b, gated_s,
 ):
     length = proj_ref.shape[0]
     square = (length, LANES)
@@ -136,7 +138,8 @@
         chan = pl.ds(pl.multiple_of(i * LANES, LANES), LANES)
         mixed = gated_s[:, chan] * inverse * gain_ref[:, chan]
         mixed_ref[:, chan] = mixed.astype(jnp.bfloat16)
-        mixed_t_ref[chan, :] = mixed.T.astype(jnp.bfloat16)
+        if transposed:
+            mixed_t_ref[chan, :] = mixed.T.astype(jnp.bfloat16)
         return 0
 
     lax.fori_loop(0, inner // LANES, scale, 0)
@@ -297,23 +300,23 @@
     ]
 
 
-def mixer_forward(projected, dt_raw, params, length):
+def mixer_forward(projected, dt_raw, params, length, transposed):
     row_count, cols = projected.shape
     inner = params[5].shape[1]
     heads = inner // HEAD_DIM
     return pl.pallas_call(
-        functools.partial(mixer_forward_kernel, inner, heads),
+        functools.partial(mixer_forward_kernel, inner, heads, transposed),
         grid=(row_count // length,),
         in_specs=[by_sequence(length, cols), by_sequence(length, LANES)]
         + [whole(p.shape) for p in params],
         out_specs=[
             by_sequence(length, inner),
-            pl.BlockSpec((inner, length), lambda s: (0, s)),
+            pl.BlockSpec((inner if transposed else LANES, length), lambda s: (0, s)),
             by_sequence(length, inner),
         ],
         out_shape=[
             jax.ShapeDtypeStruct((row_count, inner), jnp.bfloat16),
-            jax.ShapeDtypeStruct((inner, row_count), jnp.bfloat16),
+            jax.ShapeDtypeStruct((inner if transposed else LANES, row_count), jnp.bfloat16),
             jax.ShapeDtypeStruct((row_count, inner), jnp.float32),
         ],
         scratch_shapes=scratch(length, heads) + [pltpu.VMEM((length, inner), jnp.float32)],
@@ -322,7 +325,6 @@
             flops=row_count * inner * 600, bytes_accessed=row_count * (cols * 4 + inner * 6),
             transcendentals=row_count * (heads * length + 2 * cols),
         ),
-        name="mixer_forward",
     )(projected, dt_raw, *params)
 
 
@@ -363,7 +365,6 @@
             flops=row_count * inner * 1500, bytes_accessed=row_count * (cols * 6 + inner * 8),
             transcendentals=row_count * (heads * length + 3 * cols),
         ),
-        name="mixer_backward",
     )(projected, dt_raw, local, grad_mixed, *params)
 
 
@@ -587,13 +588,45 @@
     return lax.ppermute(block, axis, [(i, target(i, hop, flip, size)) for i in range(size)])
 
 
-def spread_blocks(block_for, axis):
-    size = lax.axis_size(axis)
-    me = lax.axis_index(axis)
+def arrange_kernel(counts, owner_ref, *refs):
+    sources, outs = refs[:-counts[2]], refs[-counts[2] :]
+    length = sources[0].shape[1]
+    for j, out in enumerate(outs):
+        for m in range(len(sources) // 2):
+            lanes = slice(m * length, (m + 1) * length)
+            for part, rows in enumerate(counts[:2]):
+                where = pl.ds(pl.multiple_of(owner_ref[j] * rows, 16), rows)
+                first = part * counts[0]
+                out[first : first + rows, lanes] = sources[2 * m + part][where, :]
+
+
+def arranged(kept, in_rows, out_rows):
+    size = lax.axis_size(FSDP)
+    me = lax.axis_index(FSDP)
+    owners = jnp.stack(
+        [target(me, hop, flip, size) for flip in range(2) for hop in range(size // 2)]
+    ).astype(jnp.int32)
+    sources = [block for pair in kept for block in pair]
+    shape = (in_rows + out_rows, sum(pair[0].shape[1] for pair in kept))
+    return pl.pallas_call(
+        functools.partial(arrange_kernel, (in_rows, out_rows, size)),
+        grid_spec=pltpu.PrefetchScalarGridSpec(
+            num_scalar_prefetch=1,
+            grid=(1,),
+            in_specs=[pl.BlockSpec(s.shape, lambda t, owner: (0, 0)) for s in sources],
+            out_specs=[pl.BlockSpec(shape, lambda t, owner: (0, 0)) for _ in range(size)],
+        ),
+        out_shape=[jax.ShapeDtypeStruct(shape, jnp.bfloat16) for _ in range(size)],
+        compiler_params=pltpu.CompilerParams(vmem_limit_bytes=24 * 1024 * 1024),
+    )(owners, *sources)
+
+
+def spread_blocks(blocks, axis):
+    chips = lax.axis_size(axis) // 2
     received = []
     for flip in range(2):
-        for hop in range(size // 2):
-            block = block_for(target(me, hop, flip, size))
+        for hop in range(chips):
+            block = blocks[flip * chips + hop]
             received.append(routed(block, axis, hop, flip) if hop or flip else block)
     return received
 
@@ -671,33 +704,33 @@
     ]
 
 
-def gathered_weights(owns, narrow, share):
-    size = lax.axis_size("dp")
-    chips = lax.axis_size("fsdp") // 2
+def gathered_weights(owns, narrow, share, prepared):
+    size = lax.axis_size(DP)
+    chips = lax.axis_size(FSDP) // 2
     stripes = [int(own.shape[0] * share) // (16 * size) * 16 for own in owns]
     directs = [own.shape[0] - stripe * size for own, stripe in zip(owns, stripes)]
     arrived = []
     for i, own in enumerate(owns):
-        start = directs[i] + lax.axis_index("dp") * stripes[i]
+        start = directs[i] + lax.axis_index(DP) * stripes[i]
         part = lax.dynamic_slice_in_dim(own, start, stripes[i], 0)
         hops = range(1, chips) if stripes[i] else ()
-        arrived.append([routed(part, "fsdp", hop, 0) for hop in hops])
-    narrows = [narrow] + [routed(narrow, "fsdp", hop, 0) for hop in range(1, chips)]
-    narrows += [routed(block, "fsdp", 0, 1) for block in narrows]
-    arrived, owns, narrows = lax.optimization_barrier((arrived, owns, narrows))
+        arrived.append([routed(part, FSDP, hop, 0) for hop in hops])
+    narrows = [narrow] + [routed(narrow, FSDP, hop, 0) for hop in range(1, chips)]
+    narrows += [routed(block, FSDP, 0, 1) for block in narrows]
+    arrived, owns, narrows, prepared = lax.optimization_barrier((arrived, owns, narrows, prepared))
     full = []
     for i, own in enumerate(owns):
         same = [own]
         for hop in range(1, chips):
-            same.append(routed(own[: directs[i]], "fsdp", hop, 0))
+            same.append(routed(own[: directs[i]], FSDP, hop, 0))
             if stripes[i]:
                 same.append(
-                    lax.all_gather(arrived[i][hop - 1], "dp", axis=0, tiled=True)
+                    lax.all_gather(arrived[i][hop - 1], DP, axis=0, tiled=True)
                 )
-        other = [routed(own, "fsdp", 0, 1)]
-        other += [routed(piece, "fsdp", 0, 1) for piece in same[1:]]
+        other = [routed(own, FSDP, 0, 1)]
+        other += [routed(piece, FSDP, 0, 1) for piece in same[1:]]
         full.append(same + other)
-    return full, narrows
+    return full, narrows, prepared
 
 
 def butterfly_sum(block, axis):
@@ -724,13 +757,10 @@
     gate_gain,
     out_weight,
 ):
-    first_section = lax.axis_index("section") == 0
-    (in_pieces, out_pieces), dt_blocks = gathered_weights(
-        (in_weight[0], out_weight[0]), dt_weight[0], 1 / 2
-    )
-    ranks = lax.axis_size("fsdp")
+    first_section = lax.axis_index(SECTION) == 0
+    ranks = lax.axis_size(FSDP)
     chips = ranks // 2
-    place = lax.axis_index("fsdp")
+    place = lax.axis_index(FSDP)
     order = jnp.stack(
         [
             (place // 2 - hop) % chips * 2 + (place + flip) % 2
@@ -744,14 +774,11 @@
             for owner in range(ranks)
         ]
     ).astype(jnp.int32)
-    depth = lax.axis_size("dp")
-    line = ((lax.axis_index("dp") - jnp.arange(depth)) % depth).astype(jnp.int32)
+    depth = lax.axis_size(DP)
+    line = ((lax.axis_index(DP) - jnp.arange(depth)) % depth).astype(jnp.int32)
     own_gain = norm_gain[0]
     inner = gate_gain.shape[1]
     heads = decay_log.shape[1]
-    dt_blocks = jnp.stack(dt_blocks)
-    full_dt = jnp.concatenate([dt_blocks[places[owner]] for owner in range(ranks)], axis=0)
-    full_dt = jnp.pad(full_dt, ((0, 0), (0, LANES - heads)))
     small = kernel_params(
         (conv_weight[0], conv_bias[0], dt_bias[0], decay_log[0], skip_gain[0], gate_gain[0]), inner
     )
@@ -771,7 +798,17 @@
         )
 
     def relayed(rows, distance):
-        return passed_along(rows, "section", distance).astype(jnp.float32)
+        return passed_along(rows, SECTION, distance).astype(jnp.float32)
+
+    normed = front_norm(
+        jnp.where(first_section, micro_rows(inputs, 0), empty_rows), own_gain
+    ).astype(jnp.bfloat16)
+    (in_pieces, out_pieces), dt_blocks, (normed, small, order, places, line) = gathered_weights(
+        (in_weight[0], out_weight[0]), dt_weight[0], 1 / 2, (normed, small, order, places, line)
+    )
+    dt_blocks = jnp.stack(dt_blocks)
+    full_dt = jnp.concatenate([dt_blocks[places[owner]] for owner in range(ranks)], axis=0)
+    full_dt = jnp.pad(full_dt, ((0, 0), (0, LANES - heads)))
 
     layer_inputs = []
     results = []
@@ -779,29 +816,19 @@
     for tick in range(MICRO + 1):
         arrived = relayed(output_low, 1) if tick > 0 else empty_rows
         residual = jnp.where(first_section, micro_rows(inputs, tick % MICRO), arrived)
-        normed = front_norm(residual, own_gain).astype(jnp.bfloat16)
+        if tick > 0:
+            normed = front_norm(residual, own_gain).astype(jnp.bfloat16)
         projected = forward_product(normed, in_pieces, in_rows, order, 1280)
         dt_raw = jnp.dot(normed, full_dt, preferred_element_type=jnp.float32)
-        mixed, mixed_t, local = mixer_forward(projected, dt_raw, small, length)
+        mixed, mixed_t, local = mixer_forward(projected, dt_raw, small, length, tick > 0)
         output, output_low = forward_product(mixed, out_pieces, out_rows, order, 512, residual)
         layer_inputs.append(residual)
         results.append(output)
         kept_all.append((normed.T, mixed_t, projected, dt_raw, local))
 
-    columns = [
-        jnp.concatenate([kept_all[tick][j] for tick in (MICRO, 1)], axis=1) for j in range(2)
-    ]
-
-    def columns_of(owner):
-        return jnp.concatenate(
-            [
-                lax.dynamic_slice_in_dim(columns[0], owner * in_rows, in_rows, 0),
-                lax.dynamic_slice_in_dim(columns[1], owner * out_rows, out_rows, 0),
-            ],
-            axis=0,
-        )
-
-    lefts = spread_blocks(columns_of, "fsdp")
+    lefts = spread_blocks(
+        arranged([kept_all[tick][:2] for tick in (MICRO, 1)], in_rows, out_rows), FSDP
+    )
 
     grads_back = []
     small_all = []
@@ -830,21 +857,21 @@
         grads_back.append(grad_output + grad_residual)
         if tick > 0:
             small_all.append([grad_gain] + small_terms)
-            rounded_all.append(gathered_blocks(grad_rounded, "fsdp"))
-            terms_all.append(gathered_blocks(grad_cat, "fsdp"))
+            rounded_all.append(gathered_blocks(grad_rounded, FSDP))
+            terms_all.append(gathered_blocks(grad_cat, FSDP))
 
     def by_source(gathered):
         return [blocks[j] for j in range(len(lefts)) for blocks in gathered]
 
     def scattered(part):
-        return lax.psum_scatter(part, "dp", scatter_dimension=0, tiled=True)
+        return lax.psum_scatter(part, DP, scatter_dimension=0, tiled=True)
 
     part_out = summed_product(lefts, by_source(rounded_all), in_rows, out_rows, 768)
     chunks = 2 if in_rows % (16 * depth) == 0 else 1
     count = in_rows // chunks
     rights = by_source(terms_all)
     parts = [summed_product(lefts, rights, chunk * count, count, 2304) for chunk in range(chunks)]
-    moved = line_pipeline(scattered(part_out), parts, "dp")
+    moved = line_pipeline(scattered(part_out), parts, DP)
     owned_out = expanded(moved[0], line, 0, 1, model_width, None)[0]
     owned = None
     for chunk in range(chunks):
@@ -857,7 +884,7 @@
     pieces = [
         gain, taps.reshape(-1), bias[0], head[0, :heads], head[1, :heads], skip, gate[0]
     ]
-    flat = butterfly_sum(butterfly_sum(jnp.concatenate(pieces), "fsdp"), "dp")
+    flat = butterfly_sum(butterfly_sum(jnp.concatenate(pieces), FSDP), DP)
     totals = []
     start = 0
     for piece in pieces:
@@ -900,33 +927,33 @@
 
 def solution(mesh):
     in_specs = (
-        P(("dp", "fsdp"), None, None),
-        P(("dp", "fsdp"), None, None),
-        P(("dp", "fsdp")),
-        P("section", None),
-        P("section", "fsdp", None),
-        P("section", "fsdp", None),
-        P("section", None, None),
-        P("section", None),
-        P("section", None),
-        P("section", None),
-        P("section", None),
-        P("section", None),
-        P("section", "fsdp", None),
+        P((DP, FSDP), None, None),
+        P((DP, FSDP), None, None),
+        P((DP, FSDP)),
+        P(SECTION, None),
+        P(SECTION, FSDP, None),
+        P(SECTION, FSDP, None),
+        P(SECTION, None, None),
+        P(SECTION, None),
+        P(SECTION, None),
+        P(SECTION, None),
+        P(SECTION, None),
+        P(SECTION, None),
+        P(SECTION, FSDP, None),
     )
     out_specs = (
-        P("section", ("dp", "fsdp"), None, None),
-        P("section", ("dp", "fsdp"), None, None),
-        P("section", None),
-        P("section", "fsdp", None),
-        P("section", "fsdp", None),
-        P("section", None, None),
-        P("section", None),
-        P("section", None),
-        P("section", None),
-        P("section", None),
-        P("section", None),
-        P("section", "fsdp", None),
+        P(SECTION, (DP, FSDP), None, None),
+        P(SECTION, (DP, FSDP), None, None),
+        P(SECTION, None),
+        P(SECTION, FSDP, None),
+        P(SECTION, FSDP, None),
+        P(SECTION, None, None),
+        P(SECTION, None),
+        P(SECTION, None),
+        P(SECTION, None),
+        P(SECTION, None),
+        P(SECTION, None),
+        P(SECTION, FSDP, None),
     )
     return jax.shard_map(
         per_device, mesh=mesh, in_specs=in_specs, out_specs=out_specs, check_vma=False

time: 699 us -> 695 us (level)
  other arithmetic: 44.2 us -> 31.4 us
  between operations: 16.2 us -> 24.2 us
  waiting for transfers between devices: 260 us -> 267 us
    ppermute x28, waiting for transfers between devices: 162 us -> 179 us  [routed(): lax.ppermute(block, axis, [(i, target(i, hop, flip, size)) for i in range...]
    ppermute x4, waiting for transfers between devices: 11.8 us -> 1.43 us  [passed_along(): return lax.ppermute(block, axis, route)]
    dynamic_slice x5 -> x0, local copies, waits for them, and re-layouts: 8.72 us -> none  [the longest x4 6.05 us: columns_of(): lax.dynamic_slice_in_dim(columns[0], owner * in_rows, in_rows, 0)]
    unnamed x320 -> x327, local copies, waits for them, and re-layouts: 39.9 us -> 41.8 us
    pallas_call x3 -> x4, Pallas kernels: 30.3 us -> 29 us  [the longest x3 28 us: mixer_forward(): pl.pallas_call(functools.partial(mixer_forward_kernel, inner, heads, tran...]
  transfers between devices with their start and end apart: 65 -> 65, of which waited for: 30 -> 28; matrix products, arithmetic and copies ran while one was open for 7% -> 5% of each run, Pallas kernels for 16% -> 20%
where the time goes in v3:
time: 695 us; the launch traced here: 682 us
  waiting for transfers between devices  267 us (38%)
  Pallas kernels  208 us (30%)
  starting transfers between devices  85.2 us (12%)
  local copies, waits for them, and re-layouts  59.9 us (9%)
  other arithmetic  31.4 us (5%)
  between operations  24.2 us (3%)
    ppermute x28, waiting for transfers between devices, routed(): lax.ppermute(block, axis, [(i, target(i, hop, flip, size)) for i in range...  179 us
    pallas_call x3, Pallas kernels, mixer_backward(): pl.pallas_call(functools.partial(mixer_backward_kernel, inner, heads), gr...  53.8 us
    pallas_call x6, Pallas kernels, backward_product(): pl.pallas_call(functools.partial(backward_product_kernel, rows, len(piece...  49.4 us
    ppermute x11, waiting for transfers between devices, line_pipeline(): down = lax.ppermute(job[3], axis, downs)  44.9 us
    unnamed x327, local copies, waits for them, and re-layouts  41.8 us
    pallas_call x6, Pallas kernels, forward_product(): pl.pallas_call(functools.partial(forward_product_kernel, rows, len(pieces...  39.7 us
    ppermute x11, starting transfers between devices, line_pipeline(): up = lax.ppermute(job[2], axis, ups)  31.1 us
    pallas_call x3, Pallas kernels, mixer_forward(): pl.pallas_call(functools.partial(mixer_forward_kernel, inner, heads, tran...  28 us
  transfers between devices with their start and end apart: 65, of which 28 were waited for; matrix products, arithmetic and copies ran while one was open for 5% of the time, Pallas kernels for 20%

profile of v3, /device:TPU:0, one launch (start us, length us, event | category | flops | bytes accessed | tf_op | source)
XLA Modules:
  0.0 681.7 jit_solution(13337770352857865758)
XLA Ops:
  19.5 15.6 %collective-permute-done.1 = bf16[96,1536]{1,0:T(8,128)(2,1)S(1)} collective-permute-done((bf16[96,1536]{1,0:T(8,128)(2,1)}, bf16[96,1536]{1,0:T(8,128)(2,1)S(1)}, u32[]{:S(2)}, u32[]{:S(2)}) %collective-permute-start.1) | collective-permute-done | bytes 294944 | tf_op jit(solution)/shard_map/ppermute | solution.py:588
  39.9 55.6 %collective-permute-done.5.refs_1_ = bf16[192,6400]{1,0:T(8,128)(2,1)} collective-permute-done((bf16[192,6400]{1,0:T(8,128)(2,1)}, bf16[192,6400]{1,0:T(8,128)(2,1)}, u32[]{:S(2)}, u32[]{:S(2)}) %collective-permute-start.5) | collective-permute-done | bytes 2457632 | tf_op jit(solution)/shard_map/ppermute | solution.py:588
  96.4 27.6 %collective-permute-done.9.refs_1_ = bf16[384,1536]{1,0:T(8,128)(2,1)S(1)} collective-permute-done((bf16[384,1536]{1,0:T(8,128)(2,1)S(1)}, bf16[384,1536]{1,0:T(8,128)(2,1)S(1)}, u32[]{:S(2)}, u32[]{:S(2)}) %collective-permute-start.9) | collective-permute-done | bytes 1179680 | tf_op jit(solution)/shard_map/ppermute | solution.py:588
  141.4 7.9 %shard_map.220.proj_ref = f32[128,6400]{1,0:T(8,128)S(1)} custom-call(s32[4]{0:T(128)S(1)} %get-tuple-element.92.order_ref, bf16[128,1536]{1,0:T(8,128)(2,1)S(1)} %copy-done.55, bf16[384,6400]{1,0:T(8,128)(2,1)S(1)} %bitcast.151, bf16[192,6400]{1,0:T(8,128)(2,1)} %collective-permute-done.5.refs_1_, bf16[192,6400]{1,0:T(8,128)(2,1)S(1)} %copy-done.2, ...), custom_call_target="tpu_custom_call" | custom-call | flops 2516582400 | bytes 22937600 | tf_op jit(solution)/shard_map/pallas_call | solution.py:459
  149.4 8.7 %shard_map.221 = (bf16[128,3072]{1,0:T(8,128)(2,1)S(1)}, bf16[128,128]{1,0:T(8,128)(2,1)}, f32[128,3072]{1,0:T(8,128)}) custom-call(f32[128,6400]{1,0:T(8,128)S(1)} %shard_map.220.proj_ref, f32[128,128]{1,0:T(8,128)S(1)} %fusion.48.dt_ref, f32[4,3328]{1,0:T(4,128)S(1)} %bitcast.170, f32[1,3328]{1,0:T(1,128)S(1)} %copy-done.70, f32[1,128]{1,0:T(1,128)S(1)} %copy-done.95, ...), custom_call_target="tpu_custom_call" | custom-call | flops 235929600 | bytes 5636096 | tf_op jit(solution)/shard_map/pallas_call | solution.py:307
  171.9 6.3 shard_map.229.gm_ref
  181.5 7.9 %shard_map.223.proj_ref = f32[128,6400]{1,0:T(8,128)S(1)} custom-call(s32[4]{0:T(128)S(1)} %get-tuple-element.92.order_ref, bf16[128,1536]{1,0:T(8,128)(2,1)S(1)} %multiply_convert_fusion.1.left_ref, bf16[384,6400]{1,0:T(8,128)(2,1)S(1)} %bitcast.154, bf16[192,6400]{1,0:T(8,128)(2,1)} %collective-permute-done.5.refs_1_, bf16[192,6400]{1,0:T(8,128)(2,1)S(1)} %copy-done.3, ...), custom_call_target="tpu_custom_call" | custom-call | flops 2516582400 | bytes 22937600 | tf_op jit(solution)/shard_map/pallas_call | solution.py:459
  189.5 9.7 %shard_map.224 = (bf16[128,3072]{1,0:T(8,128)(2,1)S(1)}, bf16[3072,128]{1,0:T(8,128)(2,1)S(1)}, f32[128,3072]{1,0:T(8,128)S(1)}) custom-call(f32[128,6400]{1,0:T(8,128)S(1)} %shard_map.223.proj_ref, f32[128,128]{1,0:T(8,128)S(1)} %fusion.46.dt_ref, f32[4,3328]{1,0:T(4,128)S(1)} %bitcast.171, f32[1,3328]{1,0:T(1,128)S(1)} %copy-done.71, ...), custom_call_target="tpu_custom_call" | custom-call | flops 235929600 | bytes 5636096 | tf_op jit(solution)/shard_map/pallas_call | solution.py:307
  209.5 17.5 %shard_map.230 = (bf16[128,6528]{1,0:T(8,128)(2,1)S(1)}, f32[4,3328]{1,0:T(4,128)}, f32[1,3328]{1,0:T(1,128)}, f32[1,3072]{1,0:T(1,128)}, f32[1,3072]{1,0:T(1,128)}, /*index=5*/f32[8,128]{1,0:T(8,128)}) custom-call(f32[128,6400]{1,0:T(8,128)} %copy-done.15, f32[128,128]{1,0:T(8,128)S(1)} %fusion.46.dt_ref, f32[128,3072]{1,0:T(8,128)S(1)} %copy-done.27, ...), custom_call_target="tpu_custom_call" | custom-call | flops 589824000 | bytes 8060928 | tf_op jit(solution)/shard_map/pallas_call | solution.py:336
  229.6 10.3 %shard_map.231 = f32[128,1536]{1,0:T(8,128)S(1)} custom-call(s32[4]{0:T(128)S(1)} %get-tuple-element.92.order_ref, bf16[128,6528]{1,0:T(8,128)(2,1)S(1)} %copy-done.48, bf16[384,6400]{1,0:T(8,128)(2,1)S(1)} %bitcast.155, bf16[192,6400]{1,0:T(8,128)(2,1)} %collective-permute-done.5.refs_1_, bf16[192,6400]{1,0:T(8,128)(2,1)S(1)} %copy-done.3, ...), custom_call_target="tpu_custom_call" | custom-call | flops 2516582400 | bytes 20447232 | tf_op jit(solution)/shard_map/pallas_call | solution.py:515
  244.9 7.9 %shard_map.226.proj_ref = f32[128,6400]{1,0:T(8,128)S(1)} custom-call(s32[4]{0:T(128)S(1)} %get-tuple-element.92.order_ref, bf16[128,1536]{1,0:T(8,128)(2,1)S(1)} %get-tuple-element.222.left_ref, bf16[384,6400]{1,0:T(8,128)(2,1)S(1)} %bitcast.156, bf16[192,6400]{1,0:T(8,128)(2,1)} %collective-permute-done.5.refs_1_, bf16[192,6400]{1,0:T(8,128)(2,1)S(1)} %copy-done.3, ...), custom_call_target="tpu_custom_call" | custom-call | flops 2516582400 | bytes 22937600 | tf_op jit(solution)/shard_map/pallas_call | solution.py:459
  252.9 9.7 %shard_map.227 = (bf16[128,3072]{1,0:T(8,128)(2,1)S(1)}, bf16[3072,128]{1,0:T(8,128)(2,1)S(1)}, f32[128,3072]{1,0:T(8,128)S(1)}) custom-call(f32[128,6400]{1,0:T(8,128)S(1)} %shard_map.226.proj_ref, f32[128,128]{1,0:T(8,128)S(1)} %fusion.44.dt_ref, f32[4,3328]{1,0:T(4,128)S(1)} %bitcast.173, f32[1,3328]{1,0:T(1,128)S(1)} %copy-done.71, ...), custom_call_target="tpu_custom_call" | custom-call | flops 235929600 | bytes 5636096 | tf_op jit(solution)/shard_map/pallas_call | solution.py:307
  264.6 6.2 shard_map.232.gm_ref
  270.8 18.1 %shard_map.233 = (bf16[128,6528]{1,0:T(8,128)(2,1)}, f32[4,3328]{1,0:T(4,128)S(1)}, f32[1,3328]{1,0:T(1,128)S(1)}, f32[1,3072]{1,0:T(1,128)S(1)}, f32[1,3072]{1,0:T(1,128)S(1)}, /*index=5*/f32[8,128]{1,0:T(8,128)S(1)}) custom-call(f32[128,6400]{1,0:T(8,128)} %copy-done.20, f32[128,128]{1,0:T(8,128)S(1)} %fusion.44.dt_ref, ...), custom_call_target="tpu_custom_call" | custom-call | flops 589824000 | bytes 8060928 | tf_op jit(solution)/shard_map/pallas_call | solution.py:336
  291.4 10.3 %shard_map.234 = f32[128,1536]{1,0:T(8,128)S(1)} custom-call(s32[4]{0:T(128)S(1)} %get-tuple-element.92.order_ref, bf16[128,6528]{1,0:T(8,128)(2,1)} %get-tuple-element.119.left_ref.refs_4_, bf16[384,6400]{1,0:T(8,128)(2,1)S(1)} %bitcast.157, bf16[192,6400]{1,0:T(8,128)(2,1)} %collective-permute-done.5.refs_1_, bf16[192,6400]{1,0:T(8,128)(2,1)S(1)} %copy-done.3, ...), custom_call_target="tpu_custom_call" | custom-call | flops 2516582400 | bytes 20447232 | tf_op jit(solution)/shard_map/pallas_call | solution.py:515
  319.2 11.0 %collective-permute-done.21.refs_1_ = bf16[1152,256]{1,0:T(8,128)(2,1)S(1)} collective-permute-done((bf16[1152,256]{1,0:T(8,128)(2,1)S(1)}, bf16[1152,256]{1,0:T(8,128)(2,1)S(1)}, u32[]{:S(2)}, u32[]{:S(2)}) %collective-permute-start.21) | collective-permute-done | bytes 589856 | tf_op jit(solution)/shard_map/ppermute | solution.py:588
  330.7 7.9 %collective-permute-done.32.refs_6_ = bf16[128,1536]{1,0:T(8,128)(2,1)S(1)} collective-permute-done((bf16[128,1536]{1,0:T(8,128)(2,1)S(1)}, bf16[128,1536]{1,0:T(8,128)(2,1)S(1)}, u32[]{:S(2)}, u32[]{:S(2)}) %collective-permute-start.32) | collective-permute-done | bytes 393248 | tf_op jit(solution)/shard_map/ppermute | solution.py:588
  338.6 8.4 %collective-permute-done.33.refs_7_ = bf16[128,1536]{1,0:T(8,128)(2,1)S(1)} collective-permute-done((bf16[128,1536]{1,0:T(8,128)(2,1)S(1)}, bf16[128,1536]{1,0:T(8,128)(2,1)S(1)}, u32[]{:S(2)}, u32[]{:S(2)}) %collective-permute-start.33) | collective-permute-done | bytes 393248 | tf_op jit(solution)/shard_map/ppermute | solution.py:588
  347.0 8.7 %collective-permute-done.23.refs_3_ = bf16[1152,256]{1,0:T(8,128)(2,1)S(1)} collective-permute-done((bf16[1152,256]{1,0:T(8,128)(2,1)S(1)}, bf16[1152,256]{1,0:T(8,128)(2,1)S(1)}, u32[]{:S(2)}, u32[]{:S(2)}) %collective-permute-start.23) | collective-permute-done | bytes 589856 | tf_op jit(solution)/shard_map/ppermute | solution.py:588
  367.1 6.2 shard_map.235.gm_ref
  373.3 18.1 %shard_map.236 = (bf16[128,6528]{1,0:T(8,128)(2,1)}, f32[4,3328]{1,0:T(4,128)S(1)}, f32[1,3328]{1,0:T(1,128)S(1)}, f32[1,3072]{1,0:T(1,128)S(1)}, f32[1,3072]{1,0:T(1,128)S(1)}, /*index=5*/f32[8,128]{1,0:T(8,128)S(1)}) custom-call(f32[128,6400]{1,0:T(8,128)} %copy-done.15, f32[128,128]{1,0:T(8,128)S(1)} %copy-done.69, f32[128,3072]{1,0:T(8,128)S(1)} %copy-done.28, ...), custom_call_target="tpu_custom_call" | custom-call | flops 589824000 | bytes 8060928 | tf_op jit(solution)/shard_map/pallas_call | solution.py:336
  396.2 5.9 collective-permute-done.24.refs_6_
  403.9 34.1 %collective-permute-done.25.refs_7_ = bf16[128,6528]{1,0:T(8,128)(2,1)} collective-permute-done((bf16[128,6528]{1,0:T(8,128)(2,1)}, bf16[128,6528]{1,0:T(8,128)(2,1)}, u32[]{:S(2)}, u32[]{:S(2)}) %collective-permute-start.25) | collective-permute-done | bytes 1671200 | tf_op jit(solution)/shard_map/ppermute | solution.py:588
  446.4 8.3 %shard_map.240 = bf16[192,6528]{1,0:T(8,128)(2,1)} custom-call(bf16[1152,256]{1,0:T(8,128)(2,1)S(1)} %copy-done.36, bf16[1152,256]{1,0:T(8,128)(2,1)S(1)} %copy-done.39, bf16[1152,256]{1,0:T(8,128)(2,1)S(1)} %copy-done.42, bf16[1152,256]{1,0:T(8,128)(2,1)S(1)} %copy-done.45, bf16[128,6528]{1,0:T(8,128)(2,1)} %get-tuple-element.119.left_ref.refs_4_, ...), custom_call_target="tpu_custom_call" | custom-call | flops 2566914048 | bytes 15876096 | tf_op jit(solution)/shard_map/pallas_call | solution.py:391
  479.3 5.7 collective-permute-done.30
  485.0 11.2 %collective-permute-done.41.refs_3_ = bf16[192,1536]{1,0:T(8,128)(2,1)} collective-permute-done((bf16[192,1536]{1,0:T(8,128)(2,1)}, bf16[192,1536]{1,0:T(8,128)(2,1)}, u32[]{:S(2)}, u32[]{:S(2)}) %collective-permute-start.41) | collective-permute-done | bytes 589856 | tf_op jit(solution)/shard_map/ppermute | solution.py:689
  507.9 13.1 %collective-permute-done.45.refs_1_ = bf16[192,1536]{1,0:T(8,128)(2,1)} collective-permute-done((bf16[192,1536]{1,0:T(8,128)(2,1)}, bf16[192,1536]{1,0:T(8,128)(2,1)}, u32[]{:S(2)}, u32[]{:S(2)}) %collective-permute-start.45) | collective-permute-done | bytes 589856 | tf_op jit(solution)/shard_map/ppermute | solution.py:689
  527.6 7.9 %collective-permute-done.46 = bf16[48,6528]{1,0:T(8,128)(2,1)} collective-permute-done((bf16[48,6528]{1,0:T(8,128)(2,1)}, bf16[48,6528]{1,0:T(8,128)(2,1)}, u32[]{:S(2)}, u32[]{:S(2)}) %collective-permute-start.46) | collective-permute-done | bytes 626720 | tf_op jit(solution)/shard_map/ppermute | solution.py:688
  551.0 8.3 %shard_map.239 = bf16[192,6528]{1,0:T(8,128)(2,1)} custom-call(bf16[1152,256]{1,0:T(8,128)(2,1)S(1)} %copy-done.37, bf16[1152,256]{1,0:T(8,128)(2,1)S(1)} %copy-done.40, bf16[1152,256]{1,0:T(8,128)(2,1)S(1)} %copy-done.43, bf16[1152,256]{1,0:T(8,128)(2,1)S(1)} %copy-done.46, bf16[128,6528]{1,0:T(8,128)(2,1)} %get-tuple-element.119.left_ref.refs_4_, ...), custom_call_target="tpu_custom_call" | custom-call | flops 2566914048 | bytes 15876096 | tf_op jit(solution)/shard_map/pallas_call | solution.py:391
  568.9 6.3 collective-permute-done.50.refs_2_
  602.9 10.2 %shard_map.237 = f32[128,1536]{1,0:T(8,128)S(1)} custom-call(s32[4]{0:T(128)S(1)} %get-tuple-element.92.order_ref, bf16[128,6528]{1,0:T(8,128)(2,1)} %get-tuple-element.120.left_ref.refs_5_, bf16[384,6400]{1,0:T(8,128)(2,1)S(1)} %bitcast.160, bf16[192,6400]{1,0:T(8,128)(2,1)} %collective-permute-done.5.refs_1_, bf16[192,6400]{1,0:T(8,128)(2,1)S(1)} %copy-done.4, ...), custom_call_target="tpu_custom_call" | custom-call | flops 2516582400 | bytes 20447232 | tf_op jit(solution)/shard_map/pallas_call | solution.py:515
  640.5 6.8 collective-permute-done.59.refs_3_
  (534 shorter events, 260.2 us)
Async XLA Ops:
  7.2 88.2 %all-gather.3.cloned.1.call-start = ((), (), s32[]{:S(2)}) async-start(), calls=%async_computation.1 | async-start | bytes 3072000 | tf_op jit(solution)/shard_map/all_gather | solution.py:728
  12.2 22.8 %collective-permute-start = (bf16[48,6400]{1,0:T(8,128)(2,1)}, bf16[48,6400]{1,0:T(8,128)(2,1)S(1)}, u32[]{:S(2)}, u32[]{:S(2)}) collective-permute-start(bf16[48,6400]{1,0:T(8,128)(2,1)} %dynamic-slice_bitcast_fusion.2), channel_id=1, source_target_pairs={{0,2},{1,3},{2,0},{3,1},{4,6},{5,7},{6,4},{7,5},{8,10},{9,11},{10,... | collective-permute-start | bytes 1843208 | tf_op jit(solution)/shard_map/ppermute | solution.py:588
  14.2 20.9 %collective-permute-start.1 = (bf16[96,1536]{1,0:T(8,128)(2,1)}, bf16[96,1536]{1,0:T(8,128)(2,1)S(1)}, u32[]{:S(2)}, u32[]{:S(2)}) collective-permute-start(bf16[96,1536]{1,0:T(8,128)(2,1)} %dynamic-slice_bitcast_fusion.3), channel_id=1, source_target_pairs={{0,2},{1,3},{2,0},{3,1},{4,6},{5,7},{6,4},{7,5},{8,10},{9,11},{10,... | collective-permute-start | bytes 884744 | tf_op jit(solution)/shard_map/ppermute | solution.py:588
  35.9 88.1 %all-gather.5.cloned.1.call-start = ((), (), s32[]{:S(2)}) async-start(), calls=%async_computation.2 | async-start | bytes 1474560 | tf_op jit(solution)/shard_map/all_gather | solution.py:728
  36.0 88.0 %collective-permute-start.6 = (bf16[384,6400]{1,0:T(8,128)(2,1)}, bf16[384,6400]{1,0:T(8,128)(2,1)}, u32[]{:S(2)}, u32[]{:S(2)}) collective-permute-start(bf16[384,6400]{1,0:T(8,128)(2,1)} %bitcast.149), channel_id=1, source_target_pairs={{0,1},{1,0},{2,3},{3,2},{4,5},{5,4},{6,7},{7,6},{8,9},{9,8},{10,11... | collective-permute-start | bytes 14745608 | tf_op jit(solution)/shard_map/ppermute | solution.py:588
  39.5 55.9 %collective-permute-start.5 = (bf16[192,6400]{1,0:T(8,128)(2,1)}, bf16[192,6400]{1,0:T(8,128)(2,1)}, u32[]{:S(2)}, u32[]{:S(2)}) collective-permute-start(bf16[192,6400]{1,0:T(8,128)(2,1)} %slice.81), channel_id=1, source_target_pairs={{0,2},{1,3},{2,0},{3,1},{4,6},{5,7},{6,4},{7,5},{8,10},{9,11},{10,... | collective-permute-start | bytes 7372808 | tf_op jit(solution)/shard_map/ppermute | solution.py:588
  39.8 414.9 %reduce-scatter.2.cloned.1.call-start = ((), (), s32[]{:S(2)}) async-start(), calls=%async_computation.3 | async-start | bytes 2949120 | tf_op jit(solution)/shard_map/reduce_scatter | solution.py:867
  95.4 43.2 %collective-permute-start.7 = (bf16[192,6400]{1,0:T(8,128)(2,1)}, bf16[192,6400]{1,0:T(8,128)(2,1)}, u32[]{:S(2)}, u32[]{:S(2)}) collective-permute-start(bf16[192,6400]{1,0:T(8,128)(2,1)} %collective-permute-done.5.refs_1_), channel_id=1, source_target_pairs={{0,1},{1,0},{2,3},{3,2},{4,5},{5,4},{6,7},{7,6},{8,9},{9,8},{10,11... | collective-permute-start | bytes 7372808 | tf_op jit(solution)/shard_map/ppermute | solution.py:588
  95.4 43.2 %collective-permute-start.8 = (bf16[192,6400]{1,0:T(8,128)(2,1)}, bf16[192,6400]{1,0:T(8,128)(2,1)}, u32[]{:S(2)}, u32[]{:S(2)}) collective-permute-start(bf16[192,6400]{1,0:T(8,128)(2,1)} %all-gather.3.cloned.1.call-done.refs_2_), channel_id=1, source_target_pairs={{0,1},{1,0},{2,3},{3,2},{4,5},{5,4},{6,7},{7,6},{8,9},{9,8},{10,11... | collective-permute-start | bytes 7372808 | tf_op jit(solution)/shard_map/ppermute | solution.py:588
  96.0 28.0 %collective-permute-start.9 = (bf16[384,1536]{1,0:T(8,128)(2,1)S(1)}, bf16[384,1536]{1,0:T(8,128)(2,1)S(1)}, u32[]{:S(2)}, u32[]{:S(2)}) collective-permute-start(bf16[384,1536]{1,0:T(8,128)(2,1)S(1)} %slice.86), channel_id=1, source_target_pairs={{0,2},{1,3},{2,0},{3,1},{4,6},{5,7},{6,4},{7,5},{8,10},{9,11},{10,... | collective-permute-start | bytes 3538952 | tf_op jit(solution)/shard_map/ppermute | solution.py:588
  96.4 61.7 %collective-permute-start.10 = (bf16[768,1536]{1,0:T(8,128)(2,1)S(1)}, bf16[768,1536]{1,0:T(8,128)(2,1)}, u32[]{:S(2)}, u32[]{:S(2)}) collective-permute-start(bf16[768,1536]{1,0:T(8,128)(2,1)S(1)} %bitcast.162), channel_id=1, source_target_pairs={{0,1},{1,0},{2,3},{3,2},{4,5},{5,4},{6,7},{7,6},{8,9},{9,8},{10,11... | collective-permute-start | bytes 7077896 | tf_op jit(solution)/shard_map/ppermute | solution.py:588
  124.0 34.1 %collective-permute-start.11 = (bf16[384,1536]{1,0:T(8,128)(2,1)S(1)}, bf16[384,1536]{1,0:T(8,128)(2,1)}, u32[]{:S(2)}, u32[]{:S(2)}) collective-permute-start(bf16[384,1536]{1,0:T(8,128)(2,1)S(1)} %collective-permute-done.9.refs_1_), channel_id=1, source_target_pairs={{0,1},{1,0},{2,3},{3,2},{4,5},{5,4},{6,7},{7,6},{8,9},{9,8},{10,11... | collective-permute-start | bytes 3538952 | tf_op jit(solution)/shard_map/ppermute | solution.py:588
  124.0 34.1 %collective-permute-start.12 = (bf16[384,1536]{1,0:T(8,128)(2,1)}, bf16[384,1536]{1,0:T(8,128)(2,1)}, u32[]{:S(2)}, u32[]{:S(2)}) collective-permute-start(bf16[384,1536]{1,0:T(8,128)(2,1)} %all-gather.5.cloned.1.call-done.refs_2_), channel_id=1, source_target_pairs={{0,1},{1,0},{2,3},{3,2},{4,5},{5,4},{6,7},{7,6},{8,9},{9,8},{10,11... | collective-permute-start | bytes 3538952 | tf_op jit(solution)/shard_map/ppermute | solution.py:588
  205.1 35.7 %collective-permute-start.14 = (bf16[128,1536]{1,0:T(8,128)(2,1)S(1)}, bf16[128,1536]{1,0:T(8,128)(2,1)}, u32[]{:S(2)}, u32[]{:S(2)}) collective-permute-start(bf16[128,1536]{1,0:T(8,128)(2,1)S(1)} %get-tuple-element.112), channel_id=1, source_target_pairs={{0,16},{1,17},{2,18},{3,19},{4,20},{5,21},{6,22},{7,23},{8,24},{9,... | collective-permute-start | bytes 1179656 | tf_op jit(solution)/shard_map/ppermute | solution.py:26
  243.4 19.2 %collective-permute-start.15 = (bf16[128,1536]{1,0:T(8,128)(2,1)S(1)}, bf16[128,1536]{1,0:T(8,128)(2,1)S(1)}, u32[]{:S(2)}, u32[]{:S(2)}) collective-permute-start(bf16[128,1536]{1,0:T(8,128)(2,1)S(1)} %get-tuple-element.221), channel_id=1, source_target_pairs={{16,0},{17,1},{18,2},{19,3},{20,4},{21,5},{22,6},{23,7},{24,8},{25... | collective-permute-start | bytes 1179656 | tf_op jit(solution)/shard_map/ppermute | solution.py:26
  314.5 24.1 %collective-permute-start.32 = (bf16[128,1536]{1,0:T(8,128)(2,1)S(1)}, bf16[128,1536]{1,0:T(8,128)(2,1)S(1)}, u32[]{:S(2)}, u32[]{:S(2)}) collective-permute-start(bf16[128,1536]{1,0:T(8,128)(2,1)S(1)} %copy-done.50), channel_id=1, source_target_pairs={{0,2},{1,3},{2,0},{3,1},{4,6},{5,7},{6,4},{7,5},{8,10},{9,11},{10,... | collective-permute-start | bytes 1179656 | tf_op jit(solution)/shard_map/ppermute | solution.py:588
  318.6 28.4 %collective-permute-start.33 = (bf16[128,1536]{1,0:T(8,128)(2,1)S(1)}, bf16[128,1536]{1,0:T(8,128)(2,1)S(1)}, u32[]{:S(2)}, u32[]{:S(2)}) collective-permute-start(bf16[128,1536]{1,0:T(8,128)(2,1)S(1)} %fusion.23.left_ref.refs_5_), channel_id=1, source_target_pairs={{0,2},{1,3},{2,0},{3,1},{4,6},{5,7},{6,4},{7,5},{8,10},{9,11},{10,... | collective-permute-start | bytes 1179656 | tf_op jit(solution)/shard_map/ppermute | solution.py:588
  319.2 36.6 %collective-permute-start.23 = (bf16[1152,256]{1,0:T(8,128)(2,1)S(1)}, bf16[1152,256]{1,0:T(8,128)(2,1)S(1)}, u32[]{:S(2)}, u32[]{:S(2)}) collective-permute-start(bf16[1152,256]{1,0:T(8,128)(2,1)S(1)} %get-tuple-element.137), channel_id=1, source_target_pairs={{0,3},{1,2},{2,1},{3,0},{4,7},{5,6},{6,5},{7,4},{8,11},{9,10},{10,... | collective-permute-start | bytes 1769480 | tf_op jit(solution)/shard_map/ppermute | solution.py:588
  330.2 25.6 %collective-permute-start.34 = (bf16[128,1536]{1,0:T(8,128)(2,1)S(1)}, bf16[128,1536]{1,0:T(8,128)(2,1)S(1)}, u32[]{:S(2)}, u32[]{:S(2)}) collective-permute-start(bf16[128,1536]{1,0:T(8,128)(2,1)S(1)} %copy-done.50), channel_id=1, source_target_pairs={{0,1},{1,0},{2,3},{3,2},{4,5},{5,4},{6,7},{7,6},{8,9},{9,8},{10,11... | collective-permute-start | bytes 1179656 | tf_op jit(solution)/shard_map/ppermute | solution.py:588
  330.2 25.5 %collective-permute-start.35 = (bf16[128,1536]{1,0:T(8,128)(2,1)S(1)}, bf16[128,1536]{1,0:T(8,128)(2,1)S(1)}, u32[]{:S(2)}, u32[]{:S(2)}) collective-permute-start(bf16[128,1536]{1,0:T(8,128)(2,1)S(1)} %fusion.23.left_ref.refs_5_), channel_id=1, source_target_pairs={{0,1},{1,0},{2,3},{3,2},{4,5},{5,4},{6,7},{7,6},{8,9},{9,8},{10,11... | collective-permute-start | bytes 1179656 | tf_op jit(solution)/shard_map/ppermute | solution.py:588
  363.2 38.9 %collective-permute-start.24 = (bf16[128,6528]{1,0:T(8,128)(2,1)}, bf16[128,6528]{1,0:T(8,128)(2,1)}, u32[]{:S(2)}, u32[]{:S(2)}) collective-permute-start(bf16[128,6528]{1,0:T(8,128)(2,1)} %get-tuple-element.119.left_ref.refs_4_), channel_id=1, source_target_pairs={{0,2},{1,3},{2,0},{3,1},{4,6},{5,7},{6,4},{7,5},{8,10},{9,11},{10,... | collective-permute-start | bytes 5013512 | tf_op jit(solution)/shard_map/ppermute | solution.py:588
  394.5 43.5 %collective-permute-start.25 = (bf16[128,6528]{1,0:T(8,128)(2,1)}, bf16[128,6528]{1,0:T(8,128)(2,1)}, u32[]{:S(2)}, u32[]{:S(2)}) collective-permute-start(bf16[128,6528]{1,0:T(8,128)(2,1)} %get-tuple-element.120.left_ref.refs_5_), channel_id=1, source_target_pairs={{0,2},{1,3},{2,0},{3,1},{4,6},{5,7},{6,4},{7,5},{8,10},{9,11},{10,... | collective-permute-start | bytes 5013512 | tf_op jit(solution)/shard_map/ppermute | solution.py:588
  395.7 42.9 %collective-permute-start.26 = (bf16[128,6528]{1,0:T(8,128)(2,1)}, bf16[128,6528]{1,0:T(8,128)(2,1)}, u32[]{:S(2)}, u32[]{:S(2)}) collective-permute-start(bf16[128,6528]{1,0:T(8,128)(2,1)} %get-tuple-element.119.left_ref.refs_4_), channel_id=1, source_target_pairs={{0,1},{1,0},{2,3},{3,2},{4,5},{5,4},{6,7},{7,6},{8,9},{9,8},{10,11... | collective-permute-start | bytes 5013512 | tf_op jit(solution)/shard_map/ppermute | solution.py:588
  396.2 42.4 %collective-permute-start.27 = (bf16[128,6528]{1,0:T(8,128)(2,1)}, bf16[128,6528]{1,0:T(8,128)(2,1)}, u32[]{:S(2)}, u32[]{:S(2)}) collective-permute-start(bf16[128,6528]{1,0:T(8,128)(2,1)} %get-tuple-element.120.left_ref.refs_5_), channel_id=1, source_target_pairs={{0,1},{1,0},{2,3},{3,2},{4,5},{5,4},{6,7},{7,6},{8,9},{9,8},{10,11... | collective-permute-start | bytes 5013512 | tf_op jit(solution)/shard_map/ppermute | solution.py:588
  402.1 36.5 %collective-permute-start.28 = (bf16[128,6528]{1,0:T(8,128)(2,1)}, bf16[128,6528]{1,0:T(8,128)(2,1)}, u32[]{:S(2)}, u32[]{:S(2)}) collective-permute-start(bf16[128,6528]{1,0:T(8,128)(2,1)} %collective-permute-done.24.refs_6_), channel_id=1, source_target_pairs={{0,1},{1,0},{2,3},{3,2},{4,5},{5,4},{6,7},{7,6},{8,9},{9,8},{10,11... | collective-permute-start | bytes 5013512 | tf_op jit(solution)/shard_map/ppermute | solution.py:588
  454.7 17.5 %collective-permute-start.38 = (bf16[192,1536]{1,0:T(8,128)(2,1)}, bf16[192,1536]{1,0:T(8,128)(2,1)}, u32[]{:S(2)}, u32[]{:S(2)}) collective-permute-start(bf16[192,1536]{1,0:T(8,128)(2,1)} %reduce-scatter.2.cloned.1.call-done.first_ref), channel_id=1, source_target_pairs={{0,4},{4,8},{8,12},{1,5},{5,9},{9,13},{2,6},{6,10},{10,14},{3,7},{... | collective-permute-start | bytes 1769480 | tf_op jit(solution)/shard_map/ppermute | solution.py:688
  459.0 17.5 %collective-permute-start.39 = (bf16[192,1536]{1,0:T(8,128)(2,1)}, bf16[192,1536]{1,0:T(8,128)(2,1)}, u32[]{:S(2)}, u32[]{:S(2)}) collective-permute-start(bf16[192,1536]{1,0:T(8,128)(2,1)} %reduce-scatter.2.cloned.1.call-done.first_ref), channel_id=1, source_target_pairs={{12,8},{8,4},{4,0},{13,9},{9,5},{5,1},{14,10},{10,6},{6,2},{15,11}... | collective-permute-start | bytes 1769480 | tf_op jit(solution)/shard_map/ppermute | solution.py:689
  462.7 22.3 %collective-permute-start.30 = (bf16[48,6528]{1,0:T(8,128)(2,1)}, bf16[48,6528]{1,0:T(8,128)(2,1)}, u32[]{:S(2)}, u32[]{:S(2)}) collective-permute-start(bf16[48,6528]{1,0:T(8,128)(2,1)} %get-tuple-element.211), channel_id=1, source_target_pairs={{0,4},{1,5},{2,6},{3,7},{16,20},{17,21},{18,22},{19,23}} | collective-permute-start | bytes 1880072 | tf_op jit(solution)/shard_map/ppermute | solution.py:688
  478.0 18.2 %collective-permute-start.41 = (bf16[192,1536]{1,0:T(8,128)(2,1)}, bf16[192,1536]{1,0:T(8,128)(2,1)}, u32[]{:S(2)}, u32[]{:S(2)}) collective-permute-start(bf16[192,1536]{1,0:T(8,128)(2,1)} %collective-permute-done.39.refs_5_), channel_id=1, source_target_pairs={{8,4},{4,0},{9,5},{5,1},{10,6},{6,2},{11,7},{7,3},{24,20},{20,16},... | collective-permute-start | bytes 1769480 | tf_op jit(solution)/shard_map/ppermute | solution.py:689
  499.2 21.8 %collective-permute-start.42 = (bf16[48,6528]{1,0:T(8,128)(2,1)}, bf16[48,6528]{1,0:T(8,128)(2,1)}, u32[]{:S(2)}, u32[]{:S(2)}) collective-permute-start(bf16[48,6528]{1,0:T(8,128)(2,1)} %get-tuple-element.209), channel_id=1, source_target_pairs={{0,4},{4,8},{1,5},{5,9},{2,6},{6,10},{3,7},{7,11},{16,20},{20,24},... | collective-permute-start | bytes 1880072 | tf_op jit(solution)/shard_map/ppermute | solution.py:688
  647.3 21.7 %collective-permute-start.60 = (bf16[48,6528]{1,0:T(8,128)(2,1)}, bf16[48,6528]{1,0:T(8,128)(2,1)}, u32[]{:S(2)}, u32[]{:S(2)}) collective-permute-start(bf16[48,6528]{1,0:T(8,128)(2,1)} %collective-permute-done.58.refs_2_), channel_id=1, source_target_pairs={{8,12},{9,13},{10,14},{11,15},{24,28},{25,29},{26,30},{27,31}} | collective-permute-start | bytes 1880072 | tf_op jit(solution)/shard_map/ppermute | solution.py:688
  648.8 20.2 %collective-permute-start.61 = (bf16[48,6528]{1,0:T(8,128)(2,1)}, bf16[48,6528]{1,0:T(8,128)(2,1)}, u32[]{:S(2)}, u32[]{:S(2)}) collective-permute-start(bf16[48,6528]{1,0:T(8,128)(2,1)} %collective-permute-done.59.refs_3_), channel_id=1, source_target_pairs={{4,0},{5,1},{6,2},{7,3},{20,16},{21,17},{22,18},{23,19}} | collective-permute-start | bytes 1880072 | tf_op jit(solution)/shard_map/ppermute | solution.py:689
  (196 other events, 1810.1 us)
Sparse Core Ops, SparseCore 0:
  36.0 52.1 all-gather.2
  89.8 28.8 all-gather.4
  363.3 51.0 reduce-scatter.1

commit v4 on v3

--- a/solution.py
+++ b/solution.py
@@ -320,7 +320,7 @@
             jax.ShapeDtypeStruct((row_count, inner), jnp.float32),
         ],
         scratch_shapes=scratch(length, heads) + [pltpu.VMEM((length, inner), jnp.float32)],
-        compiler_params=pltpu.CompilerParams(vmem_limit_bytes=40 * 1024 * 1024),
+        compiler_params=pltpu.CompilerParams(vmem_limit_bytes=24 * 1024 * 1024),
         cost_estimate=pl.CostEstimate(
             flops=row_count * inner * 600, bytes_accessed=row_count * (cols * 4 + inner * 6),
             transcendentals=row_count * (heads * length + 2 * cols),
@@ -360,7 +360,7 @@
             jax.ShapeDtypeStruct((8, LANES), jnp.float32),
         ],
         scratch_shapes=scratch(length, heads) + [pltpu.VMEM((length, chans), jnp.float32)],
-        compiler_params=pltpu.CompilerParams(vmem_limit_bytes=48 * 1024 * 1024),
+        compiler_params=pltpu.CompilerParams(vmem_limit_bytes=28 * 1024 * 1024),
         cost_estimate=pl.CostEstimate(
             flops=row_count * inner * 1500, bytes_accessed=row_count * (cols * 6 + inner * 8),
             transcendentals=row_count * (heads * length + 3 * cols),
@@ -395,7 +395,7 @@
         + [pl.BlockSpec((length, tile), lambda t: (0, t)) for _ in rights],
         out_specs=pl.BlockSpec((count, tile), lambda t: (0, t)),
         out_shape=jax.ShapeDtypeStruct((count, columns), jnp.bfloat16),
-        compiler_params=pltpu.CompilerParams(vmem_limit_bytes=48 * 1024 * 1024),
+        compiler_params=pltpu.CompilerParams(vmem_limit_bytes=28 * 1024 * 1024),
         cost_estimate=pl.CostEstimate(
             flops=2 * count * columns * length * len(rights),
             bytes_accessed=2 * columns * (length * len(rights) + count),
@@ -469,7 +469,7 @@
         ),
         out_shape=[shape]
         + [jax.ShapeDtypeStruct((row_count, columns), jnp.bfloat16) for _ in extra],
-        compiler_params=pltpu.CompilerParams(vmem_limit_bytes=32 * 1024 * 1024),
+        compiler_params=pltpu.CompilerParams(vmem_limit_bytes=20 * 1024 * 1024),
         cost_estimate=pl.CostEstimate(
             flops=2 * row_count * depth * columns,
             bytes_accessed=2 * depth * columns + 4 * row_count * columns,
@@ -523,7 +523,7 @@
             scratch_shapes=[pltpu.VMEM((row_count, depth), jnp.float32)],
         ),
         out_shape=jax.ShapeDtypeStruct((row_count, depth), jnp.float32),
-        compiler_params=pltpu.CompilerParams(vmem_limit_bytes=32 * 1024 * 1024),
+        compiler_params=pltpu.CompilerParams(vmem_limit_bytes=20 * 1024 * 1024),
         cost_estimate=pl.CostEstimate(
             flops=2 * row_count * depth * columns,
             bytes_accessed=2 * depth * columns + 4 * row_count * depth,
@@ -568,7 +568,7 @@
         ),
         out_shape=[jax.ShapeDtypeStruct((total * chunks, w), jnp.float32) for w in widths],
         input_output_aliases={1 + len(inputs) + i: i for i in range(len(prior))},
-        compiler_params=pltpu.CompilerParams(vmem_limit_bytes=40 * 1024 * 1024),
+        compiler_params=pltpu.CompilerParams(vmem_limit_bytes=30 * 1024 * 1024),
     )(order, *inputs, *prior)
 
 
@@ -617,7 +617,7 @@
             out_specs=[pl.BlockSpec(shape, lambda t, owner: (0, 0)) for _ in range(size)],
         ),
         out_shape=[jax.ShapeDtypeStruct(shape, jnp.bfloat16) for _ in range(size)],
-        compiler_params=pltpu.CompilerParams(vmem_limit_bytes=24 * 1024 * 1024),
+        compiler_params=pltpu.CompilerParams(vmem_limit_bytes=16 * 1024 * 1024),
     )(owners, *sources)
 
 
@@ -717,12 +717,15 @@
         arrived.append([routed(part, FSDP, hop, 0) for hop in hops])
     narrows = [narrow] + [routed(narrow, FSDP, hop, 0) for hop in range(1, chips)]
     narrows += [routed(block, FSDP, 0, 1) for block in narrows]
-    arrived, owns, narrows, prepared = lax.optimization_barrier((arrived, owns, narrows, prepared))
+    fronts = [own[:direct] for own, direct in zip(owns, directs)]
+    arrived, owns, fronts, narrows, prepared = lax.optimization_barrier(
+        (arrived, owns, fronts, narrows, prepared)
+    )
     full = []
     for i, own in enumerate(owns):
         same = [own]
         for hop in range(1, chips):
-            same.append(routed(own[: directs[i]], FSDP, hop, 0))
+            same.append(routed(fronts[i], FSDP, hop, 0))
             if stripes[i]:
                 same.append(
                     lax.all_gather(arrived[i][hop - 1], DP, axis=0, tiled=True)

time: 695 us -> 677 us (0.974)
  Pallas kernels: 208 us -> 198 us
    unnamed x327 -> x283, local copies, waits for them, and re-layouts: 41.8 us -> 36.1 us
  transfers between devices with their start and end apart: 65 -> 65, of which waited for: 28 -> 29; matrix products, arithmetic and copies ran while one was open for 5% -> 6% of each run, Pallas kernels for 20% -> 20%
where the time goes in v4:
time: 677 us; the launch traced here: 664 us
  waiting for transfers between devices  265 us (39%)
  Pallas kernels  198 us (29%)
  starting transfers between devices  83.6 us (12%)
  local copies, waits for them, and re-layouts  55.2 us (8%)
  other arithmetic  31.8 us (5%)
  between operations  24 us (4%)
    ppermute x28, waiting for transfers between devices, routed(): lax.ppermute(block, axis, [(i, target(i, hop, flip, size)) for i in range...  175 us
    pallas_call x6, Pallas kernels, backward_product(): pl.pallas_call(functools.partial(backward_product_kernel, rows, len(piece...  49.9 us
    pallas_call x3, Pallas kernels, mixer_backward(): pl.pallas_call(functools.partial(mixer_backward_kernel, inner, heads), gr...  48 us
    ppermute x11, waiting for transfers between devices, line_pipeline(): down = lax.ppermute(job[3], axis, downs)  46.3 us
    pallas_call x6, Pallas kernels, forward_product(): pl.pallas_call(functools.partial(forward_product_kernel, rows, len(pieces...  39.7 us
    unnamed x283, local copies, waits for them, and re-layouts  36.1 us
    ppermute x11, starting transfers between devices, line_pipeline(): up = lax.ppermute(job[2], axis, ups)  30.2 us
    pallas_call x3, Pallas kernels, mixer_forward(): pl.pallas_call(functools.partial(mixer_forward_kernel, inner, heads, tran...  28 us
  transfers between devices with their start and end apart: 65, of which 29 were waited for; matrix products, arithmetic and copies ran while one was open for 6% of the time, Pallas kernels for 20%

profile of v4, /device:TPU:0, one launch (start us, length us, event | category | flops | bytes accessed | tf_op | source)
XLA Modules:
  0.0 663.7 jit_solution(14091704222565118622)
XLA Ops:
  25.2 9.9 %collective-permute-done.1 = bf16[96,1536]{1,0:T(8,128)(2,1)S(1)} collective-permute-done((bf16[96,1536]{1,0:T(8,128)(2,1)}, bf16[96,1536]{1,0:T(8,128)(2,1)S(1)}, u32[]{:S(2)}, u32[]{:S(2)}) %collective-permute-start.1) | collective-permute-done | bytes 294944 | tf_op jit(solution)/shard_map/ppermute | solution.py:588
  35.9 55.4 %collective-permute-done.5.refs_1_ = bf16[192,6400]{1,0:T(8,128)(2,1)} collective-permute-done((bf16[192,6400]{1,0:T(8,128)(2,1)}, bf16[192,6400]{1,0:T(8,128)(2,1)}, u32[]{:S(2)}, u32[]{:S(2)}) %collective-permute-start.5) | collective-permute-done | bytes 2457632 | tf_op jit(solution)/shard_map/ppermute | solution.py:588
  92.1 27.9 %collective-permute-done.9.refs_1_ = bf16[384,1536]{1,0:T(8,128)(2,1)S(1)} collective-permute-done((bf16[384,1536]{1,0:T(8,128)(2,1)}, bf16[384,1536]{1,0:T(8,128)(2,1)S(1)}, u32[]{:S(2)}, u32[]{:S(2)}) %collective-permute-start.9) | collective-permute-done | bytes 1179680 | tf_op jit(solution)/shard_map/ppermute | solution.py:588
  137.4 7.9 %shard_map.220.proj_ref = f32[128,6400]{1,0:T(8,128)S(1)} custom-call(s32[4]{0:T(128)S(1)} %get-tuple-element.94.order_ref, bf16[128,1536]{1,0:T(8,128)(2,1)S(1)} %copy-done.52, bf16[384,6400]{1,0:T(8,128)(2,1)S(1)} %bitcast.154, bf16[192,6400]{1,0:T(8,128)(2,1)} %collective-permute-done.5.refs_1_, bf16[192,6400]{1,0:T(8,128)(2,1)S(1)} %copy-done.2, ...), custom_call_target="tpu_custom_call" | custom-call | flops 2516582400 | bytes 22937600 | tf_op jit(solution)/shard_map/pallas_call | solution.py:459
  145.4 8.7 %shard_map.221 = (bf16[128,3072]{1,0:T(8,128)(2,1)S(1)}, bf16[128,128]{1,0:T(8,128)(2,1)}, f32[128,3072]{1,0:T(8,128)}) custom-call(f32[128,6400]{1,0:T(8,128)S(1)} %shard_map.220.proj_ref, f32[128,128]{1,0:T(8,128)S(1)} %fusion.48.dt_ref, f32[4,3328]{1,0:T(4,128)S(1)} %bitcast.180, f32[1,3328]{1,0:T(1,128)S(1)} %copy-done.69, f32[1,128]{1,0:T(1,128)S(1)} %copy-done.94, ...), custom_call_target="tpu_custom_call" | custom-call | flops 235929600 | bytes 5636096 | tf_op jit(solution)/shard_map/pallas_call | solution.py:307
  167.9 6.3 shard_map.229.gm_ref
  177.5 7.9 %shard_map.223.proj_ref = f32[128,6400]{1,0:T(8,128)S(1)} custom-call(s32[4]{0:T(128)S(1)} %get-tuple-element.94.order_ref, bf16[128,1536]{1,0:T(8,128)(2,1)S(1)} %multiply_convert_fusion.1.left_ref, bf16[384,6400]{1,0:T(8,128)(2,1)S(1)} %bitcast.157, bf16[192,6400]{1,0:T(8,128)(2,1)} %collective-permute-done.5.refs_1_, bf16[192,6400]{1,0:T(8,128)(2,1)S(1)} %copy-done.3, ...), custom_call_target="tpu_custom_call" | custom-call | flops 2516582400 | bytes 22937600 | tf_op jit(solution)/shard_map/pallas_call | solution.py:459
  185.5 9.7 %shard_map.224 = (bf16[128,3072]{1,0:T(8,128)(2,1)S(1)}, bf16[3072,128]{1,0:T(8,128)(2,1)S(1)}, f32[128,3072]{1,0:T(8,128)S(1)}) custom-call(f32[128,6400]{1,0:T(8,128)S(1)} %shard_map.223.proj_ref, f32[128,128]{1,0:T(8,128)S(1)} %fusion.46.dt_ref, f32[4,3328]{1,0:T(4,128)S(1)} %bitcast.181, f32[1,3328]{1,0:T(1,128)S(1)} %copy-done.70, ...), custom_call_target="tpu_custom_call" | custom-call | flops 235929600 | bytes 5636096 | tf_op jit(solution)/shard_map/pallas_call | solution.py:307
  204.0 15.6 %shard_map.230 = (bf16[128,6528]{1,0:T(8,128)(2,1)S(1)}, f32[4,3328]{1,0:T(4,128)}, f32[1,3328]{1,0:T(1,128)}, f32[1,3072]{1,0:T(1,128)}, f32[1,3072]{1,0:T(1,128)}, /*index=5*/f32[8,128]{1,0:T(8,128)}) custom-call(f32[128,6400]{1,0:T(8,128)S(1)} %shard_map.223.proj_ref, f32[128,128]{1,0:T(8,128)S(1)} %fusion.46.dt_ref, ...), custom_call_target="tpu_custom_call" | custom-call | flops 589824000 | bytes 8060928 | tf_op jit(solution)/shard_map/pallas_call | solution.py:336
  219.6 10.3 %shard_map.231 = f32[128,1536]{1,0:T(8,128)S(1)} custom-call(s32[4]{0:T(128)S(1)} %get-tuple-element.94.order_ref, bf16[128,6528]{1,0:T(8,128)(2,1)S(1)} %get-tuple-element.121.left_ref, bf16[384,6400]{1,0:T(8,128)(2,1)S(1)} %bitcast.158, bf16[192,6400]{1,0:T(8,128)(2,1)} %collective-permute-done.5.refs_1_, bf16[192,6400]{1,0:T(8,128)(2,1)S(1)} %copy-done.3, ...), custom_call_target="tpu_custom_call" | custom-call | flops 2516582400 | bytes 20447232 | tf_op jit(solution)/shard_map/pallas_call | solution.py:515
  233.6 7.9 %shard_map.226.proj_ref = f32[128,6400]{1,0:T(8,128)S(1)} custom-call(s32[4]{0:T(128)S(1)} %get-tuple-element.94.order_ref, bf16[128,1536]{1,0:T(8,128)(2,1)S(1)} %get-tuple-element.226.left_ref, bf16[384,6400]{1,0:T(8,128)(2,1)S(1)} %bitcast.159, bf16[192,6400]{1,0:T(8,128)(2,1)} %collective-permute-done.5.refs_1_, bf16[192,6400]{1,0:T(8,128)(2,1)S(1)} %copy-done.3, ...), custom_call_target="tpu_custom_call" | custom-call | flops 2516582400 | bytes 22937600 | tf_op jit(solution)/shard_map/pallas_call | solution.py:459
  241.6 9.7 %shard_map.227 = (bf16[128,3072]{1,0:T(8,128)(2,1)S(1)}, bf16[3072,128]{1,0:T(8,128)(2,1)S(1)}, f32[128,3072]{1,0:T(8,128)S(1)}) custom-call(f32[128,6400]{1,0:T(8,128)S(1)} %shard_map.226.proj_ref, f32[128,128]{1,0:T(8,128)S(1)} %fusion.44.dt_ref, f32[4,3328]{1,0:T(4,128)S(1)} %bitcast.183, f32[1,3328]{1,0:T(1,128)S(1)} %copy-done.70, ...), custom_call_target="tpu_custom_call" | custom-call | flops 235929600 | bytes 5636096 | tf_op jit(solution)/shard_map/pallas_call | solution.py:307
  251.5 6.2 shard_map.232.gm_ref
  257.7 16.2 %shard_map.233 = (bf16[128,6528]{1,0:T(8,128)(2,1)}, f32[4,3328]{1,0:T(4,128)S(1)}, f32[1,3328]{1,0:T(1,128)S(1)}, f32[1,3072]{1,0:T(1,128)S(1)}, f32[1,3072]{1,0:T(1,128)S(1)}, /*index=5*/f32[8,128]{1,0:T(8,128)S(1)}) custom-call(f32[128,6400]{1,0:T(8,128)S(1)} %shard_map.226.proj_ref, f32[128,128]{1,0:T(8,128)S(1)} %fusion.44.dt_ref, ...), custom_call_target="tpu_custom_call" | custom-call | flops 589824000 | bytes 8060928 | tf_op jit(solution)/shard_map/pallas_call | solution.py:336
  273.9 10.3 %shard_map.234 = f32[128,1536]{1,0:T(8,128)S(1)} custom-call(s32[4]{0:T(128)S(1)} %get-tuple-element.94.order_ref, bf16[128,6528]{1,0:T(8,128)(2,1)} %get-tuple-element.123.left_ref.refs_4_, bf16[384,6400]{1,0:T(8,128)(2,1)S(1)} %bitcast.160, bf16[192,6400]{1,0:T(8,128)(2,1)} %collective-permute-done.5.refs_1_, bf16[192,6400]{1,0:T(8,128)(2,1)S(1)} %copy-done.3, ...), custom_call_target="tpu_custom_call" | custom-call | flops 2516582400 | bytes 20447232 | tf_op jit(solution)/shard_map/pallas_call | solution.py:515
  301.5 11.1 %collective-permute-done.21.refs_1_ = bf16[1152,256]{1,0:T(8,128)(2,1)S(1)} collective-permute-done((bf16[1152,256]{1,0:T(8,128)(2,1)S(1)}, bf16[1152,256]{1,0:T(8,128)(2,1)S(1)}, u32[]{:S(2)}, u32[]{:S(2)}) %collective-permute-start.21) | collective-permute-done | bytes 589856 | tf_op jit(solution)/shard_map/ppermute | solution.py:588
  313.1 7.9 %collective-permute-done.32.refs_6_ = bf16[128,1536]{1,0:T(8,128)(2,1)S(1)} collective-permute-done((bf16[128,1536]{1,0:T(8,128)(2,1)S(1)}, bf16[128,1536]{1,0:T(8,128)(2,1)S(1)}, u32[]{:S(2)}, u32[]{:S(2)}) %collective-permute-start.32) | collective-permute-done | bytes 393248 | tf_op jit(solution)/shard_map/ppermute | solution.py:588
  321.0 8.4 %collective-permute-done.33.refs_7_ = bf16[128,1536]{1,0:T(8,128)(2,1)S(1)} collective-permute-done((bf16[128,1536]{1,0:T(8,128)(2,1)S(1)}, bf16[128,1536]{1,0:T(8,128)(2,1)S(1)}, u32[]{:S(2)}, u32[]{:S(2)}) %collective-permute-start.33) | collective-permute-done | bytes 393248 | tf_op jit(solution)/shard_map/ppermute | solution.py:588
  329.5 8.7 %collective-permute-done.23.refs_3_ = bf16[1152,256]{1,0:T(8,128)(2,1)S(1)} collective-permute-done((bf16[1152,256]{1,0:T(8,128)(2,1)S(1)}, bf16[1152,256]{1,0:T(8,128)(2,1)S(1)}, u32[]{:S(2)}, u32[]{:S(2)}) %collective-permute-start.23) | collective-permute-done | bytes 589856 | tf_op jit(solution)/shard_map/ppermute | solution.py:588
  350.0 6.5 shard_map.235.gm_ref
  356.7 16.2 %shard_map.236 = (bf16[128,6528]{1,0:T(8,128)(2,1)}, f32[4,3328]{1,0:T(4,128)S(1)}, f32[1,3328]{1,0:T(1,128)S(1)}, f32[1,3072]{1,0:T(1,128)S(1)}, f32[1,3072]{1,0:T(1,128)S(1)}, /*index=5*/f32[8,128]{1,0:T(8,128)S(1)}) custom-call(f32[128,6400]{1,0:T(8,128)S(1)} %copy-done.15, f32[128,128]{1,0:T(8,128)S(1)} %copy-done.68, f32[128,3072]{1,0:T(8,128)S(1)} %copy-done.26, ...), custom_call_target="tpu_custom_call" | custom-call | flops 589824000 | bytes 8060928 | tf_op jit(solution)/shard_map/pallas_call | solution.py:336
  377.6 7.5 %collective-permute-done.24.refs_6_ = bf16[128,6528]{1,0:T(8,128)(2,1)} collective-permute-done((bf16[128,6528]{1,0:T(8,128)(2,1)}, bf16[128,6528]{1,0:T(8,128)(2,1)}, u32[]{:S(2)}, u32[]{:S(2)}) %collective-permute-start.24) | collective-permute-done | bytes 1671200 | tf_op jit(solution)/shard_map/ppermute | solution.py:588
  386.8 34.1 %collective-permute-done.25.refs_7_ = bf16[128,6528]{1,0:T(8,128)(2,1)} collective-permute-done((bf16[128,6528]{1,0:T(8,128)(2,1)}, bf16[128,6528]{1,0:T(8,128)(2,1)}, u32[]{:S(2)}, u32[]{:S(2)}) %collective-permute-start.25) | collective-permute-done | bytes 1671200 | tf_op jit(solution)/shard_map/ppermute | solution.py:588
  429.3 6.8 %shard_map.240 = bf16[192,6528]{1,0:T(8,128)(2,1)S(1)} custom-call(bf16[1152,256]{1,0:T(8,128)(2,1)S(1)} %copy-done.35, bf16[1152,256]{1,0:T(8,128)(2,1)S(1)} %copy-done.38, bf16[1152,256]{1,0:T(8,128)(2,1)S(1)} %copy-done.41, bf16[1152,256]{1,0:T(8,128)(2,1)S(1)} %copy-done.44, bf16[128,6528]{1,0:T(8,128)(2,1)} %get-tuple-element.123.left_ref.refs_4_, ...), custom_call_target="tpu_custom_call" | custom-call | flops 2566914048 | bytes 15876096 | tf_op jit(solution)/shard_map/pallas_call | solution.py:391
  462.2 5.7 collective-permute-done.30
  467.9 11.2 %collective-permute-done.41.refs_3_ = bf16[192,1536]{1,0:T(8,128)(2,1)} collective-permute-done((bf16[192,1536]{1,0:T(8,128)(2,1)}, bf16[192,1536]{1,0:T(8,128)(2,1)}, u32[]{:S(2)}, u32[]{:S(2)}) %collective-permute-start.41) | collective-permute-done | bytes 589856 | tf_op jit(solution)/shard_map/ppermute | solution.py:689
  490.9 13.1 %collective-permute-done.45.refs_1_ = bf16[192,1536]{1,0:T(8,128)(2,1)} collective-permute-done((bf16[192,1536]{1,0:T(8,128)(2,1)}, bf16[192,1536]{1,0:T(8,128)(2,1)}, u32[]{:S(2)}, u32[]{:S(2)}) %collective-permute-start.45) | collective-permute-done | bytes 589856 | tf_op jit(solution)/shard_map/ppermute | solution.py:689
  510.5 7.9 %collective-permute-done.46 = bf16[48,6528]{1,0:T(8,128)(2,1)} collective-permute-done((bf16[48,6528]{1,0:T(8,128)(2,1)}, bf16[48,6528]{1,0:T(8,128)(2,1)}, u32[]{:S(2)}, u32[]{:S(2)}) %collective-permute-start.46) | collective-permute-done | bytes 626720 | tf_op jit(solution)/shard_map/ppermute | solution.py:688
  534.1 6.8 %shard_map.239 = bf16[192,6528]{1,0:T(8,128)(2,1)S(1)} custom-call(bf16[1152,256]{1,0:T(8,128)(2,1)S(1)} %copy-done.36, bf16[1152,256]{1,0:T(8,128)(2,1)S(1)} %copy-done.39, bf16[1152,256]{1,0:T(8,128)(2,1)S(1)} %copy-done.42, bf16[1152,256]{1,0:T(8,128)(2,1)S(1)} %copy-done.45, bf16[128,6528]{1,0:T(8,128)(2,1)} %get-tuple-element.123.left_ref.refs_4_, ...), custom_call_target="tpu_custom_call" | custom-call | flops 2566914048 | bytes 15876096 | tf_op jit(solution)/shard_map/pallas_call | solution.py:391
  551.0 6.3 collective-permute-done.50.refs_2_
  585.0 10.2 %shard_map.237 = f32[128,1536]{1,0:T(8,128)S(1)} custom-call(s32[4]{0:T(128)S(1)} %get-tuple-element.94.order_ref, bf16[128,6528]{1,0:T(8,128)(2,1)} %get-tuple-element.124.left_ref.refs_5_, bf16[384,6400]{1,0:T(8,128)(2,1)S(1)} %bitcast.163, bf16[192,6400]{1,0:T(8,128)(2,1)} %collective-permute-done.5.refs_1_, bf16[192,6400]{1,0:T(8,128)(2,1)S(1)} %copy-done.4, ...), custom_call_target="tpu_custom_call" | custom-call | flops 2516582400 | bytes 20447232 | tf_op jit(solution)/shard_map/pallas_call | solution.py:515
  622.7 7.6 %collective-permute-done.59.refs_3_ = bf16[48,6528]{1,0:T(8,128)(2,1)} collective-permute-done((bf16[48,6528]{1,0:T(8,128)(2,1)}, bf16[48,6528]{1,0:T(8,128)(2,1)}, u32[]{:S(2)}, u32[]{:S(2)}) %collective-permute-start.59) | collective-permute-done | bytes 626720 | tf_op jit(solution)/shard_map/ppermute | solution.py:689
  (490 shorter events, 253.7 us)
Async XLA Ops:
  7.2 84.1 %all-gather.3.cloned.1.call-start = ((), (), s32[]{:S(2)}) async-start(), calls=%async_computation.1 | async-start | bytes 3072000 | tf_op jit(solution)/shard_map/all_gather | solution.py:731
  12.2 22.8 %collective-permute-start = (bf16[48,6400]{1,0:T(8,128)(2,1)}, bf16[48,6400]{1,0:T(8,128)(2,1)}, u32[]{:S(2)}, u32[]{:S(2)}) collective-permute-start(bf16[48,6400]{1,0:T(8,128)(2,1)} %dynamic-slice_bitcast_fusion.2), channel_id=1, source_target_pairs={{0,2},{1,3},{2,0},{3,1},{4,6},{5,7},{6,4},{7,5},{8,10},{9,11},{10,... | collective-permute-start | bytes 1843208 | tf_op jit(solution)/shard_map/ppermute | solution.py:588
  14.0 21.0 %collective-permute-start.1 = (bf16[96,1536]{1,0:T(8,128)(2,1)}, bf16[96,1536]{1,0:T(8,128)(2,1)S(1)}, u32[]{:S(2)}, u32[]{:S(2)}) collective-permute-start(bf16[96,1536]{1,0:T(8,128)(2,1)} %dynamic-slice_bitcast_fusion.3), channel_id=1, source_target_pairs={{0,2},{1,3},{2,0},{3,1},{4,6},{5,7},{6,4},{7,5},{8,10},{9,11},{10,... | collective-permute-start | bytes 884744 | tf_op jit(solution)/shard_map/ppermute | solution.py:588
  35.1 85.0 %all-gather.5.cloned.1.call-start = ((), (), s32[]{:S(2)}) async-start(), calls=%async_computation.2 | async-start | bytes 1474560 | tf_op jit(solution)/shard_map/all_gather | solution.py:731
  35.1 84.9 %collective-permute-start.6 = (bf16[384,6400]{1,0:T(8,128)(2,1)}, bf16[384,6400]{1,0:T(8,128)(2,1)}, u32[]{:S(2)}, u32[]{:S(2)}) collective-permute-start(bf16[384,6400]{1,0:T(8,128)(2,1)} %bitcast.153), channel_id=1, source_target_pairs={{0,1},{1,0},{2,3},{3,2},{4,5},{5,4},{6,7},{7,6},{8,9},{9,8},{10,11... | collective-permute-start | bytes 14745608 | tf_op jit(solution)/shard_map/ppermute | solution.py:588
  35.2 56.1 %collective-permute-start.5 = (bf16[192,6400]{1,0:T(8,128)(2,1)}, bf16[192,6400]{1,0:T(8,128)(2,1)}, u32[]{:S(2)}, u32[]{:S(2)}) collective-permute-start(bf16[192,6400]{1,0:T(8,128)(2,1)} %slice_bitcast_fusion), channel_id=1, source_target_pairs={{0,2},{1,3},{2,0},{3,1},{4,6},{5,7},{6,4},{7,5},{8,10},{9,11},{10,... | collective-permute-start | bytes 7372808 | tf_op jit(solution)/shard_map/ppermute | solution.py:588
  35.8 401.8 %reduce-scatter.2.cloned.1.call-start = ((), (), s32[]{:S(2)}) async-start(), calls=%async_computation.3 | async-start | bytes 2949120 | tf_op jit(solution)/shard_map/reduce_scatter | solution.py:870
  91.3 43.4 %collective-permute-start.7 = (bf16[192,6400]{1,0:T(8,128)(2,1)}, bf16[192,6400]{1,0:T(8,128)(2,1)}, u32[]{:S(2)}, u32[]{:S(2)}) collective-permute-start(bf16[192,6400]{1,0:T(8,128)(2,1)} %collective-permute-done.5.refs_1_), channel_id=1, source_target_pairs={{0,1},{1,0},{2,3},{3,2},{4,5},{5,4},{6,7},{7,6},{8,9},{9,8},{10,11... | collective-permute-start | bytes 7372808 | tf_op jit(solution)/shard_map/ppermute | solution.py:588
  91.3 43.3 %collective-permute-start.8 = (bf16[192,6400]{1,0:T(8,128)(2,1)}, bf16[192,6400]{1,0:T(8,128)(2,1)}, u32[]{:S(2)}, u32[]{:S(2)}) collective-permute-start(bf16[192,6400]{1,0:T(8,128)(2,1)} %all-gather.3.cloned.1.call-done.refs_2_), channel_id=1, source_target_pairs={{0,1},{1,0},{2,3},{3,2},{4,5},{5,4},{6,7},{7,6},{8,9},{9,8},{10,11... | collective-permute-start | bytes 7372808 | tf_op jit(solution)/shard_map/ppermute | solution.py:588
  91.8 28.2 %collective-permute-start.9 = (bf16[384,1536]{1,0:T(8,128)(2,1)}, bf16[384,1536]{1,0:T(8,128)(2,1)S(1)}, u32[]{:S(2)}, u32[]{:S(2)}) collective-permute-start(bf16[384,1536]{1,0:T(8,128)(2,1)} %slice_bitcast_fusion.1), channel_id=1, source_target_pairs={{0,2},{1,3},{2,0},{3,1},{4,6},{5,7},{6,4},{7,5},{8,10},{9,11},{10,... | collective-permute-start | bytes 3538952 | tf_op jit(solution)/shard_map/ppermute | solution.py:588
  92.1 61.9 %collective-permute-start.10 = (bf16[768,1536]{1,0:T(8,128)(2,1)S(1)}, bf16[768,1536]{1,0:T(8,128)(2,1)}, u32[]{:S(2)}, u32[]{:S(2)}) collective-permute-start(bf16[768,1536]{1,0:T(8,128)(2,1)S(1)} %bitcast.164), channel_id=1, source_target_pairs={{0,1},{1,0},{2,3},{3,2},{4,5},{5,4},{6,7},{7,6},{8,9},{9,8},{10,11... | collective-permute-start | bytes 7077896 | tf_op jit(solution)/shard_map/ppermute | solution.py:588
  120.0 34.1 %collective-permute-start.11 = (bf16[384,1536]{1,0:T(8,128)(2,1)S(1)}, bf16[384,1536]{1,0:T(8,128)(2,1)}, u32[]{:S(2)}, u32[]{:S(2)}) collective-permute-start(bf16[384,1536]{1,0:T(8,128)(2,1)S(1)} %collective-permute-done.9.refs_1_), channel_id=1, source_target_pairs={{0,1},{1,0},{2,3},{3,2},{4,5},{5,4},{6,7},{7,6},{8,9},{9,8},{10,11... | collective-permute-start | bytes 3538952 | tf_op jit(solution)/shard_map/ppermute | solution.py:588
  120.0 34.1 %collective-permute-start.12 = (bf16[384,1536]{1,0:T(8,128)(2,1)}, bf16[384,1536]{1,0:T(8,128)(2,1)}, u32[]{:S(2)}, u32[]{:S(2)}) collective-permute-start(bf16[384,1536]{1,0:T(8,128)(2,1)} %all-gather.5.cloned.1.call-done.refs_2_), channel_id=1, source_target_pairs={{0,1},{1,0},{2,3},{3,2},{4,5},{5,4},{6,7},{7,6},{8,9},{9,8},{10,11... | collective-permute-start | bytes 3538952 | tf_op jit(solution)/shard_map/ppermute | solution.py:588
  201.8 29.0 %collective-permute-start.14 = (bf16[128,1536]{1,0:T(8,128)(2,1)S(1)}, bf16[128,1536]{1,0:T(8,128)(2,1)S(1)}, u32[]{:S(2)}, u32[]{:S(2)}) collective-permute-start(bf16[128,1536]{1,0:T(8,128)(2,1)S(1)} %get-tuple-element.116), channel_id=1, source_target_pairs={{0,16},{1,17},{2,18},{3,19},{4,20},{5,21},{6,22},{7,23},{8,24},{9,... | collective-permute-start | bytes 1179656 | tf_op jit(solution)/shard_map/ppermute | solution.py:26
  232.1 19.2 %collective-permute-start.15 = (bf16[128,1536]{1,0:T(8,128)(2,1)S(1)}, bf16[128,1536]{1,0:T(8,128)(2,1)S(1)}, u32[]{:S(2)}, u32[]{:S(2)}) collective-permute-start(bf16[128,1536]{1,0:T(8,128)(2,1)S(1)} %get-tuple-element.225), channel_id=1, source_target_pairs={{16,0},{17,1},{18,2},{19,3},{20,4},{21,5},{22,6},{23,7},{24,8},{25... | collective-permute-start | bytes 1179656 | tf_op jit(solution)/shard_map/ppermute | solution.py:26
  296.9 24.1 %collective-permute-start.32 = (bf16[128,1536]{1,0:T(8,128)(2,1)S(1)}, bf16[128,1536]{1,0:T(8,128)(2,1)S(1)}, u32[]{:S(2)}, u32[]{:S(2)}) collective-permute-start(bf16[128,1536]{1,0:T(8,128)(2,1)S(1)} %copy-done.47), channel_id=1, source_target_pairs={{0,2},{1,3},{2,0},{3,1},{4,6},{5,7},{6,4},{7,5},{8,10},{9,11},{10,... | collective-permute-start | bytes 1179656 | tf_op jit(solution)/shard_map/ppermute | solution.py:588
  301.0 28.5 %collective-permute-start.33 = (bf16[128,1536]{1,0:T(8,128)(2,1)S(1)}, bf16[128,1536]{1,0:T(8,128)(2,1)S(1)}, u32[]{:S(2)}, u32[]{:S(2)}) collective-permute-start(bf16[128,1536]{1,0:T(8,128)(2,1)S(1)} %fusion.23.left_ref.refs_5_), channel_id=1, source_target_pairs={{0,2},{1,3},{2,0},{3,1},{4,6},{5,7},{6,4},{7,5},{8,10},{9,11},{10,... | collective-permute-start | bytes 1179656 | tf_op jit(solution)/shard_map/ppermute | solution.py:588
  301.5 36.6 %collective-permute-start.23 = (bf16[1152,256]{1,0:T(8,128)(2,1)S(1)}, bf16[1152,256]{1,0:T(8,128)(2,1)S(1)}, u32[]{:S(2)}, u32[]{:S(2)}) collective-permute-start(bf16[1152,256]{1,0:T(8,128)(2,1)S(1)} %get-tuple-element.141), channel_id=1, source_target_pairs={{0,3},{1,2},{2,1},{3,0},{4,7},{5,6},{6,5},{7,4},{8,11},{9,10},{10,... | collective-permute-start | bytes 1769480 | tf_op jit(solution)/shard_map/ppermute | solution.py:588
  312.6 25.6 %collective-permute-start.34 = (bf16[128,1536]{1,0:T(8,128)(2,1)S(1)}, bf16[128,1536]{1,0:T(8,128)(2,1)S(1)}, u32[]{:S(2)}, u32[]{:S(2)}) collective-permute-start(bf16[128,1536]{1,0:T(8,128)(2,1)S(1)} %copy-done.47), channel_id=1, source_target_pairs={{0,1},{1,0},{2,3},{3,2},{4,5},{5,4},{6,7},{7,6},{8,9},{9,8},{10,11... | collective-permute-start | bytes 1179656 | tf_op jit(solution)/shard_map/ppermute | solution.py:588
  312.6 25.6 %collective-permute-start.35 = (bf16[128,1536]{1,0:T(8,128)(2,1)S(1)}, bf16[128,1536]{1,0:T(8,128)(2,1)S(1)}, u32[]{:S(2)}, u32[]{:S(2)}) collective-permute-start(bf16[128,1536]{1,0:T(8,128)(2,1)S(1)} %fusion.23.left_ref.refs_5_), channel_id=1, source_target_pairs={{0,1},{1,0},{2,3},{3,2},{4,5},{5,4},{6,7},{7,6},{8,9},{9,8},{10,11... | collective-permute-start | bytes 1179656 | tf_op jit(solution)/shard_map/ppermute | solution.py:588
  346.1 39.0 %collective-permute-start.24 = (bf16[128,6528]{1,0:T(8,128)(2,1)}, bf16[128,6528]{1,0:T(8,128)(2,1)}, u32[]{:S(2)}, u32[]{:S(2)}) collective-permute-start(bf16[128,6528]{1,0:T(8,128)(2,1)} %get-tuple-element.123.left_ref.refs_4_), channel_id=1, source_target_pairs={{0,2},{1,3},{2,0},{3,1},{4,6},{5,7},{6,4},{7,5},{8,10},{9,11},{10,... | collective-permute-start | bytes 5013512 | tf_op jit(solution)/shard_map/ppermute | solution.py:588
  375.9 45.0 %collective-permute-start.25 = (bf16[128,6528]{1,0:T(8,128)(2,1)}, bf16[128,6528]{1,0:T(8,128)(2,1)}, u32[]{:S(2)}, u32[]{:S(2)}) collective-permute-start(bf16[128,6528]{1,0:T(8,128)(2,1)} %get-tuple-element.124.left_ref.refs_5_), channel_id=1, source_target_pairs={{0,2},{1,3},{2,0},{3,1},{4,6},{5,7},{6,4},{7,5},{8,10},{9,11},{10,... | collective-permute-start | bytes 5013512 | tf_op jit(solution)/shard_map/ppermute | solution.py:588
  377.0 44.5 %collective-permute-start.26 = (bf16[128,6528]{1,0:T(8,128)(2,1)}, bf16[128,6528]{1,0:T(8,128)(2,1)}, u32[]{:S(2)}, u32[]{:S(2)}) collective-permute-start(bf16[128,6528]{1,0:T(8,128)(2,1)} %get-tuple-element.123.left_ref.refs_4_), channel_id=1, source_target_pairs={{0,1},{1,0},{2,3},{3,2},{4,5},{5,4},{6,7},{7,6},{8,9},{9,8},{10,11... | collective-permute-start | bytes 5013512 | tf_op jit(solution)/shard_map/ppermute | solution.py:588
  377.6 43.9 %collective-permute-start.27 = (bf16[128,6528]{1,0:T(8,128)(2,1)}, bf16[128,6528]{1,0:T(8,128)(2,1)}, u32[]{:S(2)}, u32[]{:S(2)}) collective-permute-start(bf16[128,6528]{1,0:T(8,128)(2,1)} %get-tuple-element.124.left_ref.refs_5_), channel_id=1, source_target_pairs={{0,1},{1,0},{2,3},{3,2},{4,5},{5,4},{6,7},{7,6},{8,9},{9,8},{10,11... | collective-permute-start | bytes 5013512 | tf_op jit(solution)/shard_map/ppermute | solution.py:588
  385.1 36.4 %collective-permute-start.28 = (bf16[128,6528]{1,0:T(8,128)(2,1)}, bf16[128,6528]{1,0:T(8,128)(2,1)}, u32[]{:S(2)}, u32[]{:S(2)}) collective-permute-start(bf16[128,6528]{1,0:T(8,128)(2,1)} %collective-permute-done.24.refs_6_), channel_id=1, source_target_pairs={{0,1},{1,0},{2,3},{3,2},{4,5},{5,4},{6,7},{7,6},{8,9},{9,8},{10,11... | collective-permute-start | bytes 5013512 | tf_op jit(solution)/shard_map/ppermute | solution.py:588
  437.6 17.5 %collective-permute-start.38 = (bf16[192,1536]{1,0:T(8,128)(2,1)}, bf16[192,1536]{1,0:T(8,128)(2,1)}, u32[]{:S(2)}, u32[]{:S(2)}) collective-permute-start(bf16[192,1536]{1,0:T(8,128)(2,1)} %reduce-scatter.2.cloned.1.call-done.first_ref), channel_id=1, source_target_pairs={{0,4},{4,8},{8,12},{1,5},{5,9},{9,13},{2,6},{6,10},{10,14},{3,7},{... | collective-permute-start | bytes 1769480 | tf_op jit(solution)/shard_map/ppermute | solution.py:688
  441.9 17.5 %collective-permute-start.39 = (bf16[192,1536]{1,0:T(8,128)(2,1)}, bf16[192,1536]{1,0:T(8,128)(2,1)}, u32[]{:S(2)}, u32[]{:S(2)}) collective-permute-start(bf16[192,1536]{1,0:T(8,128)(2,1)} %reduce-scatter.2.cloned.1.call-done.first_ref), channel_id=1, source_target_pairs={{12,8},{8,4},{4,0},{13,9},{9,5},{5,1},{14,10},{10,6},{6,2},{15,11}... | collective-permute-start | bytes 1769480 | tf_op jit(solution)/shard_map/ppermute | solution.py:689
  445.6 22.3 %collective-permute-start.30 = (bf16[48,6528]{1,0:T(8,128)(2,1)}, bf16[48,6528]{1,0:T(8,128)(2,1)}, u32[]{:S(2)}, u32[]{:S(2)}) collective-permute-start(bf16[48,6528]{1,0:T(8,128)(2,1)} %get-tuple-element.215), channel_id=1, source_target_pairs={{0,4},{1,5},{2,6},{3,7},{16,20},{17,21},{18,22},{19,23}} | collective-permute-start | bytes 1880072 | tf_op jit(solution)/shard_map/ppermute | solution.py:688
  460.9 18.2 %collective-permute-start.41 = (bf16[192,1536]{1,0:T(8,128)(2,1)}, bf16[192,1536]{1,0:T(8,128)(2,1)}, u32[]{:S(2)}, u32[]{:S(2)}) collective-permute-start(bf16[192,1536]{1,0:T(8,128)(2,1)} %collective-permute-done.39.refs_5_), channel_id=1, source_target_pairs={{8,4},{4,0},{9,5},{5,1},{10,6},{6,2},{11,7},{7,3},{24,20},{20,16},... | collective-permute-start | bytes 1769480 | tf_op jit(solution)/shard_map/ppermute | solution.py:689
  482.1 21.9 %collective-permute-start.42 = (bf16[48,6528]{1,0:T(8,128)(2,1)}, bf16[48,6528]{1,0:T(8,128)(2,1)}, u32[]{:S(2)}, u32[]{:S(2)}) collective-permute-start(bf16[48,6528]{1,0:T(8,128)(2,1)} %get-tuple-element.213), channel_id=1, source_target_pairs={{0,4},{4,8},{1,5},{5,9},{2,6},{6,10},{3,7},{7,11},{16,20},{20,24},... | collective-permute-start | bytes 1880072 | tf_op jit(solution)/shard_map/ppermute | solution.py:688
  630.3 20.9 %collective-permute-start.60 = (bf16[48,6528]{1,0:T(8,128)(2,1)}, bf16[48,6528]{1,0:T(8,128)(2,1)S(1)}, u32[]{:S(2)}, u32[]{:S(2)}) collective-permute-start(bf16[48,6528]{1,0:T(8,128)(2,1)} %collective-permute-done.58.refs_2_), channel_id=1, source_target_pairs={{8,12},{9,13},{10,14},{11,15},{24,28},{25,29},{26,30},{27,31}} | collective-permute-start | bytes 1880072 | tf_op jit(solution)/shard_map/ppermute | solution.py:688
  631.0 20.2 %collective-permute-start.61 = (bf16[48,6528]{1,0:T(8,128)(2,1)}, bf16[48,6528]{1,0:T(8,128)(2,1)}, u32[]{:S(2)}, u32[]{:S(2)}) collective-permute-start(bf16[48,6528]{1,0:T(8,128)(2,1)} %collective-permute-done.59.refs_3_), channel_id=1, source_target_pairs={{4,0},{5,1},{6,2},{7,3},{20,16},{21,17},{22,18},{23,19}} | collective-permute-start | bytes 1880072 | tf_op jit(solution)/shard_map/ppermute | solution.py:689
  (174 other events, 1724.3 us)
Sparse Core Ops, SparseCore 0:
  35.2 52.1 all-gather.2
  89.0 28.8 all-gather.4
  346.3 51.1 reduce-scatter.1
